TPU v7x, 32 devices: a whole 2x2x4 slice. The times are simulated.
32 devices in a mesh: items: 8 (over z, x), patch: 4 (over y, core).
Axes of the slice: x: 2, y: 2, z: 4, core: 2. Of those that a mesh axis runs over, the one named last changes fastest.
Arguments:
- text: bfloat16 [10240, 768], P(('items', 'patch')), may hold values from -6 to 6
- cotangent: bfloat16 [10240, 768], P(('items', 'patch')), may hold values from -6 to 6
- patches: bfloat16 [256, 148, 1024], P('items', 'patch'), may hold values from -6 to 6
- text_lengths: int32 [256], P(('items', 'patch')), may hold values from 4 to 40
- patch_mask: int32 [256, 148], P('items', 'patch'), may hold values 0 or 1
- w_qkv: float32 [768, 2304], P(('items', 'patch')), may hold values from -0.21875 to 0.21875
- w_out: float32 [768, 768], P(('items', 'patch')), may hold values from -0.875 to 0.875
- w_cross_q: float32 [768, 768], P(('items', 'patch')), may hold values from -0.21875 to 0.21875
- w_cross_kv: float32 [1024, 1536], P(('items', 'patch')), may hold values from -0.1875 to 0.1875
- w_cross_out: float32 [768, 768], P(('items', 'patch')), may hold values from -1.75 to 1.75
- w_inner: float32 [768, 3072], P(('items', 'patch')), may hold values from -0.21875 to 0.21875
- w_outer: float32 [3072, 768], P(('items', 'patch')), may hold values from -0.109375 to 0.109375
- norm_rows: float32 [6, 768], P(None, ('items', 'patch')), may hold values from -0.4 to 1.4, as said below
- first_qkv: float32 [768, 2304], P(('items', 'patch')), may hold values from -32 to 32
- first_out: float32 [768, 768], P(('items', 'patch')), may hold values from -32 to 32
- first_cross_q: float32 [768, 768], P(('items', 'patch')), may hold values from -20 to 20
- first_cross_kv: float32 [1024, 1536], P(('items', 'patch')), may hold values from -64 to 64
- first_cross_out: float32 [768, 768], P(('items', 'patch')), may hold values from -14 to 14
- first_inner: float32 [768, 3072], P(('items', 'patch')), may hold values from -20 to 20
- first_outer: float32 [3072, 768], P(('items', 'patch')), may hold values from -40 to 40
- first_norms: float32 [6, 768], P(None, ('items', 'patch')), may hold values from -64 to 64
- second_qkv: float32 [768, 2304], P(('items', 'patch')), may hold values from 2.56 to 10.24
- second_out: float32 [768, 768], P(('items', 'patch')), may hold values from 2.56 to 10.24
- second_cross_q: float32 [768, 768], P(('items', 'patch')), may hold values from 0.9216 to 3.6864
- second_cross_kv: float32 [1024, 1536], P(('items', 'patch')), may hold values from 9.472 to 37.888
- second_cross_out: float32 [768, 768], P(('items', 'patch')), may hold values from 0.4096 to 1.6384
- second_inner: float32 [768, 3072], P(('items', 'patch')), may hold values from 0.9216 to 3.6864
- second_outer: float32 [3072, 768], P(('items', 'patch')), may hold values from 3.6864 to 14.7456
- second_norms: float32 [6, 768], P(None, ('items', 'patch')), may hold values from 10.24 to 40.96
Outputs:
- block_output: bfloat16 [10240, 768], P(('items', 'patch'))
- text_grad: float32 [10240, 768], P(('items', 'patch'))
- patch_grad: float32 [256, 148, 1024], P('items', 'patch')
- new_w_qkv: float32 [768, 2304], P(('items', 'patch'))
- new_w_out: float32 [768, 768], P(('items', 'patch'))
- new_w_cross_q: float32 [768, 768], P(('items', 'patch'))
- new_w_cross_kv: float32 [1024, 1536], P(('items', 'patch'))
- new_w_cross_out: float32 [768, 768], P(('items', 'patch'))
- new_w_inner: float32 [768, 3072], P(('items', 'patch'))
- new_w_outer: float32 [3072, 768], P(('items', 'patch'))
- new_norm_rows: float32 [6, 768], P(None, ('items', 'patch'))
- new_first_qkv: float32 [768, 2304], P(('items', 'patch'))
- new_first_out: float32 [768, 768], P(('items', 'patch'))
- new_first_cross_q: float32 [768, 768], P(('items', 'patch'))
- new_first_cross_kv: float32 [1024, 1536], P(('items', 'patch'))
- new_first_cross_out: float32 [768, 768], P(('items', 'patch'))
- new_first_inner: float32 [768, 3072], P(('items', 'patch'))
- new_first_outer: float32 [3072, 768], P(('items', 'patch'))
- new_first_norms: float32 [6, 768], P(None, ('items', 'patch'))
- new_second_qkv: float32 [768, 2304], P(('items', 'patch'))
- new_second_out: float32 [768, 768], P(('items', 'patch'))
- new_second_cross_q: float32 [768, 768], P(('items', 'patch'))
- new_second_cross_kv: float32 [1024, 1536], P(('items', 'patch'))
- new_second_cross_out: float32 [768, 768], P(('items', 'patch'))
- new_second_inner: float32 [768, 3072], P(('items', 'patch'))
- new_second_outer: float32 [3072, 768], P(('items', 'patch'))
- new_second_norms: float32 [6, 768], P(None, ('items', 'patch'))
Inputs may be any that keep to these rules, and one draw needn't show every extreme that they name: `norm_rows`: rows 0, 2 and 4 are gains near one, rows 1, 3 and 5 biases near zero.
All inputs are finite; a program needn't handle non-finite values. No bound on the sum of `patch_mask` on one device may be relied on, other than what follows from the above.
Results may differ from a plain program's by a relative error of at most 0.033.
Values may be sent and summed in bfloat16 or wider, within the bound.
A program may use at most 256 MiB of HBM per device.

v0:
```python
import jax
import jax.numpy as jnp
from jax import lax
from jax.sharding import PartitionSpec as P

D = 768
HEADS = 12
HEAD_DIM = 64
ENC = 1024
TEXT = 40
VALID = 145


step_rates = (0.05, 0.15, 0.05, 0.05, 0.3, 0.05, 0.05, 0.5)
step_decays = (0.01, 0.01, 0.01, 0.01, 0.01, 0.01, 0.01, 0.0)


def merged(array, axis, join):
    gathered = jax.tree.map(
        lambda a, kind: lax.all_gather(a.astype(kind), axis), array, (jnp.bfloat16, jnp.bfloat16)
    )

    def take(source):
        return jax.tree.map(
            lambda a, own: lax.dynamic_index_in_dim(a, source, 0, False).astype(own.dtype),
            gathered,
            array,
        )

    return lax.fori_loop(
        1, lax.axis_size(axis), lambda source, state: join(state, take(source)), take(0)
    )


def matmul(left_side, right_side):
    return jnp.dot(left_side, right_side, preferred_element_type=jnp.float32)


def grad_weight(inputs_low, grads_low):
    return lax.dot_general(
        inputs_low, grads_low, (((0,), (0,)), ((), ())), preferred_element_type=jnp.float32
    )


def grad_inputs(grads_low, weight_low):
    return lax.dot_general(
        grads_low, weight_low, (((1,), (1,)), ((), ())), preferred_element_type=jnp.float32
    )


def norm_forward(values, norm_gain, norm_shift):
    center = values - jnp.mean(values, axis=-1, keepdims=True)
    inverse = lax.rsqrt(jnp.mean(center * center, axis=-1, keepdims=True) + 1e-12)
    normed = center * inverse
    return (normed * norm_gain + norm_shift, normed, inverse)


def norm_backward(grad_out, normed, inverse, norm_gain):
    grad_gain = jnp.sum(grad_out * normed, axis=0)
    grad_shift = jnp.sum(grad_out, axis=0)
    scaled = grad_out * norm_gain
    grad_values = inverse * (
        scaled
        - jnp.mean(scaled, axis=-1, keepdims=True)
        - normed * jnp.mean(scaled * normed, axis=-1, keepdims=True)
    )
    return (grad_values, grad_gain, grad_shift)


def gelu_exact(values):
    return jax.nn.gelu(values, approximate=False)


def score_rows(query_rows, key_rows, key_bias):
    scores = jnp.einsum("bqhe,bkhe->bhqk", query_rows, key_rows, preferred_element_type=jnp.float32)
    return scores * HEAD_DIM ** (-0.5) + key_bias[:, None, None, :]


def attend_forward(query_rows, key_rows, value_rows, key_bias):
    scores = score_rows(query_rows, key_rows, key_bias)
    row_top = jnp.max(scores, axis=-1, keepdims=True)
    exp_scores = jnp.exp(scores - row_top)
    row_total = jnp.sum(exp_scores, axis=-1, keepdims=True)
    probs_low = (exp_scores / row_total).astype(jnp.bfloat16)
    context = jnp.einsum(
        "bhqk,bkhe->bqhe", probs_low, value_rows, preferred_element_type=jnp.float32
    )
    return (context, row_top + jnp.log(row_total))


def attend_backward(query_rows, key_rows, value_rows, key_bias, log_total, grad_context):
    probs_full = jnp.exp(score_rows(query_rows, key_rows, key_bias) - log_total)
    grad_probs = jnp.einsum(
        "bqhe,bkhe->bhqk", grad_context, value_rows, preferred_element_type=jnp.float32
    )
    row_delta = jnp.sum(probs_full * grad_probs, axis=-1, keepdims=True)
    grad_scores = (probs_full * (grad_probs - row_delta)).astype(jnp.bfloat16)
    grad_query = jnp.einsum(
        "bhqk,bkhe->bqhe", grad_scores, key_rows, preferred_element_type=jnp.float32
    ) * HEAD_DIM ** (-0.5)
    grad_key = jnp.einsum(
        "bhqk,bqhe->bkhe", grad_scores, query_rows, preferred_element_type=jnp.float32
    ) * HEAD_DIM ** (-0.5)
    grad_value = jnp.einsum(
        "bhqk,bqhe->bkhe",
        probs_full.astype(jnp.bfloat16),
        grad_context,
        preferred_element_type=jnp.float32,
    )
    return (grad_query, grad_key, grad_value)


def merge_stats(earlier, latter):
    row_top = jnp.maximum(earlier[0], latter[0])
    row_total = earlier[1] * jnp.exp(earlier[0] - row_top) + latter[1] * jnp.exp(
        latter[0] - row_top
    )
    return (row_top, row_total)


def adamw_step(master, gradient, first_moment, second_moment, rate, decay):
    first_new = 0.9 * first_moment + 0.1 * gradient
    second_new = 0.999 * second_moment + 0.001 * gradient * gradient
    step_size = first_new / (1.0 - 0.9**10) / (jnp.sqrt(second_new / (1.0 - 0.999**10)) + 1e-08)
    return (master - rate * (step_size + decay * master), first_new, second_new)


def on_device(
    text,
    cotangent,
    patches,
    text_lengths,
    patch_mask,
    w_qkv,
    w_out,
    w_cross_q,
    w_cross_kv,
    w_cross_out,
    w_inner,
    w_outer,
    norm_rows,
    first_qkv,
    first_out,
    first_cross_q,
    first_cross_kv,
    first_cross_out,
    first_inner,
    first_outer,
    first_norms,
    second_qkv,
    second_out,
    second_cross_q,
    second_cross_kv,
    second_cross_out,
    second_inner,
    second_outer,
    second_norms,
):
    bf16 = jnp.bfloat16
    (
        full_qkv,
        full_out,
        full_cross_q,
        full_cross_kv,
        full_cross_out,
        full_inner,
        full_outer,
        full_norms,
    ) = (
        lax.all_gather(w_qkv.astype(bf16), ("items", "patch"), axis=0, tiled=True),
        lax.all_gather(w_out.astype(bf16), ("items", "patch"), axis=0, tiled=True),
        lax.all_gather(w_cross_q.astype(bf16), ("items", "patch"), axis=0, tiled=True),
        lax.all_gather(w_cross_kv.astype(bf16), ("items", "patch"), axis=0, tiled=True),
        lax.all_gather(w_cross_out.astype(bf16), ("items", "patch"), axis=0, tiled=True),
        lax.all_gather(w_inner.astype(bf16), ("items", "patch"), axis=0, tiled=True),
        lax.all_gather(w_outer.astype(bf16), ("items", "patch"), axis=0, tiled=True),
        lax.all_gather(norm_rows.astype(bf16), ("items", "patch"), axis=1, tiled=True),
    )
    norm_float = full_norms.astype(jnp.float32)
    row_count = text.shape[0]
    items_here = row_count // TEXT
    group_items = patches.shape[0]
    local_patches = patches.shape[1]
    positions = jnp.arange(TEXT, dtype=jnp.int32)
    self_bias = jnp.where(positions[None, :] < text_lengths[:, None], 0.0, -10000.0).astype(
        jnp.float32
    )
    patch_index = lax.axis_index("patch") * local_patches + jnp.arange(
        local_patches, dtype=jnp.int32
    )
    patch_valid = (patch_mask > 0) & (patch_index[None, :] < VALID)
    patch_bias = jnp.where(patch_valid, 0.0, -10000.0).astype(jnp.float32)
    mixed_rows = matmul(text, full_qkv).astype(bf16).reshape(items_here, TEXT, 3, HEADS, HEAD_DIM)
    self_context, self_lse = attend_forward(
        mixed_rows[:, :, 0], mixed_rows[:, :, 1], mixed_rows[:, :, 2], self_bias
    )
    self_low = self_context.reshape(row_count, D).astype(bf16)
    pre_first = text.astype(jnp.float32) + matmul(self_low, full_out)
    after_self, normed_one, inverse_one = norm_forward(pre_first, norm_float[0], norm_float[1])
    self_norm_low = after_self.astype(bf16)
    cross_query = matmul(self_norm_low, full_cross_q).astype(bf16)
    image_flat = patches.reshape(group_items * local_patches, ENC)
    memory = (
        matmul(image_flat, full_cross_kv)
        .astype(bf16)
        .reshape(group_items, local_patches, 2, HEADS, HEAD_DIM)
    )
    query_all = lax.all_gather(cross_query, "patch", axis=0, tiled=True).reshape(
        group_items, TEXT, HEADS, HEAD_DIM
    )
    cross_scores = score_rows(query_all, memory[:, :, 0], patch_bias)
    part_top = jnp.max(cross_scores, axis=-1)
    part_total = jnp.sum(jnp.exp(cross_scores - part_top[..., None]), axis=-1)
    cross_top, cross_total = merged((part_top, part_total), "patch", merge_stats)
    cross_lse = (cross_top + jnp.log(cross_total))[..., None]
    cross_probs = (jnp.exp(cross_scores - cross_top[..., None]) / cross_total[..., None]).astype(
        bf16
    )
    part_context = jnp.einsum(
        "bhqk,bkhe->bqhe", cross_probs, memory[:, :, 1], preferred_element_type=jnp.float32
    )
    cross_context = lax.psum_scatter(
        part_context.reshape(group_items * TEXT, D).astype(jnp.bfloat16),
        "patch",
        scatter_dimension=0,
        tiled=True,
    ).astype(jnp.float32)
    cross_low = cross_context.astype(bf16)
    pre_second = after_self + matmul(cross_low, full_cross_out)
    after_cross, normed_two, inverse_two = norm_forward(pre_second, norm_float[2], norm_float[3])
    cross_norm_low = after_cross.astype(bf16)
    inner_pre = matmul(cross_norm_low, full_inner)
    hidden_value, gelu_pull = jax.vjp(gelu_exact, inner_pre)
    hidden_low = hidden_value.astype(bf16)
    pre_third = after_cross + matmul(hidden_low, full_outer)
    result, normed_three, inverse_three = norm_forward(pre_third, norm_float[4], norm_float[5])
    block_output = result.astype(bf16)
    grad_third, grad_gain_three, grad_shift_three = norm_backward(
        cotangent.astype(jnp.float32), normed_three, inverse_three, norm_float[4]
    )
    grad_third_low = grad_third.astype(bf16)
    grad_w_outer = grad_weight(hidden_low, grad_third_low)
    grad_inner_low = gelu_pull(grad_inputs(grad_third_low, full_outer))[0].astype(bf16)
    grad_w_inner = grad_weight(cross_norm_low, grad_inner_low)
    grad_after_cross = grad_third + grad_inputs(grad_inner_low, full_inner)
    grad_second, grad_gain_two, grad_shift_two = norm_backward(
        grad_after_cross, normed_two, inverse_two, norm_float[2]
    )
    grad_second_low = grad_second.astype(bf16)
    grad_w_cross_out = grad_weight(cross_low, grad_second_low)
    grad_cross_ctx = grad_inputs(grad_second_low, full_cross_out).astype(bf16)
    grad_ctx_all = lax.all_gather(grad_cross_ctx, "patch", axis=0, tiled=True).reshape(
        group_items, TEXT, HEADS, HEAD_DIM
    )
    probs_again = jnp.exp(score_rows(query_all, memory[:, :, 0], patch_bias) - cross_lse)
    grad_probs = jnp.einsum(
        "bqhe,bkhe->bhqk", grad_ctx_all, memory[:, :, 1], preferred_element_type=jnp.float32
    )
    part_delta = jnp.sum(probs_again * grad_probs, axis=-1)
    row_delta = lax.psum(part_delta.astype(jnp.bfloat16), "patch").astype(jnp.float32)
    grad_scores = (probs_again * (grad_probs - row_delta[..., None])).astype(bf16)
    part_query = jnp.einsum(
        "bhqk,bkhe->bqhe", grad_scores, memory[:, :, 0], preferred_element_type=jnp.float32
    ) * HEAD_DIM ** (-0.5)
    grad_cross_query = (
        lax.psum_scatter(
            part_query.reshape(group_items * TEXT, D).astype(jnp.bfloat16),
            "patch",
            scatter_dimension=0,
            tiled=True,
        )
        .astype(jnp.float32)
        .astype(bf16)
    )
    grad_key = jnp.einsum(
        "bhqk,bqhe->bkhe", grad_scores, query_all, preferred_element_type=jnp.float32
    ) * HEAD_DIM ** (-0.5)
    grad_value = jnp.einsum(
        "bhqk,bqhe->bkhe",
        probs_again.astype(bf16),
        grad_ctx_all,
        preferred_element_type=jnp.float32,
    )
    grad_memory = jnp.stack([grad_key, grad_value], axis=2).astype(bf16)
    grad_memory_flat = grad_memory.reshape(group_items * local_patches, 2 * D)
    grad_w_cross_kv = grad_weight(image_flat, grad_memory_flat)
    patch_grad = grad_inputs(grad_memory_flat, full_cross_kv).reshape(
        group_items, local_patches, ENC
    )
    grad_w_cross_q = grad_weight(self_norm_low, grad_cross_query)
    grad_after_self = grad_second + grad_inputs(grad_cross_query, full_cross_q)
    grad_first, grad_gain_one, grad_shift_one = norm_backward(
        grad_after_self, normed_one, inverse_one, norm_float[0]
    )
    grad_first_low = grad_first.astype(bf16)
    grad_w_out = grad_weight(self_low, grad_first_low)
    grad_self_ctx = (
        grad_inputs(grad_first_low, full_out)
        .astype(bf16)
        .reshape(items_here, TEXT, HEADS, HEAD_DIM)
    )
    self_query, self_key, self_value = attend_backward(
        mixed_rows[:, :, 0],
        mixed_rows[:, :, 1],
        mixed_rows[:, :, 2],
        self_bias,
        self_lse,
        grad_self_ctx,
    )
    grad_mixed = (
        jnp.stack([self_query, self_key, self_value], axis=2).astype(bf16).reshape(row_count, 3 * D)
    )
    grad_w_qkv = grad_weight(text, grad_mixed)
    text_grad = grad_first + grad_inputs(grad_mixed, full_qkv)
    grad_norms = jnp.stack(
        [
            grad_gain_one,
            grad_shift_one,
            grad_gain_two,
            grad_shift_two,
            grad_gain_three,
            grad_shift_three,
        ],
        axis=0,
    )
    local_grads = (
        grad_w_qkv,
        grad_w_out,
        grad_w_cross_q,
        grad_w_cross_kv,
        grad_w_cross_out,
        grad_w_inner,
        grad_w_outer,
        grad_norms,
    )
    reduced = (
        lax.psum_scatter(local_grads[0], ("items", "patch"), scatter_dimension=0, tiled=True),
        lax.psum_scatter(local_grads[1], ("items", "patch"), scatter_dimension=0, tiled=True),
        lax.psum_scatter(local_grads[2], ("items", "patch"), scatter_dimension=0, tiled=True),
        lax.psum_scatter(local_grads[3], ("items", "patch"), scatter_dimension=0, tiled=True),
        lax.psum_scatter(local_grads[4], ("items", "patch"), scatter_dimension=0, tiled=True),
        lax.psum_scatter(local_grads[5], ("items", "patch"), scatter_dimension=0, tiled=True),
        lax.psum_scatter(local_grads[6], ("items", "patch"), scatter_dimension=0, tiled=True),
        lax.psum_scatter(local_grads[7], ("items", "patch"), scatter_dimension=1, tiled=True),
    )
    masters = (w_qkv, w_out, w_cross_q, w_cross_kv, w_cross_out, w_inner, w_outer, norm_rows)
    firsts = (
        first_qkv,
        first_out,
        first_cross_q,
        first_cross_kv,
        first_cross_out,
        first_inner,
        first_outer,
        first_norms,
    )
    seconds = (
        second_qkv,
        second_out,
        second_cross_q,
        second_cross_kv,
        second_cross_out,
        second_inner,
        second_outer,
        second_norms,
    )
    new_masters = []
    new_firsts = []
    new_seconds = []
    for position in range(8):
        updated = adamw_step(
            masters[position],
            reduced[position],
            firsts[position],
            seconds[position],
            step_rates[position],
            step_decays[position],
        )
        new_masters.append(updated[0])
        new_firsts.append(updated[1])
        new_seconds.append(updated[2])
    return (
        block_output,
        text_grad,
        patch_grad,
        new_masters[0],
        new_masters[1],
        new_masters[2],
        new_masters[3],
        new_masters[4],
        new_masters[5],
        new_masters[6],
        new_masters[7],
        new_firsts[0],
        new_firsts[1],
        new_firsts[2],
        new_firsts[3],
        new_firsts[4],
        new_firsts[5],
        new_firsts[6],
        new_firsts[7],
        new_seconds[0],
        new_seconds[1],
        new_seconds[2],
        new_seconds[3],
        new_seconds[4],
        new_seconds[5],
        new_seconds[6],
        new_seconds[7],
    )


def solution(mesh):
    return jax.shard_map(
        on_device,
        mesh=mesh,
        in_specs=(
            P(("items", "patch"), None),
            P(("items", "patch"), None),
            P("items", "patch", None),
            P(("items", "patch")),
            P("items", "patch"),
            P(("items", "patch"), None),
            P(("items", "patch"), None),
            P(("items", "patch"), None),
            P(("items", "patch"), None),
            P(("items", "patch"), None),
            P(("items", "patch"), None),
            P(("items", "patch"), None),
            P(None, ("items", "patch")),
            P(("items", "patch"), None),
            P(("items", "patch"), None),
            P(("items", "patch"), None),
            P(("items", "patch"), None),
            P(("items", "patch"), None),
            P(("items", "patch"), None),
            P(("items", "patch"), None),
            P(None, ("items", "patch")),
            P(("items", "patch"), None),
            P(("items", "patch"), None),
            P(("items", "patch"), None),
            P(("items", "patch"), None),
            P(("items", "patch"), None),
            P(("items", "patch"), None),
            P(("items", "patch"), None),
            P(None, ("items", "patch")),
        ),
        out_specs=(
            P(("items", "patch"), None),
            P(("items", "patch"), None),
            P("items", "patch", None),
            P(("items", "patch"), None),
            P(("items", "patch"), None),
            P(("items", "patch"), None),
            P(("items", "patch"), None),
            P(("items", "patch"), None),
            P(("items", "patch"), None),
            P(("items", "patch"), None),
            P(None, ("items", "patch")),
            P(("items", "patch"), None),
            P(("items", "patch"), None),
            P(("items", "patch"), None),
            P(("items", "patch"), None),
            P(("items", "patch"), None),
            P(("items", "patch"), None),
            P(("items", "patch"), None),
            P(None, ("items", "patch")),
            P(("items", "patch"), None),
            P(("items", "patch"), None),
            P(("items", "patch"), None),
            P(("items", "patch"), None),
            P(("items", "patch"), None),
            P(("items", "patch"), None),
            P(("items", "patch"), None),
            P(None, ("items", "patch")),
        ),
        check_vma=False,
    )
```

profile of v0, /device:TPU:16, one launch (start us, length us, event | category | flops | bytes accessed | tf_op | source)
XLA Modules:
  0.0 1467.0 jit_solution(13840569589412100638)
XLA Ops:
  14.4 31.8 %all-gather.2 = bf16[32,24,6]{1,2,0:T(8,128)(2,1)S(1)} all-gather(bf16[1,24,6]{1,2,0:T(8,128)(2,1)S(1)} %convert_bitcast_fusion.1), channel_id=1, replica_groups=mesh['items'=8,'patch'=4] {'items','patch'}, dimensions={0}, use_global_device_ids=true | all-gather | bytes 9504 | tf_op jit(solution)/shard_map/all_gather | solution.py:177
  47.4 24.2 %all-gather.13.cloned.1.call-done = bf16[768,2304]{1,0:T(8,128)(2,1)} async-done(((bf16[24,2304]{1,0:T(8,128)(2,1)}), bf16[768,2304]{1,0:T(8,128)(2,1)}) %all-gather.13.cloned.1.call-update) | async-done | bytes 3538960 | tf_op jit(solution)/shard_map/all_gather | solution.py:170
  85.9 41.9 %all-gather.15.cloned.1.call-done = bf16[768,768]{1,0:T(8,128)(2,1)} async-done(((bf16[24,768]{1,0:T(8,128)(2,1)}), bf16[768,768]{1,0:T(8,128)(2,1)}) %all-gather.15.cloned.1.call-update) | async-done | bytes 1179664 | tf_op jit(solution)/shard_map/all_gather | solution.py:171
  130.1 54.3 %all-gather.19.cloned.1.call-done = bf16[768,768]{1,0:T(8,128)(2,1)} async-done(((bf16[24,768]{1,0:T(8,128)(2,1)}), bf16[768,768]{1,0:T(8,128)(2,1)}) %all-gather.19.cloned.1.call-update) | async-done | bytes 1179664 | tf_op jit(solution)/shard_map/all_gather | solution.py:172
  195.8 49.6 %all-gather.17.cloned.1.call-done = bf16[1024,1536]{1,0:T(8,128)(2,1)} async-done(((bf16[32,1536]{1,0:T(8,128)(2,1)}), bf16[1024,1536]{1,0:T(8,128)(2,1)}) %all-gather.17.cloned.1.call-update) | async-done | bytes 3145744 | tf_op jit(solution)/shard_map/all_gather | solution.py:173
  252.6 12.7 reshape.221
  306.4 11.4 convert_bitcast_fusion
  332.8 29.8 %reduce-scatter.15.cloned.1.call-done = bf16[320,768]{1,0:T(8,128)(2,1)} async-done(((bf16[1280,768]{1,0:T(8,128)(2,1)}), bf16[320,768]{1,0:T(8,128)(2,1)}) %reduce-scatter.15.cloned.1.call-update) | async-done | bytes 491536 | tf_op jit(solution)/shard_map/reduce_scatter | solution.py:222
  365.0 64.8 %all-gather.25.cloned.1.call-done = bf16[768,3072]{1,0:T(8,128)(2,1)} async-done(((bf16[24,3072]{1,0:T(8,128)(2,1)}), bf16[768,3072]{1,0:T(8,128)(2,1)}) %all-gather.25.cloned.1.call-update) | async-done | bytes 4718608 | tf_op jit(solution)/shard_map/all_gather | solution.py:175
  429.9 13.2 multiply_convert_fusion.2
  443.0 53.1 %all-gather.27.cloned.1.call-done = bf16[3072,768]{1,0:T(8,128)(2,1)} async-done(((bf16[96,768]{1,0:T(8,128)(2,1)}), bf16[3072,768]{1,0:T(8,128)(2,1)}) %all-gather.27.cloned.1.call-update) | async-done | bytes 4718608 | tf_op jit(solution)/shard_map/all_gather | solution.py:176
  512.3 20.6 %all-gather.29.cloned.1.call-done = bf16[1280,768]{1,0:T(8,128)(2,1)} async-done(((bf16[320,768]{1,0:T(8,128)(2,1)}), bf16[1280,768]{1,0:T(8,128)(2,1)}) %all-gather.29.cloned.1.call-update) | async-done | bytes 1966096 | tf_op jit(solution)/shard_map/all_gather | solution.py:252
  540.0 13.2 multiply_reduce_fusion
  553.2 12.0 psum.7
  591.9 29.2 %reduce-scatter.17.cloned.1.call-done = bf16[320,768]{1,0:T(8,128)(2,1)} async-done(((bf16[1280,768]{1,0:T(8,128)(2,1)}), bf16[320,768]{1,0:T(8,128)(2,1)}) %reduce-scatter.17.cloned.1.call-update) | async-done | bytes 491536 | tf_op jit(solution)/shard_map/reduce_scatter | solution.py:266
  663.8 13.1 convert_element_type.265
  739.5 10.4 copy.244
  749.9 13.0 reshape.242
  774.0 39.9 %all-reduce = f32[6,768]{1,0:T(8,128)S(1)} all-reduce(f32[6,768]{1,0:T(8,128)S(1)} %stack.59), channel_id=13, replica_groups=mesh['items'=8,'patch'=4] {'items','patch'}, use_global_device_ids=true, to_apply=%region_36.37.clone | all-reduce | flops 4608 | bytes 36864
  830.3 101.6 %reduce-scatter.19.cloned.1.call-done = f32[24,768]{1,0:T(8,128)} async-done(((f32[768,768]{1,0:T(8,128)}), f32[24,768]{1,0:T(8,128)}) %reduce-scatter.19.cloned.1.call-update) | async-done | bytes 73744 | tf_op jit(solution)/shard_map/reduce_scatter | solution.py:338
  933.6 118.6 %reduce-scatter.31.cloned.1.call-done = f32[32,1536]{1,0:T(8,128)} async-done(((f32[1024,1536]{1,0:T(8,128)}), f32[32,1536]{1,0:T(8,128)}) %reduce-scatter.31.cloned.1.call-update) | async-done | bytes 196624 | tf_op jit(solution)/shard_map/reduce_scatter | solution.py:340
  1054.2 138.5 %reduce-scatter.27.cloned.1.call-done = f32[96,768]{1,0:T(8,128)} async-done(((f32[3072,768]{1,0:T(8,128)}), f32[96,768]{1,0:T(8,128)}) %reduce-scatter.27.cloned.1.call-update) | async-done | bytes 294928 | tf_op jit(solution)/shard_map/reduce_scatter | solution.py:343
  1194.8 139.3 %reduce-scatter.25.cloned.1.call-done = f32[24,3072]{1,0:T(8,128)} async-done(((f32[768,3072]{1,0:T(8,128)}), f32[24,3072]{1,0:T(8,128)}) %reduce-scatter.25.cloned.1.call-update) | async-done | bytes 294928 | tf_op jit(solution)/shard_map/reduce_scatter | solution.py:342
  1336.1 121.9 %reduce-scatter.29.cloned.1.call-done = f32[24,2304]{1,0:T(8,128)} async-done(((f32[768,2304]{1,0:T(8,128)}), f32[24,2304]{1,0:T(8,128)}) %reduce-scatter.29.cloned.1.call-update) | async-done | bytes 221200 | tf_op jit(solution)/shard_map/reduce_scatter | solution.py:337
  (293 shorter events, 293.8 us)
Async XLA Ops:
  7.2 64.4 %all-gather.13.cloned.1.call-start = ((), (), s32[]{:S(2)}) async-start(), calls=%async_computation.9 | async-start | bytes 3649536 | tf_op jit(solution)/shard_map/all_gather | solution.py:170
  8.9 119.0 %all-gather.15.cloned.1.call-start = ((), (), s32[]{:S(2)}) async-start(), calls=%async_computation.10 | async-start | bytes 1216512 | tf_op jit(solution)/shard_map/all_gather | solution.py:171
  10.4 174.0 %all-gather.19.cloned.1.call-start = ((), (), s32[]{:S(2)}) async-start(), calls=%async_computation.12 | async-start | bytes 1216512 | tf_op jit(solution)/shard_map/all_gather | solution.py:172
  12.0 233.4 %all-gather.17.cloned.1.call-start = ((), (), s32[]{:S(2)}) async-start(), calls=%async_computation.11 | async-start | bytes 3244032 | tf_op jit(solution)/shard_map/all_gather | solution.py:173
  13.7 261.1 %all-gather.21.cloned.1.call-start = ((), (), s32[]{:S(2)}) async-start(), calls=%async_computation.13 | async-start | bytes 2457600 | tf_op jit(solution)/shard_map/all_gather | solution.py:208
  187.1 145.7 %all-gather.23.cloned.1.call-start = ((), (), s32[]{:S(2)}) async-start(), calls=%async_computation.15 | async-start | bytes 1216512 | tf_op jit(solution)/shard_map/all_gather | solution.py:174
  187.8 174.8 %reduce-scatter.15.cloned.1.call-start = ((), (), s32[]{:S(2)}) async-start(), calls=%async_computation.14 | async-start | bytes 2457600 | tf_op jit(solution)/shard_map/reduce_scatter | solution.py:222
  331.2 98.6 %all-gather.25.cloned.1.call-start = ((), (), s32[]{:S(2)}) async-start(), calls=%async_computation.16 | async-start | bytes 4866048 | tf_op jit(solution)/shard_map/all_gather | solution.py:175
  332.0 164.2 %all-gather.27.cloned.1.call-start = ((), (), s32[]{:S(2)}) async-start(), calls=%async_computation.17 | async-start | bytes 4866048 | tf_op jit(solution)/shard_map/all_gather | solution.py:176
  332.8 200.1 %all-gather.29.cloned.1.call-start = ((), (), s32[]{:S(2)}) async-start(), calls=%async_computation.18 | async-start | bytes 2457600 | tf_op jit(solution)/shard_map/all_gather | solution.py:252
  511.8 109.3 %reduce-scatter.17.cloned.1.call-start = ((), (), s32[]{:S(2)}) async-start(), calls=%async_computation.19 | async-start | bytes 2457600 | tf_op jit(solution)/shard_map/reduce_scatter | solution.py:266
  589.5 182.8 %reduce-scatter.23.cloned.1.call-start = ((), (), s32[]{:S(2)}) async-start(), calls=%async_computation.22 | async-start | bytes 2433024 | tf_op jit(solution)/shard_map/reduce_scatter | solution.py:341
  591.8 236.9 %reduce-scatter.21.cloned.1.call-start = ((), (), s32[]{:S(2)}) async-start(), calls=%async_computation.21 | async-start | bytes 2433024 | tf_op jit(solution)/shard_map/reduce_scatter | solution.py:339
  624.5 307.4 %reduce-scatter.19.cloned.1.call-start = ((), (), s32[]{:S(2)}) async-start(), calls=%async_computation.20 | async-start | bytes 2433024 | tf_op jit(solution)/shard_map/reduce_scatter | solution.py:338
  630.3 421.9 %reduce-scatter.31.cloned.1.call-start = ((), (), s32[]{:S(2)}) async-start(), calls=%async_computation.26 | async-start | bytes 6488064 | tf_op jit(solution)/shard_map/reduce_scatter | solution.py:340
  691.8 500.9 %reduce-scatter.27.cloned.1.call-start = ((), (), s32[]{:S(2)}) async-start(), calls=%async_computation.24 | async-start | bytes 9732096 | tf_op jit(solution)/shard_map/reduce_scatter | solution.py:343
  699.1 635.0 %reduce-scatter.25.cloned.1.call-start = ((), (), s32[]{:S(2)}) async-start(), calls=%async_computation.23 | async-start | bytes 9732096 | tf_op jit(solution)/shard_map/reduce_scatter | solution.py:342
  706.3 751.7 %reduce-scatter.29.cloned.1.call-start = ((), (), s32[]{:S(2)}) async-start(), calls=%async_computation.25 | async-start | bytes 7299072 | tf_op jit(solution)/shard_map/reduce_scatter | solution.py:337
  819.1 515.0 %copy-start.32 = (f32[24,3072]{1,0:T(8,128)S(1)}, f32[24,3072]{1,0:T(8,128)}, u32[]{:S(2)}) copy-start(f32[24,3072]{1,0:T(8,128)} %param.41) | copy-start | bytes 884740
  819.1 515.0 %copy-start.44 = (f32[24,3072]{1,0:T(8,128)S(1)}, f32[24,3072]{1,0:T(8,128)}, u32[]{:S(2)}) copy-start(f32[24,3072]{1,0:T(8,128)} %param.49) | copy-start | bytes 884740
  819.1 515.0 %copy-start.45 = (f32[24,3072]{1,0:T(8,128)S(1)}, f32[24,3072]{1,0:T(8,128)}, u32[]{:S(2)}) copy-start(f32[24,3072]{1,0:T(8,128)} %param.57) | copy-start | bytes 884740
  819.1 639.0 %copy-start.34 = (f32[24,2304]{1,0:T(8,128)S(1)}, f32[24,2304]{1,0:T(8,128)}, u32[]{:S(2)}) copy-start(f32[24,2304]{1,0:T(8,128)} %param.36) | copy-start | bytes 663556
  819.1 639.0 %copy-start.48 = (f32[24,2304]{1,0:T(8,128)S(1)}, f32[24,2304]{1,0:T(8,128)}, u32[]{:S(2)}) copy-start(f32[24,2304]{1,0:T(8,128)} %param.44) | copy-start | bytes 663556
  819.1 639.0 %copy-start.49 = (f32[24,2304]{1,0:T(8,128)S(1)}, f32[24,2304]{1,0:T(8,128)}, u32[]{:S(2)}) copy-start(f32[24,2304]{1,0:T(8,128)} %param.52) | copy-start | bytes 663556
  (59 other events, 1930.6 us)
Sparse Core Ops, SparseCore 0:
  11.5 60.0 all-gather.12
  75.1 52.7 all-gather.14
  131.3 53.0 all-gather.18
  187.7 57.6 all-gather.16
  247.4 22.4 all-gather.20
  273.2 52.6 all-gather.22
  331.4 31.2 reduce-scatter.14
  366.5 63.2 all-gather.24
  433.8 62.3 all-gather.26
  511.9 20.9 all-gather.28
  589.6 31.3 reduce-scatter.16
  626.2 98.0 reduce-scatter.22
  730.4 98.2 reduce-scatter.20
  833.8 98.0 reduce-scatter.18
  938.3 113.8 reduce-scatter.30
  1058.0 134.6 reduce-scatter.26
  1199.4 134.6 reduce-scatter.24
  1339.6 118.3 reduce-scatter.28
where the time goes:
time: 1480 us; the launch traced here: 1470 us
  waiting for transfers between devices  997 us (67%)
  local copies, waits for them, and re-layouts  159 us (11%)
  matrix products  149 us (10%)
  blocking collectives  97 us (7%)
  other arithmetic  47.3 us (3%)
  between operations  15.4 us (1%)
    reduce_scatter x1, waiting for transfers between devices, on_device(): lax.psum_scatter(local_grads[5], ('items', 'patch'), scatter_dimension=0,...  139 us
    reduce_scatter x1, waiting for transfers between devices, on_device(): lax.psum_scatter(local_grads[6], ('items', 'patch'), scatter_dimension=0,...  138 us
    reduce_scatter x1, waiting for transfers between devices, on_device(): lax.psum_scatter(local_grads[0], ('items', 'patch'), scatter_dimension=0,...  122 us
    reduce_scatter x1, waiting for transfers between devices, on_device(): lax.psum_scatter(local_grads[3], ('items', 'patch'), scatter_dimension=0,...  119 us
    reduce_scatter x1, waiting for transfers between devices, on_device(): lax.psum_scatter(local_grads[1], ('items', 'patch'), scatter_dimension=0,...  102 us
    all_gather x1, waiting for transfers between devices, on_device(): lax.all_gather(w_inner.astype(bf16), ('items', 'patch'), axis=0, tiled=True)  64.8 us
    all_gather x1, waiting for transfers between devices, on_device(): lax.all_gather(w_cross_q.astype(bf16), ('items', 'patch'), axis=0, tiled=...  54.3 us
    all_gather x1, waiting for transfers between devices, on_device(): lax.all_gather(w_outer.astype(bf16), ('items', 'patch'), axis=0, tiled=True)  53.1 us
  transfers between devices with their start and end apart: 18, of which 15 were waited for; matrix products, arithmetic and copies ran while one was open for 19% of the time, Pallas kernels for 0%

commit v1 on v0

v1 whole, which is shorter than its diff:
```python
import functools

import jax
import jax.numpy as jnp
from jax import lax
from jax.experimental import pallas as pl
from jax.experimental.pallas import tpu as pltpu
from jax.sharding import PartitionSpec as P

D = 768
HEADS = 12
HEAD_DIM = 64
ENC = 1024
TEXT = 40
VALID = 145
PAIR = 2 * HEAD_DIM
PAIRS = HEADS // 2
SCALE = HEAD_DIM ** (-0.5)
OUTSIDE = -1e30
bf16, f32 = jnp.bfloat16, jnp.float32


def dot(a, b):
    return jnp.dot(a, b, preferred_element_type=f32)


def dot_nt(a, b):
    return lax.dot_general(a, b, (((1,), (1,)), ((), ())), preferred_element_type=f32)


def dot_tn(a, b):
    return lax.dot_general(a, b, (((0,), (0,)), ((), ())), preferred_element_type=f32)


def tiles(total, step, body):
    def run(k, carry):
        body(pl.ds(pl.multiple_of(k * step, step), step))
        return carry

    lax.fori_loop(0, total // step, run, 0)


def norm_forward(values):
    center = values - jnp.mean(values, axis=-1, keepdims=True)
    inverse = lax.rsqrt(jnp.mean(center * center, axis=-1, keepdims=True) + 1e-12)
    return center * inverse, inverse


def norm_backward(grad_out, normed, inverse, gain):
    grad_gain = jnp.sum(grad_out * normed, axis=0, keepdims=True)
    grad_shift = jnp.sum(grad_out, axis=0, keepdims=True)
    scaled = grad_out * gain
    grad_values = inverse * (
        scaled
        - jnp.mean(scaled, axis=-1, keepdims=True)
        - normed * jnp.mean(scaled * normed, axis=-1, keepdims=True)
    )
    return grad_values, grad_gain, grad_shift


def low_half():
    return lax.broadcasted_iota(jnp.int32, (TEXT, PAIR), 1) < HEAD_DIM


def expand(rows):
    low = low_half()
    return jnp.concatenate(
        [jnp.where(low, rows, 0.0), jnp.where(low, 0.0, rows)], axis=0
    ).astype(bf16)


def fold(rows):
    return jnp.where(low_half(), rows[:TEXT], rows[TEXT:])


def softmax(scores):
    top = jnp.max(scores, axis=-1, keepdims=True)
    powers = jnp.exp(scores - top)
    return powers / jnp.sum(powers, axis=-1, keepdims=True)


def pair_cols(j, start=0):
    return slice(start + PAIR * j, start + PAIR * (j + 1))


def pair_rows(j):
    return slice(2 * TEXT * j, 2 * TEXT * (j + 1))


def attend_forward(query, keys, values, bias, probs, item, context, rows):
    js = range(PAIRS)
    scores = [dot_nt(expand(query(j)), keys(j)) * SCALE + bias for j in js]
    weights = [softmax(s) for s in scores]
    for j in js:
        probs[item, pair_rows(j), :] = weights[j]
    parts = [dot(weights[j].astype(bf16), values(j)) for j in js]
    for j in js:
        context[rows, pair_cols(j)] = fold(parts[j])


def attend_backward(query, keys, values, probs, item, grad_context, put_q, put_k, put_v):
    js = range(PAIRS)
    outer = [expand(grad_context(j)) for j in js]
    grads = [dot_nt(outer[j], values(j)) for j in js]
    inner = []
    for j in js:
        weights = probs[item, pair_rows(j), :]
        delta = jnp.sum(weights * grads[j], axis=-1, keepdims=True)
        inner.append((weights * (grads[j] - delta)).astype(bf16))
    for j in js:
        put_v(j, dot_tn(probs[item, pair_rows(j), :].astype(bf16), outer[j]))
    for j in js:
        put_q(j, fold(dot(inner[j], keys(j))) * SCALE)
    for j in js:
        put_k(j, dot_tn(inner[j], expand(query(j))) * SCALE)


def self_forward(lengths, text, w_qkv, w_out, norms, mixed, probs, ctx, normed, inverse, mix, context):
    def project(cols):
        got = dot(text[...], w_qkv[:, cols]).astype(bf16)
        mixed[:, cols] = got
        mix[:, cols] = got.astype(f32)

    tiles(3 * D, 256, project)
    position = lax.broadcasted_iota(jnp.int32, (1, TEXT), 1)

    def one(item, carry):
        rows = pl.ds(pl.multiple_of(item * TEXT, 8), TEXT)
        bias = jnp.where(position < lengths[item], 0.0, -10000.0).astype(f32)
        attend_forward(
            lambda j: mix[rows, pair_cols(j)],
            lambda j: mix[rows, pair_cols(j, D)].astype(bf16),
            lambda j: mix[rows, pair_cols(j, 2 * D)].astype(bf16),
            bias, probs, item, context, rows,
        )
        return carry

    lax.fori_loop(0, probs.shape[0], one, 0)
    ctx[...] = context[...].astype(bf16)
    pre = text[...].astype(f32) + dot(ctx[...], w_out[...])
    n, r = norm_forward(pre)
    normed[...] = n
    inverse[...] = r


def self_backward(text, mixed, probs, ctx, normed, inverse, grad_after, w_qkv, w_out, norms,
                  g_qkv, g_out, text_grad, g_norm, mix, grad_ctx, grad_mix, low_mix):
    grad_pre, grad_gain, grad_shift = norm_backward(grad_after[...], normed[...], inverse[...], norms[0:1, :])
    g_norm[0:1, :] = grad_gain
    g_norm[1:2, :] = grad_shift
    low = grad_pre.astype(bf16)
    g_out[...] = dot_tn(ctx[...], low).astype(bf16)
    grad_ctx[...] = dot_nt(low, w_out[...]).astype(bf16).astype(f32)
    text_grad[...] = grad_pre
    mix[...] = mixed[...].astype(f32)

    def one(item, carry):
        rows = pl.ds(pl.multiple_of(item * TEXT, 8), TEXT)

        def put(start):
            def store(j, value):
                grad_mix[rows, pair_cols(j, start)] = value
            return store

        attend_backward(
            lambda j: mix[rows, pair_cols(j)],
            lambda j: mix[rows, pair_cols(j, D)].astype(bf16),
            lambda j: mix[rows, pair_cols(j, 2 * D)].astype(bf16),
            probs, item, lambda j: grad_ctx[rows, pair_cols(j)],
            put(0), put(D), put(2 * D),
        )
        return carry

    lax.fori_loop(0, probs.shape[0], one, 0)
    low_mix[...] = grad_mix[...].astype(bf16)

    def weights(cols):
        g_qkv[:, cols] = dot_tn(text[...], low_mix[:, cols]).astype(bf16)
        text_grad[...] += dot_nt(low_mix[:, cols], w_qkv[:, cols])

    tiles(3 * D, 256, weights)


def cross_forward(patches, bias, w_kv, w_q, w_out, norms, normed_one,
                  image, memory, query, probs, ctx, normed, inverse, context, wide):
    chunks, items, local, _ = patches.shape
    slots = bias.shape[1]
    step = slots // chunks
    image[...] = jnp.zeros_like(image)

    def lay(item, carry):
        for c in range(chunks):
            start = pl.multiple_of(item * slots + c * step, 16)
            image[pl.ds(start, local), :] = patches[c, item]
        return carry

    lax.fori_loop(0, items, lay, 0)

    def project(cols):
        memory[:, cols] = dot(image[...], w_kv[:, cols]).astype(bf16)

    tiles(2 * D, 256, project)
    after = normed_one[...] * norms[0:1, :] + norms[1:2, :]
    low = dot(after.astype(bf16), w_q[...]).astype(bf16)
    query[...] = low
    wide[...] = low.astype(f32)

    def one(item, carry):
        rows = pl.ds(pl.multiple_of(item * TEXT, 8), TEXT)
        slot = pl.ds(pl.multiple_of(item * slots, 16), slots)
        attend_forward(
            lambda j: wide[rows, pair_cols(j)],
            lambda j: memory[slot, pair_cols(j)],
            lambda j: memory[slot, pair_cols(j, D)],
            bias[pl.ds(item, 1), :], probs, item, context, rows,
        )
        return carry

    lax.fori_loop(0, items, one, 0)
    ctx[...] = context[...].astype(bf16)
    pre = after + dot(ctx[...], w_out[...])
    n, r = norm_forward(pre)
    normed[...] = n
    inverse[...] = r


def cross_backward(image, memory, query, probs, ctx, normed, inverse, normed_one, grad_after,
                   w_kv, w_q, w_out, norms,
                   g_kv, g_q, g_out, patch_grad, grad_self, g_norm, wide, grad_ctx, grad_q, grad_mem):
    chunks, items, local, _ = patch_grad.shape
    slots = image.shape[0] // items
    step = slots // chunks
    grad_pre, grad_gain, grad_shift = norm_backward(grad_after[...], normed[...], inverse[...], norms[2:3, :])
    g_norm[0:1, :] = grad_gain
    g_norm[1:2, :] = grad_shift
    low = grad_pre.astype(bf16)
    g_out[...] = dot_tn(ctx[...], low).astype(bf16)
    grad_ctx[...] = dot_nt(low, w_out[...]).astype(bf16).astype(f32)
    wide[...] = query[...].astype(f32)

    def one(item, carry):
        rows = pl.ds(pl.multiple_of(item * TEXT, 8), TEXT)
        slot = pl.ds(pl.multiple_of(item * slots, 16), slots)

        def put_q(j, value):
            grad_q[rows, pair_cols(j)] = value

        def put(start):
            def store(j, value):
                grad_mem[slot, pair_cols(j, start)] = value.astype(bf16)
            return store

        attend_backward(
            lambda j: wide[rows, pair_cols(j)],
            lambda j: memory[slot, pair_cols(j)],
            lambda j: memory[slot, pair_cols(j, D)],
            probs, item, lambda j: grad_ctx[rows, pair_cols(j)],
            put_q, put(0), put(D),
        )
        return carry

    lax.fori_loop(0, items, one, 0)
    low_q = grad_q[...].astype(bf16)
    after = (normed_one[...] * norms[0:1, :] + norms[1:2, :]).astype(bf16)
    g_q[...] = dot_tn(after, low_q).astype(bf16)
    grad_self[...] = grad_pre + dot_nt(low_q, w_q[...])

    def weights(cols):
        g_kv[:, cols] = dot_tn(image[...], grad_mem[:, cols]).astype(bf16)

    tiles(2 * D, 256, weights)

    def back(item, carry):
        slot = pl.ds(pl.multiple_of(item * slots, 16), slots)
        got = dot_nt(grad_mem[slot, :], w_kv[...])
        for c in range(chunks):
            patch_grad[c, item] = got[c * step : c * step + local].astype(bf16)
        return carry

    lax.fori_loop(0, items, back, 0)


def feed_forward(normed_two, cotangent, w_inner, w_outer, norms,
                 block_output, g_inner, g_outer, grad_after, g_norm, low_in, hidden, slope, total, grad_low, grad_hid):
    after = normed_two[...] * norms[2:3, :] + norms[3:4, :]
    low_in[...] = after.astype(bf16)
    total[...] = after

    def up(cols):
        pre = dot(low_in[...], w_inner[:, cols])
        bell = 0.5 * (1.0 + lax.erf(pre * (0.5 ** 0.5)))
        low = (pre * bell).astype(bf16)
        hidden[:, cols] = low
        slope[:, cols] = bell + pre * jnp.exp(-0.5 * pre * pre) * 0.3989422804014327
        total[...] += dot(low, w_outer[cols, :])

    ff = w_inner.shape[1]
    tiles(ff, 256, up)
    n, r = norm_forward(total[...])
    gain = norms[4:5, :]
    block_output[...] = (n * gain + norms[5:6, :]).astype(bf16)
    grad_pre, grad_gain, grad_shift = norm_backward(cotangent[...].astype(f32), n, r, gain)
    g_norm[0:1, :] = grad_gain
    g_norm[1:2, :] = grad_shift
    grad_after[...] = grad_pre
    grad_low[...] = grad_pre.astype(bf16)

    def down(cols):
        low = (dot_nt(grad_low[...], w_outer[cols, :]) * slope[:, cols]).astype(bf16)
        g_inner[:, cols] = dot_tn(low_in[...], low).astype(bf16)
        g_outer[cols, :] = dot_tn(hidden[:, cols], grad_low[...]).astype(bf16)
        grad_after[...] += dot_nt(low, w_inner[:, cols])

    tiles(ff, 256, down)


VM = pl.BlockSpec(memory_space=pltpu.VMEM)


def call(body, args, outs, scratch, name, smem=0, limit=60 << 20):
    return pl.pallas_call(
        body,
        out_shape=[jax.ShapeDtypeStruct(s, k) for s, k in outs],
        in_specs=[pl.BlockSpec(memory_space=pltpu.SMEM)] * smem + [VM] * (len(args) - smem),
        out_specs=[VM] * len(outs),
        scratch_shapes=[pltpu.VMEM(s, k) for s, k in scratch],
        compiler_params=pltpu.CompilerParams(vmem_limit_bytes=limit),
        name=name,
    )(*args)


def local_step(text, cotangent, pbuf, pbias, lengths, ws, norms):
    w_qkv, w_out, w_cq, w_kv, w_co, w_in, w_outer = ws
    rows = text.shape[0]
    items = rows // TEXT
    slots = pbias.shape[1]
    pairs = HEADS * TEXT
    row = ((rows, D), f32)
    rowl = ((rows, D), bf16)
    one = ((rows, 1), f32)
    gn = ((2, D), f32)
    mixed, probs, ctx, n1, r1 = call(
        self_forward, (lengths, text, w_qkv, w_out, norms),
        [((rows, 3 * D), bf16), ((items, pairs, TEXT), f32), rowl, row, one],
        [((rows, 3 * D), f32), row], "self_forward", smem=1)
    image, memory, query, cprobs, cctx, n2, r2 = call(
        cross_forward, (pbuf, pbias, w_kv, w_cq, w_co, norms, n1),
        [((items * slots, ENC), bf16), ((items * slots, 2 * D), bf16), rowl, ((items, pairs, slots), f32), rowl, row, one],
        [row, row], "cross_forward")
    ff = w_in.shape[1]
    block_output, g_in, g_outer, grad_after, gn3 = call(
        feed_forward, (n2, cotangent, w_in, w_outer, norms),
        [rowl, ((D, ff), bf16), ((ff, D), bf16), row, gn],
        [rowl, ((rows, ff), bf16), ((rows, ff), f32), row, rowl, rowl], "feed_forward")
    g_kv, g_cq, g_co, patch_grad, grad_self, gn2 = call(
        cross_backward, (image, memory, query, cprobs, cctx, n2, r2, n1, grad_after, w_kv, w_cq, w_co, norms),
        [((ENC, 2 * D), bf16), ((D, D), bf16), ((D, D), bf16), (pbuf.shape, bf16), row, gn],
        [row, row, row, ((items * slots, 2 * D), bf16)], "cross_backward")
    g_qkv, g_out, text_grad, gn1 = call(
        self_backward, (text, mixed, probs, ctx, n1, r1, grad_self, w_qkv, w_out, norms),
        [((D, 3 * D), bf16), ((D, D), bf16), row, gn],
        [((rows, 3 * D), f32), row, ((rows, 3 * D), f32), ((rows, 3 * D), bf16)], "self_backward")
    g_norms = jnp.concatenate([gn1, gn2, gn3], axis=0)
    return block_output, text_grad, patch_grad, (g_qkv, g_out, g_cq, g_kv, g_co, g_in, g_outer), g_norms


MESH = pl.DeviceIdType.MESH
Z, X, Y, C = 4, 2, 2, 2
PLANE_FIRST = (0, 3)


class Place:
    def __init__(self):
        item, self.me = lax.axis_index("items"), lax.axis_index("patch")
        self.z, self.x, self.y, self.c = item // X, item % X, self.me // C, self.me % C
        z, x, y, c = self.z, self.x, self.y, self.c
        self.left = (item - X, self.me)
        self.right = (item + X, self.me)
        self.xdev = (z * X + (1 - x), self.me)
        self.ypeer, self.cpeer, self.dpeer = (1 - y) * C + c, y * C + (1 - c), (1 - y) * C + (1 - c)
        self.ydev, self.cdev, self.ddev = (item, self.ypeer), (item, self.cpeer), (item, self.dpeer)

    def at(self, zz, xx, yy, cc):
        return ((zz * X + xx) * Y + yy) * C + cc

    def greet(self, barrier):
        for dev in (self.xdev, self.ydev, self.cdev, self.ddev):
            pl.semaphore_signal(barrier, inc=1, device_id=dev, device_id_type=MESH)

        @pl.when(self.z > 0)
        def _():
            pl.semaphore_signal(barrier, inc=1, device_id=self.left, device_id_type=MESH)

        @pl.when(self.z < Z - 1)
        def _():
            pl.semaphore_signal(barrier, inc=1, device_id=self.right, device_id_type=MESH)

    def met(self, barrier):
        pl.semaphore_wait(barrier, 4 + (self.z > 0).astype(jnp.int32) + (self.z < Z - 1).astype(jnp.int32))

    def both(self, d, step):
        if d == 0:
            step(self.z, None)
            return

        @pl.when(self.z >= d)
        def _():
            step(self.z - d, True)

        @pl.when(self.z + d < Z)
        def _():
            step(self.z + d, False)


def gather_kernel(nw, plane_first, nx, *refs):
    shards = refs[:nw]
    sources = refs[nw : nw + nx]
    outs = refs[nw + nx : 2 * nw + nx]
    swaps = refs[2 * nw + nx : 2 * nw + 2 * nx]
    low = refs[2 * nw + 2 * nx : 3 * nw + 2 * nx]
    recv, sendx, sendy, sendc, sendl, sendr, local, psend, precv, plocal = refs[3 * nw + 2 * nx :]
    p = Place()
    z, x, y, c, me = p.z, p.x, p.y, p.c, p.me
    barrier = pltpu.get_barrier_semaphore()
    p.greet(barrier)
    for w in range(nw):
        low[w][...] = shards[w][...].astype(low[w].dtype)
    p.met(barrier)

    def send(w, block, dev, sem, own=False):
        pltpu.make_async_remote_copy(
            src_ref=low[w] if own else outs[w].at[block],
            dst_ref=outs[w].at[block],
            send_sem=sem.at[w],
            recv_sem=recv.at[w, block],
            device_id=dev,
            device_id_type=MESH,
        ).start()

    def arrived(w, block):
        pltpu.make_async_remote_copy(
            src_ref=outs[w].at[block],
            dst_ref=outs[w].at[block],
            send_sem=sendx.at[w],
            recv_sem=recv.at[w, block],
            device_id=p.xdev,
            device_id_type=MESH,
        ).wait_recv()

    every = range(nw)
    line = [w for w in every if w not in plane_first]
    plane = [w for w in every if w in plane_first]
    mine = p.at(z, x, y, c)

    def to_left(w, block, own=False):
        @pl.when(z > 0)
        def _():
            send(w, block, p.left, sendl, own)

    def to_right(w, block, own=False):
        @pl.when(z < Z - 1)
        def _():
            send(w, block, p.right, sendr, own)

    def to_x(w, block, own=False):
        send(w, block, p.xdev, sendx, own)

    def to_y(w, block, own=False):
        send(w, block, p.ydev, sendy, own)

    def to_core(w, block, own=False):
        send(w, block, p.cdev, sendc, own)

    for w in plane:
        to_x(w, mine, True)
        to_y(w, mine, True)
    for w in line:
        to_left(w, mine, True)
        to_right(w, mine, True)
        to_y(w, mine, True)
        to_x(w, mine, True)
    for w in plane:
        to_left(w, mine, True)
        to_right(w, mine, True)
    for w in every:
        to_core(w, mine, True)
        pltpu.make_async_copy(low[w], outs[w].at[mine], local.at[w]).start()
    for s in range(nx):
        here = swaps[s].shape[1]
        for k, (dev, peer) in enumerate(((p.ydev, p.ypeer), (p.cdev, p.cpeer), (p.ddev, p.dpeer))):
            pltpu.make_async_remote_copy(
                src_ref=sources[s].at[pl.ds(peer * here, here)],
                dst_ref=swaps[s].at[me],
                send_sem=psend.at[s, k],
                recv_sem=precv.at[s, k],
                device_id=dev,
                device_id_type=MESH,
            ).start()
        pltpu.make_async_copy(sources[s].at[pl.ds(me * here, here)], swaps[s].at[me], plocal.at[s]).start()

    def plane_x():
        for w in plane:
            block = p.at(z, 1 - x, y, c)
            arrived(w, block)
            to_y(w, block)
            to_left(w, block)
            to_right(w, block)
            to_core(w, block)

    def plane_y(xx):
        for w in plane:
            block = p.at(z, xx, 1 - y, c)
            arrived(w, block)
            to_left(w, block)
            to_right(w, block)
            to_core(w, block)

    def plane_z(zz, from_left):
        for xx, yy in ((x, y), (1 - x, y), (x, 1 - y), (1 - x, 1 - y)):
            for w in plane:
                block = p.at(zz, xx, yy, c)
                arrived(w, block)
                (to_right if from_left else to_left)(w, block)
                to_core(w, block)

    def line_z(zz, from_left):
        block = p.at(zz, x, y, c)
        for w in line:
            arrived(w, block)
            (to_right if from_left else to_left)(w, block)
            to_y(w, block)
            to_x(w, block)
            to_core(w, block)

    def line_y(zz, _):
        block = p.at(zz, x, 1 - y, c)
        for w in line:
            arrived(w, block)
            to_x(w, block)
            to_core(w, block)

    def line_x(zz, _):
        for yy in (y, 1 - y):
            block = p.at(zz, 1 - x, yy, c)
            for w in line:
                arrived(w, block)
                to_core(w, block)

    plane_x()
    p.both(1, line_z)
    plane_y(x)
    plane_y(1 - x)
    p.both(0, line_y)
    p.both(1, plane_z)
    p.both(2, line_z)
    p.both(1, line_y)
    p.both(0, line_x)
    p.both(2, plane_z)
    p.both(3, line_z)
    p.both(2, line_y)
    p.both(1, line_x)
    p.both(3, plane_z)
    p.both(3, line_y)
    p.both(2, line_x)
    p.both(3, line_x)
    for zz in range(Z):
        for xx in range(X):
            for yy in range(Y):
                for w in every:
                    arrived(w, p.at(zz, xx, yy, 1 - c))
    for w in every:
        pltpu.make_async_copy(low[w], outs[w].at[mine], local.at[w]).wait()

        def sent(count, sem):
            span = outs[w].at[pl.ds(0, count)]
            pltpu.make_async_copy(span, span, sem.at[w]).wait()

        wide = X * Y if w in plane else 1
        sent(1 if w in plane else Z * Y, sendx)
        sent(X if w in plane else Z, sendy)
        sent(Z * X * Y, sendc)
        for k in range(Z):
            @pl.when(z == k)
            def _():
                if k > 0:
                    sent(wide * (Z - k), sendl)
                if k < Z - 1:
                    sent(wide * (k + 1), sendr)
    for s in range(nx):
        here = swaps[s].shape[1]
        for k, dev in enumerate((p.ydev, p.cdev, p.ddev)):
            pltpu.make_async_remote_copy(
                src_ref=sources[s].at[pl.ds(0, here)],
                dst_ref=swaps[s].at[0],
                send_sem=psend.at[s, k],
                recv_sem=precv.at[s, k],
                device_id=dev,
                device_id_type=MESH,
            ).wait()
        pltpu.make_async_copy(sources[s].at[pl.ds(me * here, here)], swaps[s].at[me], plocal.at[s]).wait()


def gather_all(shards, kinds, swaps, plane_first=PLANE_FIRST, collective=0):
    nw, nx = len(shards), len(swaps)
    n = Z * X * Y * C
    anyspec = pl.BlockSpec(memory_space=pl.ANY)
    vm = pl.BlockSpec(memory_space=pltpu.VMEM)
    dma = pltpu.SemaphoreType.DMA
    out = pl.pallas_call(
        functools.partial(gather_kernel, nw, plane_first, nx),
        out_shape=[jax.ShapeDtypeStruct((n,) + s.shape, k) for s, k in zip(shards, kinds)]
        + [jax.ShapeDtypeStruct((Y * C, s.shape[0] // (Y * C)) + s.shape[1:], s.dtype) for s in swaps],
        in_specs=[vm] * nw + [anyspec] * nx,
        out_specs=[anyspec] * (nw + nx),
        scratch_shapes=[pltpu.VMEM(s.shape, k) for s, k in zip(shards, kinds)]
        + [dma((nw, n))] + [dma((nw,))] * 6 + [dma((nx, 3)), dma((nx, 3)), dma((nx,))],
        compiler_params=pltpu.CompilerParams(collective_id=collective, has_side_effects=True),
        name="gather",
    )(*shards, *swaps)
    return [o.reshape(n * o.shape[1], o.shape[2]) for o in out[:nw]], list(out[nw:])


step_rates = (0.05, 0.15, 0.05, 0.05, 0.3, 0.05, 0.05, 0.5)
step_decays = (0.01, 0.01, 0.01, 0.01, 0.01, 0.01, 0.01, 0.0)
BOTH = ("items", "patch")
STEP = 48


def adamw_step(master, gradient, first_moment, second_moment, rate, decay):
    first_new = 0.9 * first_moment + 0.1 * gradient
    second_new = 0.999 * second_moment + 0.001 * gradient * gradient
    step_size = first_new / (1.0 - 0.9**10) / (jnp.sqrt(second_new / (1.0 - 0.999**10)) + 1e-08)
    return (master - rate * (step_size + decay * master), first_new, second_new)


def pad_to(array, shape, value=0.0):
    return jnp.pad(array, [(0, n - k) for n, k in zip(shape, array.shape)], constant_values=value)


def on_device(direct, text, cotangent, patches, text_lengths, patch_mask, *state):
    masters, firsts, seconds = state[:8], state[8:16], state[16:]
    group, local = patch_mask.shape
    chunks = lax.axis_size("patch")
    items = group // chunks
    index = lax.axis_index("patch") * local + jnp.arange(local, dtype=jnp.int32)
    valid = (patch_mask > 0) & (index[None, :] < VALID)
    bias = pad_to(jnp.where(valid, 0.0, -10000.0).astype(f32), (group, 128), OUTSIDE)
    norms_low = masters[7].astype(bf16).astype(f32)
    if direct:
        wide = pad_to(norms_low, (8, 128))
        weights, (image, bias) = gather_all(
            list(masters[:7]) + [wide], [bf16] * 7 + [f32], [patches, bias]
        )
        norms = weights.pop().reshape(-1, 8, 128)[:, :6, : norms_low.shape[1]]
        norms = norms.transpose(1, 0, 2).reshape(6, D)
    else:
        weights = [lax.all_gather(m.astype(bf16), BOTH, axis=0, tiled=True) for m in masters[:7]]
        norms = lax.all_gather(norms_low, BOTH, axis=1, tiled=True)
        image = lax.all_to_all(patches.reshape(chunks, items, local, ENC), "patch", 0, 0)
        bias = lax.all_to_all(bias.reshape(chunks, items, 128), "patch", 0, 0)
    bias = bias[:, :, :STEP].transpose(1, 0, 2).reshape(items, chunks * STEP)
    block_output, text_grad, image_grad, grads, grad_norms = local_step(
        text, cotangent, image, bias, text_lengths, weights, norms
    )
    image_grad = lax.all_to_all(image_grad, "patch", 0, 0)
    patch_grad = image_grad.astype(f32).reshape(patches.shape)
    joined = lax.psum_scatter(
        jnp.concatenate([grads[k] for k in (0, 1, 2, 4, 5)], axis=1), BOTH, scatter_dimension=0, tiled=True
    )
    reduced = {}
    start = 0
    for k in (0, 1, 2, 4, 5):
        reduced[k] = joined[:, start : start + grads[k].shape[1]].astype(f32)
        start += grads[k].shape[1]
    for k in (3, 6):
        reduced[k] = lax.psum_scatter(grads[k], BOTH, scatter_dimension=0, tiled=True).astype(f32)
    reduced[7] = lax.psum_scatter(grad_norms, BOTH, scatter_dimension=1, tiled=True)
    updated = [
        adamw_step(masters[k], reduced[k], firsts[k], seconds[k], step_rates[k], step_decays[k])
        for k in range(8)
    ]
    return (block_output, text_grad, patch_grad, *[u[part] for part in range(3) for u in updated])


def solution(mesh):
    rows, cols = P(BOTH, None), P(None, BOTH)
    state = (*[rows] * 7, cols)
    direct = dict(mesh.shape) == {"items": Z * X, "patch": Y * C}
    return jax.shard_map(
        functools.partial(on_device, direct),
        mesh=mesh,
        in_specs=(rows, rows, P("items", "patch", None), P(BOTH), P("items", "patch"), *state * 3),
        out_specs=(rows, rows, P("items", "patch", None), *state * 3),
        check_vma=False,
    )
```

time: 1480 us -> 616 us (0.42)
  waiting for transfers between devices: 997 us -> 263 us
  Pallas kernels: 0 us -> 216 us
  matrix products: 149 us -> 0 us
  local copies, waits for them, and re-layouts: 159 us -> 23.2 us
  other arithmetic: 47.3 us -> 13.9 us
  blocking collectives: 97 us -> 78.3 us
    reduce_scatter x9 -> x3, waiting for transfers between devices: 688 us -> 262 us  [the longest x1 152 us: on_device(): lax.psum_scatter(jnp.concatenate([grads[k] for k in (0, 1, 2, 4, 5)], axi...]
    all_gather x9 -> x0, waiting for transfers between devices: 309 us -> none  [the longest x1 64.8 us: on_device(): lax.all_gather(w_inner.astype(bf16), ('items', 'patch'), axis=0, tiled=True)]
    pallas_call x0 -> x6, Pallas kernels: none -> 216 us  [the longest x5 115 us: call(): pl.pallas_call(body, out_shape=[jax.ShapeDtypeStruct(s, k) for s, k in ou...]
    dot_general x33 -> x0, matrix products: 149 us -> none  [the longest x7 35.5 us: matmul(): return jnp.dot(left_side, right_side, preferred_element_type=jnp.float32)]
    convert_element_type x13 -> x0, local copies, waits for them, and re-layouts: 77.5 us -> none  [the longest x4 46.6 us: on_device(): grad_memory = jnp.stack([grad_key, grad_value], axis=2).astype(bf16)]
    all_gather x3 -> x0, blocking collectives: 45.1 us -> none  [the longest x1 31.8 us: on_device(): lax.all_gather(norm_rows.astype(bf16), ('items', 'patch'), axis=1, tiled=...]
    unnamed x1, blocking collectives: 39.9 us -> 78.3 us
    reshape x6 -> x2, local copies, waits for them, and re-layouts: 35.8 us -> 1.39 us  [the longest x1 0.71 us: on_device(): norms = norms.transpose(1, 0, 2).reshape(6, D)]
  transfers between devices with their start and end apart: 18 -> 4, of which waited for: 15 -> 3; matrix products, arithmetic and copies ran while one was open for 19% -> 3% of each run, Pallas kernels for 0% -> 3%
where the time goes in v1:
time: 616 us; the launch traced here: 612 us
  waiting for transfers between devices  263 us (43%)
  Pallas kernels  216 us (35%)
  blocking collectives  78.3 us (13%)
  local copies, waits for them, and re-layouts  23.2 us (4%)
  between operations  14.1 us (2%)
  other arithmetic  13.9 us (2%)
    reduce_scatter x1, waiting for transfers between devices, on_device(): lax.psum_scatter(jnp.concatenate([grads[k] for k in (0, 1, 2, 4, 5)], axi...  152 us
    pallas_call x5, Pallas kernels, call(): pl.pallas_call(body, out_shape=[jax.ShapeDtypeStruct(s, k) for s, k in ou...  115 us
    reduce_scatter x2, waiting for transfers between devices, on_device(): lax.psum_scatter(grads[k], BOTH, scatter_dimension=0, tiled=True)  110 us
    pallas_call x1, Pallas kernels, gather_all(): pl.pallas_call(functools.partial(gather_kernel, nw, plane_first, nx), out...  101 us
    unnamed x1, blocking collectives  78.3 us
    unnamed x63, local copies, waits for them, and re-layouts  14.3 us
  transfers between devices with their start and end apart: 4, of which 3 were waited for; matrix products, arithmetic and copies ran while one was open for 3% of the time, Pallas kernels for 3%

profile of v1, /device:TPU:16, one launch (start us, length us, event | category | flops | bytes accessed | tf_op | source)
XLA Modules:
  0.0 612.5 jit_solution(2099523020188123116)
XLA Ops:
  7.3 4.5 copy.68.refs_8_
  13.0 101.4 %gather.1 = (bf16[32,24,2304]{2,1,0:T(8,128)(2,1)}, bf16[32,24,768]{2,1,0:T(8,128)(2,1)}, bf16[32,24,768]{2,1,0:T(8,128)(2,1)}, bf16[32,32,1536]{2,1,0:T(8,128)(...) custom-call(f32[24,2304]{1,0:T(8,128)} %refs_0_.1, ...), custom_call_target="tpu_custom_call" | custom-call | tf_op jit(solution)/shard_map/gather/pallas_call | solution.py:609
  117.5 11.3 %self_forward.1 = (bf16[320,2304]{1,0:T(8,128)(2,1)}, f32[8,480,40]{2,1,0:T(8,128)}, bf16[320,768]{1,0:T(8,128)(2,1)}, f32[320,768]{1,0:T(8,128)}, f32[320,1]{1,0:T(8,128)}) custom-call(s32[8]{0:T(128)} %lengths.1, bf16[320,768]{1,0:T(8,128)(2,1)} %text.3, bf16[768,2304]{1,0:T(8,128)(2,1)} %bitcast.16, bf16[768,768]{1,0:T(8,128)(2,1)} %bitcast.24, ...), custom_call_target="tpu_custom_call" | custom-call | tf_op jit(solution)/shard_map/self_forward/pallas_call | solution.py:321
  128.8 19.9 %cross_forward.1 = (bf16[1536,1024]{1,0:T(8,128)(2,1)}, bf16[1536,1536]{1,0:T(8,128)(2,1)}, bf16[320,768]{1,0:T(8,128)(2,1)}, f32[8,480,192]{2,1,0:T(8,128)}, bf...) custom-call(bf16[4,8,37,1024]{3,2,1,0:T(8,128)(2,1)} %get-tuple-element.64.patches, ...), custom_call_target="tpu_custom_call" | custom-call | tf_op jit(solution)/shard_map/cross_forward/pallas_call | solution.py:321
  148.6 32.7 %feed_forward.1 = (bf16[320,768]{1,0:T(8,128)(2,1)}, bf16[768,3072]{1,0:T(8,128)(2,1)}, bf16[3072,768]{1,0:T(8,128)(2,1)}, f32[320,768]{1,0:T(8,128)}, f32[2,768]{1,0:T(2,128)}) custom-call(f32[320,768]{1,0:T(8,128)} %get-tuple-element.73.normed_two.normed, bf16[320,768]{1,0:T(8,128)(2,1)} %cotangent.1, bf16[768,3072]{1,0:T(8,128)(2,1)} %bitcast.28, ...), custom_call_target="tpu_custom_call" | custom-call | tf_op jit(solution)/shard_map/feed_forward/pallas_call | solution.py:321
  181.4 33.8 %cross_backward.1 = (bf16[1024,1536]{1,0:T(8,128)(2,1)}, bf16[768,768]{1,0:T(8,128)(2,1)}, bf16[768,768]{1,0:T(8,128)(2,1)}, bf16[4,8,37,1024]{3,2,1,0:T(8,128)(...) custom-call(bf16[1536,1024]{1,0:T(8,128)(2,1)} %get-tuple-element.81.image, bf16[1536,1536]{1,0:T(8,128)(2,1)} %get-tuple-element.82.memory, ...), custom_call_target="tpu_custom_call" | custom-call | tf_op jit(solution)/shard_map/cross_backward/pallas_call | solution.py:321
  216.2 17.1 %self_backward.1 = (bf16[768,2304]{1,0:T(8,128)(2,1)}, bf16[768,768]{1,0:T(8,128)(2,1)}, f32[320,768]{1,0:T(8,128)}, f32[2,768]{1,0:T(2,128)}) custom-call(bf16[320,768]{1,0:T(8,128)(2,1)} %text.3, bf16[320,2304]{1,0:T(8,128)(2,1)} %get-tuple-element.77.mixed, f32[8,480,40]{2,1,0:T(8,128)} %get-tuple-element.78.probs, ...), custom_call_target="tpu_custom_call" | custom-call | tf_op jit(solution)/shard_map/self_backward/pallas_call | solution.py:321
  233.4 4.3 constant_dynamic-update-slice_fusion.4
  237.6 1.2 constant_dynamic-update-slice_fusion.3
  238.8 1.2 constant_dynamic-update-slice_fusion.2
  240.1 1.2 constant_dynamic-update-slice_fusion.1
  241.2 2.5 constant_dynamic-update-slice_fusion
  243.8 1.8 copy-done
  245.5 2.8 copy.71
  248.3 3.8 all-to-all-start
  252.2 78.3 %all-reduce.2 = f32[6,768]{1,0:T(8,128)S(1)} all-reduce(f32[6,768]{1,0:T(8,128)S(1)} %pad_maximum_fusion), channel_id=5, replica_groups=mesh['items'=8,'patch'=4] {'items','patch'}, use_global_device_ids=true, to_apply=%region_3.4.clone | all-reduce | flops 4608 | bytes 36864
  331.3 2.8 bitcast_convert_fusion
  334.7 2.0 multiply_subtract_fusion.3
  336.7 109.6 %reduce-scatter.9.cloned.1.call-done = bf16[96,768]{1,0:T(8,128)(2,1)} async-done(((bf16[3072,768]{1,0:T(8,128)(2,1)}), bf16[96,768]{1,0:T(8,128)(2,1)}) %reduce-scatter.9.cloned.1.call-update) | async-done | bytes 147472 | tf_op jit(solution)/shard_map/reduce_scatter | solution.py:676
  446.3 2.1 multiply_subtract_fusion
  448.4 151.8 %reduce-scatter.5.cloned.1.call-done = bf16[24,7680]{1,0:T(8,128)(2,1)} async-done(((bf16[768,7680]{1,0:T(8,128)(2,1)}), bf16[24,7680]{1,0:T(8,128)(2,1)}) %reduce-scatter.5.cloned.1.call-update) | async-done | bytes 368656 | tf_op jit(solution)/shard_map/reduce_scatter | solution.py:667
  600.2 2.2 multiply_subtract_fusion.1
  602.3 1.8 multiply_subtract_fusion.2
  604.2 1.7 multiply_subtract_fusion.4
  (79 shorter events, 6.8 us)
Async XLA Ops:
  7.2 327.5 %reduce-scatter.7.cloned.1.call-start = ((), (), s32[]{:S(2)}) async-start(), calls=%async_computation.5 | async-start | bytes 3244032 | tf_op jit(solution)/shard_map/reduce_scatter | solution.py:676
  215.2 231.1 %reduce-scatter.9.cloned.1.call-start = ((), (), s32[]{:S(2)}) async-start(), calls=%async_computation.6 | async-start | bytes 4866048 | tf_op jit(solution)/shard_map/reduce_scatter | solution.py:676
  215.9 384.2 %reduce-scatter.5.cloned.1.call-start = ((), (), s32[]{:S(2)}) async-start(), calls=%async_computation.4 | async-start | bytes 12165120 | tf_op jit(solution)/shard_map/reduce_scatter | solution.py:667
  216.2 25.1 %slice-start = ((s8[4718592]{0:T(1024)(128)(4,1)}), s8[524288]{0:T(1024)(128)(4,1)S(1)}, s32[]{:S(2)}) async-start(s8[4718592]{0:T(1024)(128)(4,1)} %bitcast.26), calls=%async_computation.7 | async-start | bytes 1048576
  233.3 5.5 copy-start.2
  233.3 7.9 %slice-start.1 = ((s8[4718592]{0:T(1024)(128)(4,1)}), s8[4194304]{0:T(1024)(128)(4,1)S(1)}, s32[]{:S(2)}) async-start(s8[4718592]{0:T(1024)(128)(4,1)} %bitcast.26), calls=%async_computation.8 | async-start | bytes 8388608
  248.3 82.2 %copy-start.25 = (f32[6,24]{1,0:T(8,128)S(1)}, f32[6,24]{1,0:T(8,128)}, u32[]{:S(2)}) copy-start(f32[6,24]{1,0:T(8,128)} %param.49) | copy-start | bytes 1732
  248.3 82.2 %copy-start.26 = (f32[6,24]{1,0:T(8,128)S(1)}, f32[6,24]{1,0:T(8,128)}, u32[]{:S(2)}) copy-start(f32[6,24]{1,0:T(8,128)} %param.57) | copy-start | bytes 1732
  248.3 82.9 %all-to-all-start = ((bf16[4,8,37,1024]{3,1,2,0:T(8,128)(2,1)}), bf16[4,8,37,1024]{3,1,2,0:T(8,128)(2,1)S(1)}, u32[]{:S(2)}, u32[]{:S(2)}) async-start(bf16[4,8,37,1024]{3,1,2,0:T(8,128)(2,1)} %copy.71), calls=%async_computation | async-start | bytes 4849664 | tf_op jit(solution)/shard_map/all_to_all | solution.py:665
  331.2 115.0 %copy-start.4 = (f32[96,768]{1,0:T(8,128)S(1)}, f32[96,768]{1,0:T(8,128)}, u32[]{:S(2)}) copy-start(f32[96,768]{1,0:T(8,128)} %refs_6_.1) | copy-start | bytes 884740
  331.2 115.0 %copy-start.8 = (f32[96,768]{1,0:T(8,128)S(1)}, f32[96,768]{1,0:T(8,128)}, u32[]{:S(2)}) copy-start(f32[96,768]{1,0:T(8,128)} %param.48) | copy-start | bytes 884740
  331.2 268.9 %copy-start.5 = (f32[24,3072]{1,0:T(8,128)S(1)}, f32[24,3072]{1,0:T(8,128)}, u32[]{:S(2)}) copy-start(f32[24,3072]{1,0:T(8,128)} %refs_5_.1) | copy-start | bytes 884740
  334.0 268.3 %copy-start.6 = (f32[24,2304]{1,0:T(8,128)S(1)}, f32[24,2304]{1,0:T(8,128)}, u32[]{:S(2)}) copy-start(f32[24,2304]{1,0:T(8,128)} %refs_0_.1) | copy-start | bytes 663556
  334.0 268.3 %copy-start.12 = (f32[24,2304]{1,0:T(8,128)S(1)}, f32[24,2304]{1,0:T(8,128)}, u32[]{:S(2)}) copy-start(f32[24,2304]{1,0:T(8,128)} %param.42) | copy-start | bytes 663556
  334.1 268.3 %copy-start.13 = (f32[24,2304]{1,0:T(8,128)S(1)}, f32[24,2304]{1,0:T(8,128)}, u32[]{:S(2)}) copy-start(f32[24,2304]{1,0:T(8,128)} %param.50) | copy-start | bytes 663556
  334.1 270.1 %copy-start.9 = (f32[24,768]{1,0:T(8,128)S(1)}, f32[24,768]{1,0:T(8,128)}, u32[]{:S(2)}) copy-start(f32[24,768]{1,0:T(8,128)} %refs_1_.1) | copy-start | bytes 221188
  334.1 270.1 %copy-start.10 = (f32[24,768]{1,0:T(8,128)S(1)}, f32[24,768]{1,0:T(8,128)}, u32[]{:S(2)}) copy-start(f32[24,768]{1,0:T(8,128)} %refs_2_.1) | copy-start | bytes 221188
  334.1 270.1 %copy-start.11 = (f32[24,768]{1,0:T(8,128)S(1)}, f32[24,768]{1,0:T(8,128)}, u32[]{:S(2)}) copy-start(f32[24,768]{1,0:T(8,128)} %refs_4_.1) | copy-start | bytes 221188
  334.1 270.1 %copy-start.14 = (f32[24,768]{1,0:T(8,128)S(1)}, f32[24,768]{1,0:T(8,128)}, u32[]{:S(2)}) copy-start(f32[24,768]{1,0:T(8,128)} %param.46) | copy-start | bytes 221188
  334.1 270.1 %copy-start.15 = (f32[24,768]{1,0:T(8,128)S(1)}, f32[24,768]{1,0:T(8,128)}, u32[]{:S(2)}) copy-start(f32[24,768]{1,0:T(8,128)} %param.54) | copy-start | bytes 221188
  334.1 270.1 %copy-start.16 = (f32[24,768]{1,0:T(8,128)S(1)}, f32[24,768]{1,0:T(8,128)}, u32[]{:S(2)}) copy-start(f32[24,768]{1,0:T(8,128)} %param.52) | copy-start | bytes 221188
  334.1 270.1 %copy-start.17 = (f32[24,768]{1,0:T(8,128)S(1)}, f32[24,768]{1,0:T(8,128)}, u32[]{:S(2)}) copy-start(f32[24,768]{1,0:T(8,128)} %param.44) | copy-start | bytes 221188
  334.1 270.1 %copy-start.18 = (f32[24,768]{1,0:T(8,128)S(1)}, f32[24,768]{1,0:T(8,128)}, u32[]{:S(2)}) copy-start(f32[24,768]{1,0:T(8,128)} %param.51) | copy-start | bytes 221188
  334.1 270.1 %copy-start.19 = (f32[24,768]{1,0:T(8,128)S(1)}, f32[24,768]{1,0:T(8,128)}, u32[]{:S(2)}) copy-start(f32[24,768]{1,0:T(8,128)} %param.43) | copy-start | bytes 221188
  (9 other events, 33.3 us)
Sparse Core Ops, SparseCore 0:
  215.3 119.3 reduce-scatter.6
  340.2 106.0 reduce-scatter.8
  453.4 146.6 reduce-scatter.4

commit v2 on v1

--- a/solution.py
+++ b/solution.py
@@ -115,7 +115,9 @@
         put_k(j, dot_tn(inner[j], expand(query(j))) * SCALE)
 
 
-def self_forward(lengths, text, w_qkv, w_out, norms, mixed, probs, ctx, normed, inverse, mix, context):
+def self_forward(lengths, text, w_qkv, w_out, blocks, mixed, probs, ctx, normed, inverse, norms, mix, context):
+    spread(blocks, norms)
+
     def project(cols):
         got = dot(text[...], w_qkv[:, cols]).astype(bf16)
         mixed[:, cols] = got
@@ -143,11 +145,14 @@
     inverse[...] = r
 
 
-def self_backward(text, mixed, probs, ctx, normed, inverse, grad_after, w_qkv, w_out, norms,
-                  g_qkv, g_out, text_grad, g_norm, mix, grad_ctx, grad_mix, low_mix):
+def self_backward(text, mixed, probs, ctx, normed, inverse, grad_after, w_qkv, w_out, norms, g_second, g_third,
+                  g_qkv, g_out, text_grad, g_blocks, mix, grad_ctx, grad_mix, low_mix):
     grad_pre, grad_gain, grad_shift = norm_backward(grad_after[...], normed[...], inverse[...], norms[0:1, :])
-    g_norm[0:1, :] = grad_gain
-    g_norm[1:2, :] = grad_shift
+    rows = jnp.concatenate([grad_gain, grad_shift, g_second[...], g_third[...], jnp.zeros((2, D), f32)], axis=0)
+    width = D // g_blocks.shape[0]
+    for b in range(g_blocks.shape[0]):
+        g_blocks[b, :, :width] = rows[:, width * b : width * (b + 1)]
+        g_blocks[b, :, width:] = jnp.zeros((8, g_blocks.shape[2] - width), f32)
     low = grad_pre.astype(bf16)
     g_out[...] = dot_tn(ctx[...], low).astype(bf16)
     grad_ctx[...] = dot_nt(low, w_out[...]).astype(bf16).astype(f32)
@@ -181,25 +186,27 @@
     tiles(3 * D, 256, weights)
 
 
-def cross_forward(patches, bias, w_kv, w_q, w_out, norms, normed_one,
-                  image, memory, query, probs, ctx, normed, inverse, context, wide):
-    chunks, items, local, _ = patches.shape
+def spread(blocks, norms):
+    width = D // blocks.shape[0]
+    for b in range(blocks.shape[0]):
+        norms[:, width * b : width * (b + 1)] = blocks[b, :, :width]
+
+
+def cross_forward(image, masks, w_kv, w_q, w_out, norms, normed_one,
+                  memory, query, probs, ctx, normed, inverse, bias, context, wide, flat):
+    items = masks.shape[1]
     slots = bias.shape[1]
-    step = slots // chunks
-    image[...] = jnp.zeros_like(image)
-
-    def lay(item, carry):
-        for c in range(chunks):
-            start = pl.multiple_of(item * slots + c * step, 16)
-            image[pl.ds(start, local), :] = patches[c, item]
+    local = slots // masks.shape[0]
+    for c in range(masks.shape[0]):
+        bias[:, local * c : local * (c + 1)] = masks[c, :, :local]
+
+    def project(k, carry):
+        got = dot(image[...], w_kv[:, pl.ds(pl.multiple_of(2 * PAIR * k, 2 * PAIR), 2 * PAIR)]).astype(bf16).astype(f32)
+        flat[2 * k] = got[:, :PAIR]
+        flat[2 * k + 1] = got[:, PAIR:]
         return carry
 
-    lax.fori_loop(0, items, lay, 0)
-
-    def project(cols):
-        memory[:, cols] = dot(image[...], w_kv[:, cols]).astype(bf16)
-
-    tiles(2 * D, 256, project)
+    lax.fori_loop(0, PAIRS, project, 0)
     after = normed_one[...] * norms[0:1, :] + norms[1:2, :]
     low = dot(after.astype(bf16), w_q[...]).astype(bf16)
     query[...] = low
@@ -207,11 +214,13 @@
 
     def one(item, carry):
         rows = pl.ds(pl.multiple_of(item * TEXT, 8), TEXT)
-        slot = pl.ds(pl.multiple_of(item * slots, 16), slots)
+        every = pl.ds(item, slots, stride=items)
+        for j in range(2 * PAIRS):
+            memory[item, :, pair_cols(j)] = flat[j, every, :].astype(bf16)
         attend_forward(
             lambda j: wide[rows, pair_cols(j)],
-            lambda j: memory[slot, pair_cols(j)],
-            lambda j: memory[slot, pair_cols(j, D)],
+            lambda j: memory[item, :, pair_cols(j)],
+            lambda j: memory[item, :, pair_cols(j, D)],
             bias[pl.ds(item, 1), :], probs, item, context, rows,
         )
         return carry
@@ -226,10 +235,8 @@
 
 def cross_backward(image, memory, query, probs, ctx, normed, inverse, normed_one, grad_after,
                    w_kv, w_q, w_out, norms,
-                   g_kv, g_q, g_out, patch_grad, grad_self, g_norm, wide, grad_ctx, grad_q, grad_mem):
-    chunks, items, local, _ = patch_grad.shape
-    slots = image.shape[0] // items
-    step = slots // chunks
+                   g_kv, g_q, g_out, image_grad, grad_self, g_norm, wide, grad_ctx, grad_q, flat, grad_mem):
+    items, slots = memory.shape[:2]
     grad_pre, grad_gain, grad_shift = norm_backward(grad_after[...], normed[...], inverse[...], norms[2:3, :])
     g_norm[0:1, :] = grad_gain
     g_norm[1:2, :] = grad_shift
@@ -240,22 +247,22 @@
 
     def one(item, carry):
         rows = pl.ds(pl.multiple_of(item * TEXT, 8), TEXT)
-        slot = pl.ds(pl.multiple_of(item * slots, 16), slots)
+        every = pl.ds(item, slots, stride=items)
 
         def put_q(j, value):
             grad_q[rows, pair_cols(j)] = value
 
         def put(start):
             def store(j, value):
-                grad_mem[slot, pair_cols(j, start)] = value.astype(bf16)
+                flat[start + j, every, :] = value
             return store
 
         attend_backward(
             lambda j: wide[rows, pair_cols(j)],
-            lambda j: memory[slot, pair_cols(j)],
-            lambda j: memory[slot, pair_cols(j, D)],
+            lambda j: memory[item, :, pair_cols(j)],
+            lambda j: memory[item, :, pair_cols(j, D)],
             probs, item, lambda j: grad_ctx[rows, pair_cols(j)],
-            put_q, put(0), put(D),
+            put_q, put(0), put(PAIRS),
         )
         return carry
 
@@ -264,20 +271,18 @@
     after = (normed_one[...] * norms[0:1, :] + norms[1:2, :]).astype(bf16)
     g_q[...] = dot_tn(after, low_q).astype(bf16)
     grad_self[...] = grad_pre + dot_nt(low_q, w_q[...])
+    for j in range(2 * PAIRS):
+        grad_mem[:, pair_cols(j)] = flat[j].astype(bf16)
 
     def weights(cols):
         g_kv[:, cols] = dot_tn(image[...], grad_mem[:, cols]).astype(bf16)
 
     tiles(2 * D, 256, weights)
 
-    def back(item, carry):
-        slot = pl.ds(pl.multiple_of(item * slots, 16), slots)
-        got = dot_nt(grad_mem[slot, :], w_kv[...])
-        for c in range(chunks):
-            patch_grad[c, item] = got[c * step : c * step + local].astype(bf16)
-        return carry
-
-    lax.fori_loop(0, items, back, 0)
+    def back(cols):
+        image_grad[:, cols] = dot_nt(grad_mem[...], w_kv[cols, :]).astype(bf16)
+
+    tiles(ENC, 256, back)
 
 
 def feed_forward(normed_two, cotangent, w_inner, w_outer, norms,
@@ -329,39 +334,56 @@
     )(*args)
 
 
-def local_step(text, cotangent, pbuf, pbias, lengths, ws, norms):
+def adamw(count, decays, rates, *refs):
+    masters, firsts, seconds, grads = (refs[count * i : count * (i + 1)] for i in range(4))
+    image_low = refs[4 * count]
+    new_m, new_f, new_s = (refs[4 * count + 1 + count * i : 4 * count + 1 + count * (i + 1)] for i in range(3))
+    image_grad = refs[7 * count + 1]
+    for k in range(count):
+        rows, cols = masters[k].shape
+        gradient = grads[k][:rows, :cols]
+        first = 0.9 * firsts[k][...] + 0.1 * gradient
+        second = 0.999 * seconds[k][...] + 0.001 * gradient * gradient
+        step = first / (1.0 - 0.9**10) / (jnp.sqrt(second / (1.0 - 0.999**10)) + 1e-08)
+        master = masters[k][...]
+        new_m[k][...] = master - rates[k] * (step + decays[k] * master)
+        new_f[k][...] = first
+        new_s[k][...] = second
+    image_grad[...] = image_low[...].astype(f32)
+
+
+def local_step(text, cotangent, image, masks, lengths, ws, blocks):
     w_qkv, w_out, w_cq, w_kv, w_co, w_in, w_outer = ws
     rows = text.shape[0]
-    items = rows // TEXT
-    slots = pbias.shape[1]
+    slots, items, _ = image.shape
+    image = image.reshape(slots * items, ENC)
     pairs = HEADS * TEXT
     row = ((rows, D), f32)
     rowl = ((rows, D), bf16)
     one = ((rows, 1), f32)
     gn = ((2, D), f32)
-    mixed, probs, ctx, n1, r1 = call(
-        self_forward, (lengths, text, w_qkv, w_out, norms),
-        [((rows, 3 * D), bf16), ((items, pairs, TEXT), f32), rowl, row, one],
+    mixed, probs, ctx, n1, r1, norms = call(
+        self_forward, (lengths, text, w_qkv, w_out, blocks),
+        [((rows, 3 * D), bf16), ((items, pairs, TEXT), f32), rowl, row, one, ((8, D), f32)],
         [((rows, 3 * D), f32), row], "self_forward", smem=1)
-    image, memory, query, cprobs, cctx, n2, r2 = call(
-        cross_forward, (pbuf, pbias, w_kv, w_cq, w_co, norms, n1),
-        [((items * slots, ENC), bf16), ((items * slots, 2 * D), bf16), rowl, ((items, pairs, slots), f32), rowl, row, one],
-        [row, row], "cross_forward")
+    memory, query, cprobs, cctx, n2, r2 = call(
+        cross_forward, (image, masks, w_kv, w_cq, w_co, norms, n1),
+        [((items, slots, 2 * D), bf16), rowl, ((items, pairs, slots), f32), rowl, row, one],
+        [((items, slots), f32), row, row, ((2 * PAIRS, items * slots, PAIR), f32)], "cross_forward")
     ff = w_in.shape[1]
     block_output, g_in, g_outer, grad_after, gn3 = call(
         feed_forward, (n2, cotangent, w_in, w_outer, norms),
         [rowl, ((D, ff), bf16), ((ff, D), bf16), row, gn],
         [rowl, ((rows, ff), bf16), ((rows, ff), f32), row, rowl, rowl], "feed_forward")
-    g_kv, g_cq, g_co, patch_grad, grad_self, gn2 = call(
+    g_kv, g_cq, g_co, image_grad, grad_self, gn2 = call(
         cross_backward, (image, memory, query, cprobs, cctx, n2, r2, n1, grad_after, w_kv, w_cq, w_co, norms),
-        [((ENC, 2 * D), bf16), ((D, D), bf16), ((D, D), bf16), (pbuf.shape, bf16), row, gn],
-        [row, row, row, ((items * slots, 2 * D), bf16)], "cross_backward")
-    g_qkv, g_out, text_grad, gn1 = call(
-        self_backward, (text, mixed, probs, ctx, n1, r1, grad_self, w_qkv, w_out, norms),
-        [((D, 3 * D), bf16), ((D, D), bf16), row, gn],
+        [((ENC, 2 * D), bf16), ((D, D), bf16), ((D, D), bf16), (image.shape, bf16), row, gn],
+        [row, row, row, ((2 * PAIRS, items * slots, PAIR), f32), ((items * slots, 2 * D), bf16)], "cross_backward")
+    g_qkv, g_out, text_grad, g_blocks = call(
+        self_backward, (text, mixed, probs, ctx, n1, r1, grad_self, w_qkv, w_out, norms, gn2, gn3),
+        [((D, 3 * D), bf16), ((D, D), bf16), row, (blocks.shape, f32)],
         [((rows, 3 * D), f32), row, ((rows, 3 * D), f32), ((rows, 3 * D), bf16)], "self_backward")
-    g_norms = jnp.concatenate([gn1, gn2, gn3], axis=0)
-    return block_output, text_grad, patch_grad, (g_qkv, g_out, g_cq, g_kv, g_co, g_in, g_outer), g_norms
+    return block_output, text_grad, image_grad, (g_qkv, g_out, g_cq, g_kv, g_co, g_in, g_outer), g_blocks
 
 
 MESH = pl.DeviceIdType.MESH
@@ -412,19 +434,38 @@
             step(self.z + d, False)
 
 
-def gather_kernel(nw, plane_first, nx, *refs):
+def patch_bias(mask, first, valid):
+    index = first + lax.broadcasted_iota(jnp.int32, mask.shape, 1)
+    return jnp.where((mask > 0) & (index < valid), 0.0, -10000.0).astype(f32)
+
+
+def gather_kernel(nw, plane_first, valid, *refs):
     shards = refs[:nw]
-    sources = refs[nw : nw + nx]
-    outs = refs[nw + nx : 2 * nw + nx]
-    swaps = refs[2 * nw + nx : 2 * nw + 2 * nx]
-    low = refs[2 * nw + 2 * nx : 3 * nw + 2 * nx]
-    recv, sendx, sendy, sendc, sendl, sendr, local, psend, precv, plocal = refs[3 * nw + 2 * nx :]
+    image, mask = refs[nw : nw + 2]
+    outs = refs[nw + 2 : 2 * nw + 2]
+    swaps = refs[2 * nw + 2 : 2 * nw + 4]
+    low = refs[2 * nw + 4 : 3 * nw + 4]
+    bias = refs[3 * nw + 4]
+    recv, sendx, sendy, sendc, sendl, sendr, local, psend, precv, plocal = refs[3 * nw + 5 :]
     p = Place()
     z, x, y, c, me = p.z, p.x, p.y, p.c, p.me
     barrier = pltpu.get_barrier_semaphore()
     p.greet(barrier)
-    for w in range(nw):
+    for w in range(nw - 1):
         low[w][...] = shards[w][...].astype(low[w].dtype)
+    low[nw - 1][...] = jnp.zeros(low[nw - 1].shape, f32)
+    rows, cols = shards[nw - 1].shape
+    low[nw - 1][:rows, :cols] = shards[nw - 1][...].astype(bf16).astype(f32)
+    slots = mask.shape[1]
+    bias[...] = jnp.zeros(bias.shape, f32)
+    bias[:, :slots] = patch_bias(mask[...], me * slots, valid)
+    here = mask.shape[0] // (Y * C)
+    peers = ((p.ydev, p.ypeer), (p.cdev, p.cpeer), (p.ddev, p.dpeer))
+
+    def part(s, peer):
+        rows = pl.ds(pl.multiple_of(peer * here, here), here)
+        return bias.at[rows] if s else image.at[:, rows]
+
     p.met(barrier)
 
     def send(w, block, dev, sem, own=False):
@@ -485,18 +526,17 @@
     for w in every:
         to_core(w, mine, True)
         pltpu.make_async_copy(low[w], outs[w].at[mine], local.at[w]).start()
-    for s in range(nx):
-        here = swaps[s].shape[1]
-        for k, (dev, peer) in enumerate(((p.ydev, p.ypeer), (p.cdev, p.cpeer), (p.ddev, p.dpeer))):
+    for s in range(2):
+        for k, (dev, peer) in enumerate(peers):
             pltpu.make_async_remote_copy(
-                src_ref=sources[s].at[pl.ds(peer * here, here)],
+                src_ref=part(s, peer),
                 dst_ref=swaps[s].at[me],
                 send_sem=psend.at[s, k],
                 recv_sem=precv.at[s, k],
                 device_id=dev,
                 device_id_type=MESH,
             ).start()
-        pltpu.make_async_copy(sources[s].at[pl.ds(me * here, here)], swaps[s].at[me], plocal.at[s]).start()
+        pltpu.make_async_copy(part(s, me), swaps[s].at[me], plocal.at[s]).start()
 
     def plane_x():
         for w in plane:
@@ -586,55 +626,258 @@
                     sent(wide * (Z - k), sendl)
                 if k < Z - 1:
                     sent(wide * (k + 1), sendr)
-    for s in range(nx):
-        here = swaps[s].shape[1]
-        for k, dev in enumerate((p.ydev, p.cdev, p.ddev)):
+    for s in range(2):
+        for k, (dev, peer) in enumerate(peers):
             pltpu.make_async_remote_copy(
-                src_ref=sources[s].at[pl.ds(0, here)],
-                dst_ref=swaps[s].at[0],
+                src_ref=part(s, peer),
+                dst_ref=swaps[s].at[me],
                 send_sem=psend.at[s, k],
                 recv_sem=precv.at[s, k],
                 device_id=dev,
                 device_id_type=MESH,
             ).wait()
-        pltpu.make_async_copy(sources[s].at[pl.ds(me * here, here)], swaps[s].at[me], plocal.at[s]).wait()
-
-
-def gather_all(shards, kinds, swaps, plane_first=PLANE_FIRST, collective=0):
-    nw, nx = len(shards), len(swaps)
+        pltpu.make_async_copy(part(s, me), swaps[s].at[me], plocal.at[s]).wait()
+
+
+def gather_all(shards, image, mask, valid, plane_first=PLANE_FIRST, collective=0):
+    nw = len(shards)
     n = Z * X * Y * C
+    shapes = [s.shape for s in shards[:-1]] + [(8, 128)]
+    kinds = [bf16] * (nw - 1) + [f32]
+    slots, group, width = image.shape
+    here = group // (Y * C)
     anyspec = pl.BlockSpec(memory_space=pl.ANY)
     vm = pl.BlockSpec(memory_space=pltpu.VMEM)
     dma = pltpu.SemaphoreType.DMA
     out = pl.pallas_call(
-        functools.partial(gather_kernel, nw, plane_first, nx),
-        out_shape=[jax.ShapeDtypeStruct((n,) + s.shape, k) for s, k in zip(shards, kinds)]
-        + [jax.ShapeDtypeStruct((Y * C, s.shape[0] // (Y * C)) + s.shape[1:], s.dtype) for s in swaps],
-        in_specs=[vm] * nw + [anyspec] * nx,
-        out_specs=[anyspec] * (nw + nx),
-        scratch_shapes=[pltpu.VMEM(s.shape, k) for s, k in zip(shards, kinds)]
-        + [dma((nw, n))] + [dma((nw,))] * 6 + [dma((nx, 3)), dma((nx, 3)), dma((nx,))],
+        functools.partial(gather_kernel, nw, plane_first, valid),
+        out_shape=[jax.ShapeDtypeStruct((n,) + s, k) for s, k in zip(shapes, kinds)]
+        + [
+            jax.ShapeDtypeStruct((Y * C, slots, here, width), image.dtype),
+            jax.ShapeDtypeStruct((Y * C, here, 128), f32),
+        ],
+        in_specs=[vm] * nw + [anyspec, vm],
+        out_specs=[anyspec] * (nw + 2),
+        scratch_shapes=[pltpu.VMEM(s, k) for s, k in zip(shapes, kinds)]
+        + [pltpu.VMEM((group, 128), f32)]
+        + [dma((nw, n))] + [dma((nw,))] * 6 + [dma((2, 3)), dma((2, 3)), dma((2,))],
         compiler_params=pltpu.CompilerParams(collective_id=collective, has_side_effects=True),
         name="gather",
-    )(*shards, *swaps)
-    return [o.reshape(n * o.shape[1], o.shape[2]) for o in out[:nw]], list(out[nw:])
+    )(*shards, image, mask)
+    whole = [o.reshape(n * o.shape[1], o.shape[2]) for o in out[: nw - 1]]
+    return whole, out[nw - 1], out[nw].reshape(Y * C * slots, here, width), out[nw + 1]
+
+
+def scatter_kernel(nw, plane_first, *refs):
+    grads = refs[:nw]
+    source = refs[nw]
+    outs = refs[nw + 1 : 2 * nw + 1]
+    swapped = refs[2 * nw + 1]
+    rest = refs[2 * nw + 2 :]
+    own, from_core, from_x, from_y, from_l, from_r = (rest[nw * i : nw * (i + 1)] for i in range(6))
+    (load, rcore, rx, ry, rl, rr, score, sx, sy, sl, sr, psend, precv, plocal) = rest[6 * nw :]
+    p = Place()
+    z, x, y, c, me = p.z, p.x, p.y, p.c, p.me
+    every = range(nw)
+    line = [w for w in every if w not in plane_first]
+    plane = [w for w in every if w in plane_first]
+    half = z // 2
+    near = z * (1 - half) + (Z - 1 - z) * half
+
+    def target(k):
+        place = (Z - 1, 2 - 2 * near, 1 + near, near)[k]
+        return half * (Z - 1) + (1 - 2 * half) * place
+
+    def copy(src, dst, send_sem, recv_sem, dev):
+        return pltpu.make_async_remote_copy(
+            src_ref=src, dst_ref=dst, send_sem=send_sem, recv_sem=recv_sem, device_id=dev, device_id_type=MESH
+        )
+
+    def arrived(dst, sem):
+        copy(dst, dst, score.at[0], sem, p.cdev).wait_recv()
+
+    def loads(w, t):
+        return pltpu.make_async_copy(grads[w].at[pl.ds(t * X * Y, X * Y), c], own[w].at[pl.ds(t * X * Y, X * Y)], load.at[w, t])
+
+    def add(w, at, count, ref, start):
+        def one(i, carry):
+            mine = own[w]
+            mine[at + i] = (mine[at + i].astype(f32) + ref[start + i].astype(f32)).astype(mine.dtype)
+            return carry
+
+        if count == 1:
+            one(0, 0)
+        else:
+            lax.fori_loop(0, count, one, 0)
+
+    def begin(k):
+        t = target(k)
+        for w in every:
+            loads(w, t).start()
+            span = pl.ds(t * X * Y, X * Y)
+            copy(grads[w].at[span, 1 - c], from_core[w].at[span], score.at[w], rcore.at[w, t], p.cdev).start()
+
+    def core(k):
+        t = target(k)
+        for w in line + plane:
+            loads(w, t).wait()
+            span = pl.ds(t * X * Y, X * Y)
+            arrived(from_core[w].at[span], rcore.at[w, t])
+            add(w, t * X * Y, X * Y, from_core[w], t * X * Y)
+            if w in line:
+                copy(own[w].at[pl.ds((t * X + 1 - x) * Y, Y)], from_x[w].at[pl.ds(t * Y, Y)], sx.at[w], rx.at[w, t], p.xdev).start()
+
+    def across(k):
+        t = target(k)
+        for w in line:
+            arrived(from_x[w].at[pl.ds(t * Y, Y)], rx.at[w, t])
+            add(w, (t * X + x) * Y, Y, from_x[w], t * Y)
+            copy(own[w].at[(t * X + x) * Y + 1 - y], from_y[w].at[t], sy.at[w], ry.at[w, t], p.ydev).start()
+
+    def along(k, ws, first, count):
+        t = target(k)
+
+        def span(ref):
+            return ref.at[pl.ds(first(t), count)]
+
+        def slot(ref):
+            return ref.at[pl.ds(t * count, count)]
+
+        def take(w, ref, sem):
+            arrived(slot(ref), sem.at[w, t])
+            add(w, first(t), count, ref, t * count)
+
+        if k < Z - 1:
+            @pl.when(t > z)
+            def _():
+                for w in ws:
+                    @pl.when(z > 0)
+                    def _():
+                        take(w, from_l[w], rl)
+
+                    copy(span(own[w]), slot(from_l[w]), sr.at[w], rl.at[w, t], p.right).start()
+
+            @pl.when(t < z)
+            def _():
+                for w in ws:
+                    @pl.when(z < Z - 1)
+                    def _():
+                        take(w, from_r[w], rr)
+
+                    copy(span(own[w]), slot(from_r[w]), sl.at[w], rr.at[w, t], p.left).start()
+        else:
+            for w in ws:
+                @pl.when(z > 0)
+                def _():
+                    take(w, from_l[w], rl)
+
+                @pl.when(z < Z - 1)
+                def _():
+                    take(w, from_r[w], rr)
+
+    def down(k):
+        t = target(k)
+        for w in line:
+            arrived(from_y[w].at[t], ry.at[w, t])
+            add(w, (t * X + x) * Y + y, 1, from_y[w], t)
+        along(k, line, lambda t: (t * X + x) * Y + y, 1)
+
+    barrier = pltpu.get_barrier_semaphore()
+    p.greet(barrier)
+    p.met(barrier)
+    begin(0)
+    here = swapped.shape[1] // (Y * C)
+    place = swapped.at[:, pl.ds(pl.multiple_of(me * here, here), here)]
+    peers = ((p.ydev, p.ypeer), (p.cdev, p.cpeer), (p.ddev, p.dpeer))
+    for k, (dev, peer) in enumerate(peers):
+        copy(source.at[peer], place, psend.at[k], precv.at[k], dev).start()
+    pltpu.make_async_copy(source.at[me], place, plocal).start()
+    for k in range(Z + 2):
+        if k + 1 < Z:
+            begin(k + 1)
+        if k < Z:
+            core(k)
+            along(k, plane, lambda t: t * X * Y, X * Y)
+        if 1 <= k <= Z:
+            across(k - 1)
+        if k == Z - 1:
+            for w in plane:
+                for xx in range(X):
+                    copy(own[w].at[(z * X + xx) * Y + 1 - y], from_y[w].at[xx], sy.at[w], ry.at[w, xx], p.ydev).start()
+        if k >= 2:
+            down(k - 2)
+        if k == Z:
+            for w in plane:
+                for xx in range(X):
+                    arrived(from_y[w].at[xx], ry.at[w, xx])
+                    add(w, (z * X + xx) * Y + y, 1, from_y[w], xx)
+                copy(own[w].at[(z * X + 1 - x) * Y + y], from_x[w].at[0], sx.at[w], rx.at[w, 0], p.xdev).start()
+    for w in plane:
+        arrived(from_x[w].at[0], rx.at[w, 0])
+        outs[w][...] = own[w][(z * X + x) * Y + y].astype(f32) + from_x[w][0].astype(f32)
+    for w in line:
+        outs[w][...] = own[w][(z * X + x) * Y + y].astype(f32)
+    for w in every:
+        wide = w in plane
+
+        def sent(count, sem):
+            span = own[w].at[pl.ds(0, count)]
+            pltpu.make_async_copy(span, span, sem.at[w]).wait()
+
+        sent(Z * X * Y, score)
+        sent(1 if wide else Z * Y, sx)
+        sent(X if wide else Z, sy)
+        per = X * Y if wide else 1
+        for k in range(Z):
+            @pl.when(z == k)
+            def _():
+                if k > 0:
+                    sent(per * k, sl)
+                if k < Z - 1:
+                    sent(per * (Z - 1 - k), sr)
+    for k, (dev, peer) in enumerate(peers):
+        copy(source.at[peer], place, psend.at[k], precv.at[k], dev).wait()
+    pltpu.make_async_copy(source.at[me], place, plocal).wait()
+
+
+def scatter_all(grads, image_grad, plane_first=PLANE_FIRST, collective=1):
+    nw = len(grads)
+    blocks = [g.shape[1:] for g in grads]
+    slots, items, width = image_grad.shape
+    anyspec = pl.BlockSpec(memory_space=pl.ANY)
+    vm = pl.BlockSpec(memory_space=pltpu.VMEM)
+    dma = pltpu.SemaphoreType.DMA
+
+    def room(line, plane):
+        return [
+            pltpu.VMEM((plane if w in plane_first else line,) + b, g.dtype)
+            for w, (b, g) in enumerate(zip(blocks, grads))
+        ]
+
+    every = Z * X * Y
+    out = pl.pallas_call(
+        functools.partial(scatter_kernel, nw, plane_first),
+        out_shape=[jax.ShapeDtypeStruct(b, f32) for b in blocks]
+        + [jax.ShapeDtypeStruct((slots // (Y * C), items * Y * C, width), image_grad.dtype)],
+        in_specs=[anyspec] * (nw + 1),
+        out_specs=[vm] * nw + [anyspec],
+        scratch_shapes=room(every, every) + room(every, every) + room(Z * Y, 1) + room(Z, X) + room(Z, every) + room(Z, every)
+        + [dma((nw, Z))] * 6 + [dma((nw,))] * 5 + [dma((3,)), dma((3,)), dma],
+        compiler_params=pltpu.CompilerParams(collective_id=collective, has_side_effects=True, vmem_limit_bytes=60 << 20),
+        name="scatter",
+    )(*[g.reshape(every, C, *b) for g, b in zip(grads, blocks)],
+      image_grad.reshape(Y * C, slots // (Y * C), items, width))
+    return list(out[:nw]), out[nw]
 
 
 step_rates = (0.05, 0.15, 0.05, 0.05, 0.3, 0.05, 0.05, 0.5)
 step_decays = (0.01, 0.01, 0.01, 0.01, 0.01, 0.01, 0.01, 0.0)
 BOTH = ("items", "patch")
-STEP = 48
-
-
-def adamw_step(master, gradient, first_moment, second_moment, rate, decay):
-    first_new = 0.9 * first_moment + 0.1 * gradient
-    second_new = 0.999 * second_moment + 0.001 * gradient * gradient
-    step_size = first_new / (1.0 - 0.9**10) / (jnp.sqrt(second_new / (1.0 - 0.999**10)) + 1e-08)
-    return (master - rate * (step_size + decay * master), first_new, second_new)
-
-
-def pad_to(array, shape, value=0.0):
-    return jnp.pad(array, [(0, n - k) for n, k in zip(shape, array.shape)], constant_values=value)
+
+
+def in_blocks(norms, count):
+    width = D // count
+    return jnp.pad(norms.reshape(6, count, width).transpose(1, 0, 2), ((0, 0), (0, 2), (0, 128 - width)))
 
 
 def on_device(direct, text, cotangent, patches, text_lengths, patch_mask, *state):
@@ -642,44 +885,37 @@
     group, local = patch_mask.shape
     chunks = lax.axis_size("patch")
     items = group // chunks
-    index = lax.axis_index("patch") * local + jnp.arange(local, dtype=jnp.int32)
-    valid = (patch_mask > 0) & (index[None, :] < VALID)
-    bias = pad_to(jnp.where(valid, 0.0, -10000.0).astype(f32), (group, 128), OUTSIDE)
-    norms_low = masters[7].astype(bf16).astype(f32)
+    devices = chunks * lax.axis_size("items")
+    by_slot = patches.transpose(1, 0, 2)
     if direct:
-        wide = pad_to(norms_low, (8, 128))
-        weights, (image, bias) = gather_all(
-            list(masters[:7]) + [wide], [bf16] * 7 + [f32], [patches, bias]
-        )
-        norms = weights.pop().reshape(-1, 8, 128)[:, :6, : norms_low.shape[1]]
-        norms = norms.transpose(1, 0, 2).reshape(6, D)
+        weights, blocks, image, masks = gather_all(masters, by_slot, patch_mask, VALID)
     else:
         weights = [lax.all_gather(m.astype(bf16), BOTH, axis=0, tiled=True) for m in masters[:7]]
-        norms = lax.all_gather(norms_low, BOTH, axis=1, tiled=True)
-        image = lax.all_to_all(patches.reshape(chunks, items, local, ENC), "patch", 0, 0)
-        bias = lax.all_to_all(bias.reshape(chunks, items, 128), "patch", 0, 0)
-    bias = bias[:, :, :STEP].transpose(1, 0, 2).reshape(items, chunks * STEP)
-    block_output, text_grad, image_grad, grads, grad_norms = local_step(
-        text, cotangent, image, bias, text_lengths, weights, norms
+        blocks = in_blocks(lax.all_gather(masters[7].astype(bf16), BOTH, axis=1, tiled=True).astype(f32), devices)
+        image = lax.all_to_all(by_slot.reshape(local, chunks, items, ENC), "patch", 1, 0)
+        image = image.reshape(chunks * local, items, ENC)
+        masks = patch_bias(patch_mask, lax.axis_index("patch") * local, VALID)
+        masks = jnp.pad(masks, ((0, 0), (0, 128 - local))).reshape(chunks, items, 128)
+        masks = lax.all_to_all(masks, "patch", 0, 0)
+    block_output, text_grad, image_grad, grads, grad_blocks = local_step(
+        text, cotangent, image, masks, text_lengths, weights, blocks
     )
-    image_grad = lax.all_to_all(image_grad, "patch", 0, 0)
-    patch_grad = image_grad.astype(f32).reshape(patches.shape)
-    joined = lax.psum_scatter(
-        jnp.concatenate([grads[k] for k in (0, 1, 2, 4, 5)], axis=1), BOTH, scatter_dimension=0, tiled=True
+    image_grad = image_grad.reshape(image.shape)
+    if direct:
+        grads = [g.reshape(devices, -1, g.shape[1]) for g in grads]
+        reduced, image_grad = scatter_all([*grads, grad_blocks], image_grad)
+    else:
+        reduced = [lax.psum_scatter(g, BOTH, scatter_dimension=0, tiled=True).astype(f32) for g in grads]
+        reduced.append(lax.psum_scatter(grad_blocks, BOTH, scatter_dimension=0, tiled=True)[0])
+        image_grad = lax.all_to_all(image_grad.reshape(chunks, local, items, ENC), "patch", 0, 1)
+        image_grad = image_grad.reshape(local, group, ENC)
+    state_shapes = [(m.shape, f32) for m in masters]
+    *updated, patch_grad = call(
+        functools.partial(adamw, 8, step_decays, step_rates),
+        (*masters, *firsts, *seconds, *reduced, image_grad),
+        [*state_shapes * 3, (image_grad.shape, f32)], [], "adamw",
     )
-    reduced = {}
-    start = 0
-    for k in (0, 1, 2, 4, 5):
-        reduced[k] = joined[:, start : start + grads[k].shape[1]].astype(f32)
-        start += grads[k].shape[1]
-    for k in (3, 6):
-        reduced[k] = lax.psum_scatter(grads[k], BOTH, scatter_dimension=0, tiled=True).astype(f32)
-    reduced[7] = lax.psum_scatter(grad_norms, BOTH, scatter_dimension=1, tiled=True)
-    updated = [
-        adamw_step(masters[k], reduced[k], firsts[k], seconds[k], step_rates[k], step_decays[k])
-        for k in range(8)
-    ]
-    return (block_output, text_grad, patch_grad, *[u[part] for part in range(3) for u in updated])
+    return (block_output, text_grad, patch_grad.transpose(1, 0, 2), *updated)
 
 
 def solution(mesh):

time: 616 us -> 333 us (0.54)
  waiting for transfers between devices: 263 us -> 0 us
  Pallas kernels: 216 us -> 332 us
  blocking collectives: 78.3 us -> 0 us
  local copies, waits for them, and re-layouts: 23.2 us -> 0 us
  other arithmetic: 13.9 us -> 0 us
  between operations: 14.1 us -> 0.86 us
    reduce_scatter x3 -> x0, waiting for transfers between devices: 262 us -> none  [the longest x1 152 us: on_device(): lax.psum_scatter(jnp.concatenate([grads[k] for k in (0, 1, 2, 4, 5)], axi...]
    pallas_call x1 -> x2, Pallas kernels: 101 us -> 217 us  [the longest x1 118 us: scatter_all(): pl.pallas_call(functools.partial(scatter_kernel, nw, plane_first), out_sh...]
    unnamed x1 -> x0, blocking collectives: 78.3 us -> none
    unnamed x63 -> x0, local copies, waits for them, and re-layouts: 14.3 us -> none
    sub x6 -> x0, other arithmetic: 10.4 us -> none  [adamw_step(): return (master - rate * (step_size + decay * master), first_new, second_new)]
    pallas_call x5 -> x6, Pallas kernels: 115 us -> 115 us  [call(): pl.pallas_call(body, out_shape=[jax.ShapeDtypeStruct(s, k) for s, k in ou...]
  transfers between devices with their start and end apart: 4 -> 0, of which waited for: 3 -> 0; matrix products, arithmetic and copies ran while one was open for 3% -> 0% of each run, Pallas kernels for 3% -> 0%
where the time goes in v2:
time: 333 us
  Pallas kernels  332 us (100%)
    pallas_call x1, Pallas kernels, scatter_all(): pl.pallas_call(functools.partial(scatter_kernel, nw, plane_first), out_sh...  118 us
    pallas_call x6, Pallas kernels, call(): pl.pallas_call(body, out_shape=[jax.ShapeDtypeStruct(s, k) for s, k in ou...  115 us
    pallas_call x1, Pallas kernels, gather_all(): pl.pallas_call(functools.partial(gather_kernel, nw, plane_first, valid),...  99.3 us

profile of v2, /device:TPU:16, one launch (start us, length us, event | category | flops | bytes accessed | tf_op | source)
XLA Modules:
  0.0 333.0 jit_solution(7687131607347347061)
XLA Ops:
  0.7 99.3 %gather.1 = (bf16[32,24,2304]{2,1,0:T(8,128)(2,1)}, bf16[32,24,768]{2,1,0:T(8,128)(2,1)}, bf16[32,24,768]{2,1,0:T(8,128)(2,1)}, bf16[32,32,1536]{2,1,0:T(8,128)(...) custom-call(f32[24,2304]{1,0:T(8,128)} %refs_0_.3, ...), custom_call_target="tpu_custom_call" | custom-call | tf_op jit(solution)/shard_map/gather/pallas_call | solution.py:652
  100.0 11.2 %self_forward.1 = (bf16[320,2304]{1,0:T(8,128)(2,1)}, f32[8,480,40]{2,1,0:T(8,128)}, bf16[320,768]{1,0:T(8,128)(2,1)}, f32[320,768]{1,0:T(8,128)}, f32[320,1]{1,0:T(8,128)}, /*index=5*/f32[8,768]{1,0:T(8,128)}) custom-call(s32[8]{0:T(128)} %lengths.1, bf16[320,768]{1,0:T(8,128)(2,1)} %text.3, bf16[768,2304]{1,0:T(8,128)(2,1)} %bitcast.19, ...), custom_call_target="tpu_custom_call" | custom-call | tf_op jit(solution)/shard_map/self_forward/pallas_call | solution.py:326
  111.2 18.0 %cross_forward.1 = (bf16[8,148,1536]{2,1,0:T(8,128)(2,1)}, bf16[320,768]{1,0:T(8,128)(2,1)}, f32[8,480,148]{2,1,0:T(8,128)}, bf16[320,768]{1,0:T(8,128)(2,1)}, f32[320,768]{1,0:T(8,128)}, /*index=5*/f32[320,1]{1,0:T(8,128)}) custom-call(bf16[1184,1024]{1,0:T(8,128)(2,1)} %bitcast.23, f32[4,8,128]{2,1,0:T(8,128)} %get-tuple-element.99.masks, ...), custom_call_target="tpu_custom_call" | custom-call | tf_op jit(solution)/shard_map/cross_forward/pallas_call | solution.py:326
  129.3 32.7 %feed_forward.1 = (bf16[320,768]{1,0:T(8,128)(2,1)}, bf16[768,3072]{1,0:T(8,128)(2,1)}, bf16[3072,768]{1,0:T(8,128)(2,1)}, f32[320,768]{1,0:T(8,128)}, f32[2,768]{1,0:T(2,128)}) custom-call(f32[320,768]{1,0:T(8,128)} %get-tuple-element.108.normed_two.normed, bf16[320,768]{1,0:T(8,128)(2,1)} %cotangent.1, bf16[768,3072]{1,0:T(8,128)(2,1)} %bitcast.27, ...), custom_call_target="tpu_custom_call" | custom-call | tf_op jit(solution)/shard_map/feed_forward/pallas_call | solution.py:326
  162.0 28.7 %cross_backward.1 = (bf16[1024,1536]{1,0:T(8,128)(2,1)}, bf16[768,768]{1,0:T(8,128)(2,1)}, bf16[768,768]{1,0:T(8,128)(2,1)}, bf16[1184,1024]{1,0:T(8,128)(2,1)}, f32[320,768]{1,0:T(8,128)}, /*index=5*/f32[2,768]{1,0:T(2,128)}) custom-call(bf16[1184,1024]{1,0:T(8,128)(2,1)} %bitcast.24, bf16[8,148,1536]{2,1,0:T(8,128)(2,1)} %get-tuple-element.116.memory, ...), custom_call_target="tpu_custom_call" | custom-call | tf_op jit(solution)/shard_map/cross_backward/pallas_call | solution.py:326
  190.7 17.0 %self_backward.1 = (bf16[768,2304]{1,0:T(8,128)(2,1)}, bf16[768,768]{1,0:T(8,128)(2,1)}, f32[320,768]{1,0:T(8,128)}, f32[32,8,128]{2,1,0:T(8,128)}) custom-call(bf16[320,768]{1,0:T(8,128)(2,1)} %text.3, bf16[320,2304]{1,0:T(8,128)(2,1)} %get-tuple-element.112.mixed, f32[8,480,40]{2,1,0:T(8,128)} %get-tuple-element.113.probs, ...), custom_call_target="tpu_custom_call" | custom-call | tf_op jit(solution)/shard_map/self_backward/pallas_call | solution.py:326
  207.7 117.9 %scatter.1 = (f32[24,2304]{1,0:T(8,128)}, f32[24,768]{1,0:T(8,128)}, f32[24,768]{1,0:T(8,128)}, f32[32,1536]{1,0:T(8,128)}, f32[24,768]{1,0:T(8,128)}, /*index=5...) custom-call(bf16[16,2,24,2304]{3,2,1,0:T(8,128)(2,1)} %bitcast.35, ...), custom_call_target="tpu_custom_call" | custom-call | tf_op jit(solution)/shard_map/scatter/pallas_call | solution.py:858
  325.7 7.2 %adamw.1 = (f32[24,2304]{1,0:T(8,128)}, f32[24,768]{1,0:T(8,128)}, f32[24,768]{1,0:T(8,128)}, f32[32,1536]{1,0:T(8,128)}, f32[24,768]{1,0:T(8,128)}, /*index=5*/...) custom-call(f32[24,2304]{1,0:T(8,128)} %refs_0_.3, ...), custom_call_target="tpu_custom_call" | custom-call | tf_op jit(solution)/shard_map/adamw/pallas_call | solution.py:326

commit v3 on v2

v3 whole, which is shorter than its diff:
```python
import functools

import jax
import jax.numpy as jnp
from jax import lax
from jax.experimental import pallas as pl
from jax.experimental.pallas import tpu as pltpu
from jax.sharding import PartitionSpec as P

D = 768
HEADS = 12
HEAD_DIM = 64
ENC = 1024
TEXT = 40
VALID = 145
PAIR = 2 * HEAD_DIM
PAIRS = HEADS // 2
SCALE = HEAD_DIM ** (-0.5)
OUTSIDE = -1e30
bf16, f32 = jnp.bfloat16, jnp.float32


def dot(a, b):
    return jnp.dot(a, b, preferred_element_type=f32)


def dot_nt(a, b):
    return lax.dot_general(a, b, (((1,), (1,)), ((), ())), preferred_element_type=f32)


def dot_tn(a, b):
    return lax.dot_general(a, b, (((0,), (0,)), ((), ())), preferred_element_type=f32)


def quiet():
    pass


def chunks_of(count, parts, body, pause):
    def run(k, carry):
        body(k)
        return carry

    for part in range(parts):
        lax.fori_loop(count * part // parts, count * (part + 1) // parts, run, 0)
        if part < parts - 1:
            pause()


def tiles(total, step, body):
    def run(k, carry):
        body(pl.ds(pl.multiple_of(k * step, step), step))
        return carry

    lax.fori_loop(0, total // step, run, 0)


def norm_forward(values):
    center = values - jnp.mean(values, axis=-1, keepdims=True)
    inverse = lax.rsqrt(jnp.mean(center * center, axis=-1, keepdims=True) + 1e-12)
    return center * inverse, inverse


def norm_backward(grad_out, normed, inverse, gain):
    grad_gain = jnp.sum(grad_out * normed, axis=0, keepdims=True)
    grad_shift = jnp.sum(grad_out, axis=0, keepdims=True)
    scaled = grad_out * gain
    grad_values = inverse * (
        scaled
        - jnp.mean(scaled, axis=-1, keepdims=True)
        - normed * jnp.mean(scaled * normed, axis=-1, keepdims=True)
    )
    return grad_values, grad_gain, grad_shift


def low_half():
    return lax.broadcasted_iota(jnp.int32, (TEXT, PAIR), 1) < HEAD_DIM


def expand(rows):
    low = low_half()
    return jnp.concatenate(
        [jnp.where(low, rows, 0.0), jnp.where(low, 0.0, rows)], axis=0
    ).astype(bf16)


def fold(rows):
    return jnp.where(low_half(), rows[:TEXT], rows[TEXT:])


def softmax(scores):
    top = jnp.max(scores, axis=-1, keepdims=True)
    powers = jnp.exp(scores - top)
    return powers / jnp.sum(powers, axis=-1, keepdims=True)


def pair_cols(j, start=0):
    return slice(start + PAIR * j, start + PAIR * (j + 1))


def pair_rows(j):
    return slice(2 * TEXT * j, 2 * TEXT * (j + 1))


def attend_forward(query, keys, values, bias, probs, item, context, rows):
    js = range(PAIRS)
    scores = [dot_nt(expand(query(j)), keys(j)) * SCALE + bias for j in js]
    weights = [softmax(s) for s in scores]
    for j in js:
        probs[item, pair_rows(j), :] = weights[j]
    parts = [dot(weights[j].astype(bf16), values(j)) for j in js]
    for j in js:
        context[rows, pair_cols(j)] = fold(parts[j])


def attend_backward(query, keys, values, probs, item, grad_context, put_q, put_k, put_v):
    js = range(PAIRS)
    outer = [expand(grad_context(j)) for j in js]
    grads = [dot_nt(outer[j], values(j)) for j in js]
    inner = []
    for j in js:
        weights = probs[item, pair_rows(j), :]
        delta = jnp.sum(weights * grads[j], axis=-1, keepdims=True)
        inner.append((weights * (grads[j] - delta)).astype(bf16))
    for j in js:
        put_v(j, dot_tn(probs[item, pair_rows(j), :].astype(bf16), outer[j]))
    for j in js:
        put_q(j, fold(dot(inner[j], keys(j))) * SCALE)
    for j in js:
        put_k(j, dot_tn(inner[j], expand(query(j))) * SCALE)


def self_forward(lengths, text, w_qkv, w_out, blocks, mixed, probs, ctx, normed, inverse, norms, mix, context,
                 pause=quiet, parts=1):
    spread(blocks, norms)

    def project(cols):
        got = dot(text[...], w_qkv[:, cols]).astype(bf16)
        mixed[:, cols] = got
        mix[:, cols] = got.astype(f32)

    tiles(3 * D, 768, project)
    pause()
    position = lax.broadcasted_iota(jnp.int32, (1, TEXT), 1)

    def one(item):
        rows = pl.ds(pl.multiple_of(item * TEXT, 8), TEXT)
        bias = jnp.where(position < lengths[item], 0.0, -10000.0).astype(f32)
        attend_forward(
            lambda j: mix[rows, pair_cols(j)],
            lambda j: mix[rows, pair_cols(j, D)].astype(bf16),
            lambda j: mix[rows, pair_cols(j, 2 * D)].astype(bf16),
            bias, probs, item, context, rows,
        )

    chunks_of(probs.shape[0], parts, one, pause)
    pause()
    ctx[...] = context[...].astype(bf16)
    pre = text[...].astype(f32) + dot(ctx[...], w_out[...])
    n, r = norm_forward(pre)
    normed[...] = n
    inverse[...] = r


def self_backward(text, mixed, probs, ctx, normed, inverse, grad_after, w_qkv, w_out, norms, g_second, g_third,
                  g_qkv, g_out, text_grad, g_blocks, mix, grad_ctx, grad_mix, low_mix,
                  pause=quiet, parts=1, wide=1):
    grad_pre, grad_gain, grad_shift = norm_backward(grad_after[...], normed[...], inverse[...], norms[0:1, :])
    rows = jnp.concatenate([grad_gain, grad_shift, g_second[...], g_third[...], jnp.zeros((2, D), f32)], axis=0)
    count = g_blocks.shape[0] // 8
    width = D // count
    g_blocks[...] = jnp.zeros(g_blocks.shape, f32)
    for b in range(count):
        g_blocks[8 * b : 8 * b + 8, :width] = rows[:, width * b : width * (b + 1)]
    low = grad_pre.astype(bf16)
    g_out[...] = dot_tn(ctx[...], low).astype(bf16)
    grad_ctx[...] = dot_nt(low, w_out[...]).astype(bf16).astype(f32)
    text_grad[...] = grad_pre
    mix[...] = mixed[...].astype(f32)
    pause()

    def one(item):
        rows = pl.ds(pl.multiple_of(item * TEXT, 8), TEXT)

        def put(start):
            def store(j, value):
                grad_mix[rows, pair_cols(j, start)] = value
            return store

        attend_backward(
            lambda j: mix[rows, pair_cols(j)],
            lambda j: mix[rows, pair_cols(j, D)].astype(bf16),
            lambda j: mix[rows, pair_cols(j, 2 * D)].astype(bf16),
            probs, item, lambda j: grad_ctx[rows, pair_cols(j)],
            put(0), put(D), put(2 * D),
        )

    chunks_of(probs.shape[0], parts, one, pause)
    pause()
    low_mix[...] = grad_mix[...].astype(bf16)

    def weights(k):
        cols = pl.ds(pl.multiple_of(k * D, D), D)
        g_qkv[:, cols] = dot_tn(text[...], low_mix[:, cols]).astype(bf16)
        text_grad[...] += dot_nt(low_mix[:, cols], w_qkv[:, cols])

    chunks_of(3, wide, weights, pause)


def spread(blocks, norms):
    count = blocks.shape[0] // 8
    width = D // count
    for b in range(count):
        norms[:, width * b : width * (b + 1)] = blocks[8 * b : 8 * b + 8, :width]


def cross_forward(image, masks, w_kv, w_q, w_out, norms, normed_one,
                  memory, query, probs, ctx, normed, inverse, bias, context, wide, flat,
                  pause=quiet, tall=1, parts=1):
    items = masks.shape[1]
    slots = bias.shape[1]
    local = slots // masks.shape[0]
    for c in range(masks.shape[0]):
        bias[:, local * c : local * (c + 1)] = masks[c, :, :local]

    def project(k):
        got = dot(image[...], w_kv[:, pl.ds(pl.multiple_of(4 * PAIR * k, 4 * PAIR), 4 * PAIR)]).astype(bf16).astype(f32)
        for j in range(4):
            flat[4 * k + j] = got[:, pair_cols(j)]

    chunks_of(PAIRS // 2, tall, project, pause)
    pause()
    after = normed_one[...] * norms[0:1, :] + norms[1:2, :]
    low = dot(after.astype(bf16), w_q[...]).astype(bf16)
    query[...] = low
    wide[...] = low.astype(f32)

    def one(item):
        rows = pl.ds(pl.multiple_of(item * TEXT, 8), TEXT)
        every = pl.ds(item, slots, stride=items)
        for j in range(2 * PAIRS):
            memory[item, :, pair_cols(j)] = flat[j, every, :].astype(bf16)
        attend_forward(
            lambda j: wide[rows, pair_cols(j)],
            lambda j: memory[item, :, pair_cols(j)],
            lambda j: memory[item, :, pair_cols(j, D)],
            bias[pl.ds(item, 1), :], probs, item, context, rows,
        )

    chunks_of(items, parts, one, pause)
    pause()
    ctx[...] = context[...].astype(bf16)
    pre = after + dot(ctx[...], w_out[...])
    n, r = norm_forward(pre)
    normed[...] = n
    inverse[...] = r


def cross_backward(memory, query, probs, ctx, normed, inverse, normed_one, grad_after, w_q, w_out, norms,
                   g_q, g_out, grad_self, g_norm, flat, wide, grad_ctx, grad_q, pause=quiet, parts=1):
    items, slots = memory.shape[:2]
    grad_pre, grad_gain, grad_shift = norm_backward(grad_after[...], normed[...], inverse[...], norms[2:3, :])
    g_norm[0:1, :] = grad_gain
    g_norm[1:2, :] = grad_shift
    grad_self[...] = grad_pre
    low = grad_pre.astype(bf16)
    g_out[...] = dot_tn(ctx[...], low).astype(bf16)
    grad_ctx[...] = dot_nt(low, w_out[...]).astype(bf16).astype(f32)
    wide[...] = query[...].astype(f32)
    pause()

    def one(item):
        rows = pl.ds(pl.multiple_of(item * TEXT, 8), TEXT)
        every = pl.ds(item, slots, stride=items)

        def put_q(j, value):
            grad_q[rows, pair_cols(j)] = value

        def put(start):
            def store(j, value):
                flat[start + j, every, :] = value
            return store

        attend_backward(
            lambda j: wide[rows, pair_cols(j)],
            lambda j: memory[item, :, pair_cols(j)],
            lambda j: memory[item, :, pair_cols(j, D)],
            probs, item, lambda j: grad_ctx[rows, pair_cols(j)],
            put_q, put(0), put(PAIRS),
        )

    chunks_of(items, parts, one, pause)
    low_q = grad_q[...].astype(bf16)
    after = (normed_one[...] * norms[0:1, :] + norms[1:2, :]).astype(bf16)
    g_q[...] = dot_tn(after, low_q).astype(bf16)
    grad_self[...] += dot_nt(low_q, w_q[...])


def memory_backward(image, w_kv, flat, g_kv, image_grad, grad_mem, pause=quiet, wide=1):
    for j in range(2 * PAIRS):
        grad_mem[:, pair_cols(j)] = flat[j].astype(bf16)
    step = 4 * PAIR

    def weights(k):
        cols = pl.ds(pl.multiple_of(k * step, step), step)
        g_kv[:, cols] = dot_tn(image[...], grad_mem[:, cols]).astype(bf16)

    chunks_of(2 * D // step, wide, weights, pause)
    pause()

    def back(k):
        cols = pl.ds(pl.multiple_of(k * step, step), step)
        image_grad[:, cols] = dot_nt(grad_mem[...], w_kv[cols, :]).astype(bf16)

    chunks_of(ENC // step, 1, back, pause)


def feed_forward(normed_two, cotangent, w_inner, w_outer, norms,
                 block_output, g_inner, g_outer, grad_after, g_norm, low_in, hidden, slope, total, grad_low, grad_hid):
    after = normed_two[...] * norms[2:3, :] + norms[3:4, :]
    low_in[...] = after.astype(bf16)
    total[...] = after

    def up(cols):
        pre = dot(low_in[...], w_inner[:, cols])
        bell = 0.5 * (1.0 + lax.erf(pre * (0.5 ** 0.5)))
        low = (pre * bell).astype(bf16)
        hidden[:, cols] = low
        slope[:, cols] = bell + pre * jnp.exp(-0.5 * pre * pre) * 0.3989422804014327
        total[...] += dot(low, w_outer[cols, :])

    ff = w_inner.shape[1]
    tiles(ff, 768, up)
    n, r = norm_forward(total[...])
    gain = norms[4:5, :]
    block_output[...] = (n * gain + norms[5:6, :]).astype(bf16)
    grad_pre, grad_gain, grad_shift = norm_backward(cotangent[...].astype(f32), n, r, gain)
    g_norm[0:1, :] = grad_gain
    g_norm[1:2, :] = grad_shift
    grad_after[...] = grad_pre
    grad_low[...] = grad_pre.astype(bf16)

    def down(cols):
        low = (dot_nt(grad_low[...], w_outer[cols, :]) * slope[:, cols]).astype(bf16)
        g_inner[:, cols] = dot_tn(low_in[...], low).astype(bf16)
        g_outer[cols, :] = dot_tn(hidden[:, cols], grad_low[...]).astype(bf16)
        grad_after[...] += dot_nt(low, w_inner[:, cols])

    tiles(ff, 768, down)


VM = pl.BlockSpec(memory_space=pltpu.VMEM)


def call(body, args, outs, scratch, name, smem=0, limit=60 << 20):
    return pl.pallas_call(
        body,
        out_shape=[jax.ShapeDtypeStruct(s, k) for s, k in outs],
        in_specs=[pl.BlockSpec(memory_space=pltpu.SMEM)] * smem + [VM] * (len(args) - smem),
        out_specs=[VM] * len(outs),
        scratch_shapes=[pltpu.VMEM(s, k) for s, k in scratch],
        compiler_params=pltpu.CompilerParams(vmem_limit_bytes=limit),
        name=name,
    )(*args)


def adamw(count, decays, rates, *refs):
    masters, firsts, seconds, grads = (refs[count * i : count * (i + 1)] for i in range(4))
    image_low = refs[4 * count]
    new_m, new_f, new_s = (refs[4 * count + 1 + count * i : 4 * count + 1 + count * (i + 1)] for i in range(3))
    image_grad = refs[7 * count + 1]
    for k in range(count):
        rows, cols = masters[k].shape
        gradient = grads[k][:rows, :cols]
        first = 0.9 * firsts[k][...] + 0.1 * gradient
        second = 0.999 * seconds[k][...] + 0.001 * gradient * gradient
        step = first / (1.0 - 0.9**10) / (jnp.sqrt(second / (1.0 - 0.999**10)) + 1e-08)
        master = masters[k][...]
        new_m[k][...] = master - rates[k] * (step + decays[k] * master)
        new_f[k][...] = first
        new_s[k][...] = second
    image_grad[...] = image_low[...].astype(f32)


def forward_local(text, lengths, image, masks, ws, blocks):
    w_qkv, w_out, w_cq, w_kv, w_co = ws[:5]
    rows = text.shape[0]
    items = rows // TEXT
    slots = image.shape[0] // items
    pairs = HEADS * TEXT
    row = ((rows, D), f32)
    rowl = ((rows, D), bf16)
    one = ((rows, 1), f32)
    *first, norms = call(
        self_forward, (lengths, text, w_qkv, w_out, blocks),
        [((rows, 3 * D), bf16), ((items, pairs, TEXT), f32), rowl, row, one, ((8, D), f32)],
        [((rows, 3 * D), f32), row], "self_forward", smem=1)
    second = call(
        cross_forward, (image, masks, w_kv, w_cq, w_co, norms, first[3]),
        [((items, slots, 2 * D), bf16), rowl, ((items, pairs, slots), f32), rowl, row, one],
        [((items, slots), f32), row, row, ((2 * PAIRS, items * slots, PAIR), f32)], "cross_forward")
    return norms, [*first, *second]


def feed_forward_call(cotangent, ws, norms, n2):
    w_in, w_outer = ws
    rows, ff = n2.shape[0], w_in.shape[1]
    row = ((rows, D), f32)
    rowl = ((rows, D), bf16)
    return call(
        feed_forward, (n2, cotangent, w_in, w_outer, norms),
        [rowl, ((D, ff), bf16), ((ff, D), bf16), row, ((2, D), f32)],
        [rowl, ((rows, ff), bf16), ((rows, ff), f32), row, rowl, rowl], "feed_forward")


def backward_local(text, image, ws, norms, saved, grad_after, gn3, count):
    w_qkv, w_out, w_cq, w_kv, w_co = ws
    mixed, probs, ctx, n1, r1, memory, query, cprobs, cctx, n2, r2 = saved
    rows = text.shape[0]
    row = ((rows, D), f32)
    flat = (2 * PAIRS, image.shape[0], PAIR)
    g_cq, g_co, grad_self, gn2, flat_grad = call(
        cross_backward, (memory, query, cprobs, cctx, n2, r2, n1, grad_after, w_cq, w_co, norms),
        [((D, D), bf16), ((D, D), bf16), row, ((2, D), f32), (flat, f32)], [row, row, row], "cross_backward")
    g_kv, image_grad = call(
        memory_backward, (image, w_kv, flat_grad), [((ENC, 2 * D), bf16), (image.shape, bf16)],
        [((image.shape[0], 2 * D), bf16)], "memory_backward")
    g_qkv, g_out, text_grad, g_blocks = call(
        self_backward, (text, mixed, probs, ctx, n1, r1, grad_self, w_qkv, w_out, norms, gn2, gn3),
        [((D, 3 * D), bf16), ((D, D), bf16), row, ((count * 8, 128), f32)],
        [((rows, 3 * D), f32), row, ((rows, 3 * D), f32), ((rows, 3 * D), bf16)], "self_backward")
    return text_grad, image_grad, (g_qkv, g_out, g_cq, g_kv, g_co), g_blocks


MESH = pl.DeviceIdType.MESH
Z, X, Y, C = 4, 2, 2, 2
PLANE_FIRST = (0, 6)
SETS = ((0, 1, 7, 3, 2, 4), (5, 6))
PLANE_LAST = (6, 3)
PLAN = (
    ("0", "00", "01", "1", "02", "10", "swap", "03", "11", "04", "12", "05", "06", "swapped"),
    ((), ("13",)),
    (),
    (("14",), (), (), ("15",)),
    ("16",),
)
ROUNDS = tuple((k, (6, 5)) for k in range(4)) + tuple((k, (0, 1, 2, 3, 4, 7)) for k in range(4))
BACK_PLAN = (
    (100, 101), (0, 102), (), (1, 103), (), (2,), (), (3,), (), (), (), (),
    (104, 105, 200, 4, 106), (5, 107), (6,), (7,), (8,), (9,),
)
bf16, f32 = jnp.bfloat16, jnp.float32


class Place:
    def __init__(self):
        item, self.me = lax.axis_index("items"), lax.axis_index("patch")
        self.z, self.x, self.y, self.c = item // X, item % X, self.me // C, self.me % C
        z, x, y, c = self.z, self.x, self.y, self.c
        self.left = (item - X, self.me)
        self.right = (item + X, self.me)
        self.xdev = (z * X + (1 - x), self.me)
        self.ypeer, self.cpeer, self.dpeer = (1 - y) * C + c, y * C + (1 - c), (1 - y) * C + (1 - c)
        self.ydev, self.cdev, self.ddev = (item, self.ypeer), (item, self.cpeer), (item, self.dpeer)

    def at(self, zz, xx, yy, cc):
        return ((zz * X + xx) * Y + yy) * C + cc

    def greet(self, barrier):
        for dev in (self.xdev, self.ydev, self.cdev, self.ddev):
            pl.semaphore_signal(barrier, inc=1, device_id=dev, device_id_type=MESH)

        @pl.when(self.z > 0)
        def _():
            pl.semaphore_signal(barrier, inc=1, device_id=self.left, device_id_type=MESH)

        @pl.when(self.z < Z - 1)
        def _():
            pl.semaphore_signal(barrier, inc=1, device_id=self.right, device_id_type=MESH)

    def met(self, barrier):
        pl.semaphore_wait(barrier, 4 + (self.z > 0).astype(jnp.int32) + (self.z < Z - 1).astype(jnp.int32))

    def both(self, d, step):
        if d == 0:
            step(self.z, None)
            return

        @pl.when(self.z >= d)
        def _():
            step(self.z - d, True)

        @pl.when(self.z + d < Z)
        def _():
            step(self.z + d, False)


def patch_bias(mask, first, valid):
    index = first + lax.broadcasted_iota(jnp.int32, mask.shape, 1)
    return jnp.where((mask > 0) & (index < valid), 0.0, -10000.0).astype(f32)


class Gather:
    def __init__(self, place, plane_first, low, outs, recv, to_x, to_y, to_c, to_l, to_r, local):
        self.place, self.plane_first, self.low, self.outs, self.recv, self.local = place, plane_first, low, outs, recv, local
        self.sems = {"x": to_x, "y": to_y, "c": to_c, "l": to_l, "r": to_r}
        self.devs = {"x": place.xdev, "y": place.ydev, "c": place.cdev, "l": place.left, "r": place.right}
        self.mine = place.at(place.z, place.x, place.y, place.c)

    def blocks(self, w, first, count=1):
        rows = self.low[w].shape[0]
        return self.outs[w].at[pl.ds(pl.multiple_of(first * rows, rows), count * rows)]

    def copy(self, w, block, way, own=False):
        return pltpu.make_async_remote_copy(
            src_ref=self.low[w] if own else self.blocks(w, block),
            dst_ref=self.blocks(w, block),
            send_sem=self.sems[way].at[w],
            recv_sem=self.recv.at[w, block],
            device_id=self.devs[way],
            device_id_type=MESH,
        )

    def send(self, w, block, ways, own=False):
        z = self.place.z
        for way in ways:
            if way == "l":
                @pl.when(z > 0)
                def _():
                    self.copy(w, block, "l", own).start()
            elif way == "r":
                @pl.when(z < Z - 1)
                def _():
                    self.copy(w, block, "r", own).start()
            else:
                self.copy(w, block, way, own).start()

    def arrived(self, w, block):
        self.copy(w, block, "x").wait_recv()

    def pass_on(self, w, block, ways):
        self.arrived(w, block)
        self.send(w, block, ways)

    def keep(self, w):
        return pltpu.make_async_copy(self.low[w], self.blocks(w, self.mine), self.local.at[w])

    def start(self, ws):
        for w in ws:
            self.send(w, self.mine, "xylr" if w in self.plane_first else "lryx", True)
        for w in ws:
            self.send(w, self.mine, "c", True)
            self.keep(w).start()

    def stages(self, ws):
        p = self.place
        x, y, c = p.x, p.y, p.c
        line = [w for w in ws if w not in self.plane_first]
        plane = [w for w in ws if w in self.plane_first]

        def plane_x():
            for w in plane:
                self.pass_on(w, p.at(p.z, 1 - x, y, c), "ylrc")

        def plane_y():
            for xx in (x, 1 - x):
                for w in plane:
                    self.pass_on(w, p.at(p.z, xx, 1 - y, c), "lrc")

        def plane_z(zz, from_left):
            for xx, yy in ((x, y), (1 - x, y), (x, 1 - y), (1 - x, 1 - y)):
                for w in plane:
                    self.pass_on(w, p.at(zz, xx, yy, c), "rc" if from_left else "lc")

        def line_z(zz, from_left):
            for w in line:
                self.pass_on(w, p.at(zz, x, y, c), "ryxc" if from_left else "lyxc")

        def line_y(zz, _):
            for w in line:
                self.pass_on(w, p.at(zz, x, 1 - y, c), "xc")

        def line_x(zz, _):
            for yy in (y, 1 - y):
                for w in line:
                    self.pass_on(w, p.at(zz, 1 - x, yy, c), "c")

        def from_core():
            for zz in range(Z):
                for xx in range(X):
                    for yy in range(Y):
                        for w in ws:
                            self.arrived(w, p.at(zz, xx, yy, 1 - c))
            for w in ws:
                self.keep(w).wait()

        def steps(*pairs):
            def run():
                for d, step in pairs:
                    if d is None:
                        step()
                    else:
                        p.both(d, step)
            return run

        first = [(None, plane_x)] if plane else []
        second = [(None, plane_y)] if plane else []

        def deep(d):
            return [(d, plane_z)] if plane else []

        if not line:
            return [steps(*first), steps(*second), steps(*deep(1)), steps(*deep(2)), steps(*deep(3)), quiet, from_core]
        return [
            steps(*first, (1, line_z)),
            steps(*second, (0, line_y)),
            steps(*deep(1), (2, line_z), (1, line_y), (0, line_x)),
            steps(*deep(2), (3, line_z), (2, line_y), (1, line_x)),
            steps(*deep(3), (3, line_y), (2, line_x)),
            steps((3, line_x)),
            from_core,
        ]

    def finish(self):
        z = self.place.z
        for w in range(len(self.low)):
            def sent(count, way):
                span = self.blocks(w, 0, count)
                pltpu.make_async_copy(span, span, self.sems[way].at[w]).wait()

            plane = w in self.plane_first
            wide = X * Y if plane else 1
            sent(1 if plane else Z * Y, "x")
            sent(X if plane else Z, "y")
            sent(Z * X * Y, "c")
            for k in range(Z):
                @pl.when(z == k)
                def _():
                    if k > 0:
                        sent(wide * (Z - k), "l")
                    if k < Z - 1:
                        sent(wide * (k + 1), "r")


def forward_kernel(plane_first, sets, plan, valid, *refs):
    nw = 8
    refs = list(refs)

    def take(count):
        got = refs[:count]
        del refs[:count]
        return got

    (lengths,), shards, (image, mask, text) = take(1), take(nw), take(3)
    whole, (image_out, norms) = take(nw - 1), take(2)
    saved = take(11)
    low, (blocks, masks, bias_here) = take(nw), take(3)
    w_qkv, w_out, w_cq, w_kv, w_co = take(5)
    image_in, mix, context, bias, wide, flat = take(6)
    kept = take(11)
    recv, to_x, to_y, to_c, to_l, to_r, local, psend, precv, plocal, load, save = take(12)
    p = Place()
    me = p.me
    barrier = pltpu.get_barrier_semaphore()
    p.greet(barrier)
    for w in range(nw - 1):
        low[w][...] = shards[w][...].astype(low[w].dtype)
    low[nw - 1][...] = jnp.zeros(low[nw - 1].shape, f32)
    rows, cols = shards[nw - 1].shape
    low[nw - 1][:rows, :cols] = shards[nw - 1][...].astype(bf16).astype(f32)
    slots = mask.shape[1]
    bias_here[...] = jnp.zeros(bias_here.shape, f32)
    bias_here[:, :slots] = patch_bias(mask[...], me * slots, valid)
    here = mask.shape[0] // (Y * C)
    peers = ((p.ydev, p.ypeer), (p.cdev, p.cpeer), (p.ddev, p.dpeer))
    swaps = (image_out, masks)

    def part(s, peer):
        rows = pl.ds(pl.multiple_of(peer * here, here), here)
        return bias_here.at[rows] if s else image.at[:, rows]

    def swap(s, k):
        dev, peer = peers[k]
        return pltpu.make_async_remote_copy(
            src_ref=part(s, peer),
            dst_ref=swaps[s].at[me],
            send_sem=psend.at[s, k],
            recv_sem=precv.at[s, k],
            device_id=dev,
            device_id_type=MESH,
        )

    def stay(s):
        return pltpu.make_async_copy(part(s, me), swaps[s].at[me], plocal.at[s])

    gather = Gather(p, plane_first, low, [*whole, blocks], recv, to_x, to_y, to_c, to_l, to_r, local)
    staged = [gather.stages(ws) for ws in sets]
    p.met(barrier)

    def start_swaps():
        for s in range(2):
            for k in range(3):
                swap(s, k).start()
            stay(s).start()

    def end_swaps():
        for s in range(2):
            for k in range(3):
                swap(s, k).wait()
            stay(s).wait()

    def loads(pairs):
        return [pltpu.make_async_copy(src, dst, load.at[k]) for k, src, dst in pairs]

    early = loads([(0, whole[0], w_qkv), (1, whole[1], w_out)])
    late = loads([(2, whole[2], w_cq), (3, whole[3], w_kv), (4, whole[4], w_co)])

    def flatten(k, carry):
        rows = pl.ds(pl.multiple_of(k * here, here), here)
        pltpu.make_async_copy(image_out.at[k // slots, k % slots], image_in.at[rows], load.at[5]).start()
        return carry
    saves = [pltpu.make_async_copy(src, dst, save.at[k]) for k, (src, dst) in enumerate(zip(kept, saved))]

    def run(tokens):
        for token in tokens:
            if token == "swap":
                start_swaps()
            elif token == "swapped":
                end_swaps()
            elif len(token) == 1:
                gather.start(sets[int(token)])
            else:
                staged[int(token[0])][int(token[1])]()

    def queue(events):
        left = list(events)

        def pause():
            if left:
                run(left.pop(0))

        return pause

    before, during_self, between, during_cross, after = plan
    run(before)
    for copy in early:
        copy.start()
    for copy in early:
        copy.wait()
    mixed, probs, ctx, normed, inverse, memory, query, cross_probs, cross_ctx, normed_two, inverse_two = kept
    self_forward(
        lengths, text, w_qkv, w_out, blocks, mixed, probs, ctx, normed, inverse, norms, mix, context,
        queue(during_self), 2,
    )
    for copy in saves[:5]:
        copy.start()
    run(between)
    for copy in late:
        copy.start()
    lax.fori_loop(0, Y * C * slots, flatten, 0)
    for copy in late:
        copy.wait()
    pltpu.make_async_copy(image_in, image_in, load.at[5]).wait()
    cross_forward(
        image_in, masks, w_kv, w_cq, w_co, norms, normed,
        memory, query, cross_probs, cross_ctx, normed_two, inverse_two, bias, context, wide, flat,
        queue(during_cross), 2, 4,
    )
    for copy in saves[5:]:
        copy.start()
    run(after)
    gather.finish()
    for copy in saves:
        copy.wait()


def forward_all(text, lengths, shards, image, mask, valid, plane_first=PLANE_FIRST, sets=SETS, plan=PLAN, collective=0):
    nw = len(shards)
    n = Z * X * Y * C
    shapes = [s.shape for s in shards[:-1]] + [(8, 128)]
    kinds = [bf16] * (nw - 1) + [f32]
    slots, group, width = image.shape
    items = group // (Y * C)
    rows = text.shape[0]
    every = slots * Y * C
    pairs = HEADS * TEXT
    row, low_row, one = ((rows, D), f32), ((rows, D), bf16), ((rows, 1), f32)
    keep = [
        ((rows, 3 * D), bf16), ((items, pairs, TEXT), f32), low_row, row, one,
        ((items, every, 2 * D), bf16), low_row, ((items, pairs, every), f32), low_row, row, one,
    ]
    anyspec = pl.BlockSpec(memory_space=pl.ANY)
    dma = pltpu.SemaphoreType.DMA
    shape = jax.ShapeDtypeStruct
    out = pl.pallas_call(
        functools.partial(forward_kernel, plane_first, sets, plan, valid),
        out_shape=[shape((n * s[0], s[1]), bf16) for s in shapes[:-1]]
        + [shape((Y * C, slots, items, width), image.dtype), shape((8, D), f32)]
        + [shape(*k) for k in keep],
        in_specs=[pl.BlockSpec(memory_space=pltpu.SMEM)] + [VM] * nw + [anyspec, VM, VM],
        out_specs=[anyspec] * nw + [VM] + [anyspec] * len(keep),
        scratch_shapes=[pltpu.VMEM(s, k) for s, k in zip(shapes, kinds)]
        + [pltpu.VMEM((n * 8, 128), f32), pltpu.VMEM((Y * C, items, 128), f32), pltpu.VMEM((group, 128), f32)]
        + [pltpu.VMEM((n * shapes[w][0], shapes[w][1]), bf16) for w in range(5)]
        + [pltpu.VMEM(s, k) for s, k in (
            ((every * items, width), bf16), ((rows, 3 * D), f32), row, ((items, every), f32), row,
            ((2 * PAIRS, items * every, PAIR), f32), *keep)]
        + [dma((nw, n))] + [dma((nw,))] * 6 + [dma((2, 3)), dma((2, 3)), dma((2,)), dma((6,)), dma((len(keep),))],
        compiler_params=pltpu.CompilerParams(collective_id=collective, has_side_effects=True, vmem_limit_bytes=60 << 20),
        name="forward",
    )(lengths, *shards, image, mask, text)
    return out[: nw - 1], out[nw - 1].reshape(every * items, width), out[nw], out[nw + 1 :]


class Scatter:
    def __init__(self, place, plane_first, grads, own, from_core, from_x, from_y, from_z, sems):
        self.place, self.plane_first, self.grads, self.own = place, plane_first, grads, own
        self.from_core, self.from_x, self.from_y, self.from_z = from_core, from_x, from_y, from_z
        self.load, self.rcore, self.rx, self.ry, self.rl, self.rr, self.score, self.sx, self.sy, self.sl, self.sr = sems

    def target(self, k):
        half = self.place.z // 2
        near = self.place.z * (1 - half) + (Z - 1 - self.place.z) * half
        return half * (Z - 1) + (1 - 2 * half) * (Z - 1, 2 - 2 * near, 1 + near, near)[k]

    def copy(self, src, dst, send_sem, recv_sem, dev):
        return pltpu.make_async_remote_copy(
            src_ref=src, dst_ref=dst, send_sem=send_sem, recv_sem=recv_sem, device_id=dev, device_id_type=MESH
        )

    def arrived(self, dst, sem):
        self.copy(dst, dst, self.score.at[0], sem, self.place.cdev).wait_recv()

    def block(self, w, b):
        rows = self.own[w].shape[1]
        return self.grads[w].at[pl.ds(pl.multiple_of(b * rows, rows), rows)]

    def add(self, w, at, count, ref, start):
        mine = self.own[w]

        def one(i, carry):
            mine[at + i] = (mine[at + i].astype(f32) + ref[start + i].astype(f32)).astype(mine.dtype)
            return carry

        if count == 1:
            one(0, 0)
        else:
            lax.fori_loop(0, count, one, 0)

    def begin(self, k, ws):
        t, c = self.target(k), self.place.c
        for w in ws:
            for s in range(X * Y):
                q = t * X * Y + s
                pltpu.make_async_copy(self.block(w, q * C + c), self.own[w].at[q], self.load.at[w, t]).start()
                self.copy(
                    self.block(w, q * C + 1 - c), self.from_core[w].at[q], self.score.at[w], self.rcore.at[w, t], self.place.cdev
                ).start()

    def core(self, k, ws):
        t, p = self.target(k), self.place
        span = pl.ds(t * X * Y, X * Y)
        for w in ws:
            mine = self.own[w].at[span]
            pltpu.make_async_copy(mine, mine, self.load.at[w, t]).wait()
            self.arrived(self.from_core[w].at[span], self.rcore.at[w, t])
            self.add(w, t * X * Y, X * Y, self.from_core[w], t * X * Y)
            if w not in self.plane_first:
                self.copy(
                    self.own[w].at[pl.ds((t * X + 1 - p.x) * Y, Y)], self.from_x[w].at[pl.ds(t * Y, Y)],
                    self.sx.at[w], self.rx.at[w, t], p.xdev,
                ).start()

    def across(self, k, ws):
        t, p = self.target(k), self.place
        for w in ws:
            self.arrived(self.from_x[w].at[pl.ds(t * Y, Y)], self.rx.at[w, t])
            self.add(w, (t * X + p.x) * Y, Y, self.from_x[w], t * Y)
            self.copy(
                self.own[w].at[(t * X + p.x) * Y + 1 - p.y], self.from_y[w].at[t], self.sy.at[w], self.ry.at[w, t], p.ydev
            ).start()

    def along(self, k, ws, first, count):
        t, z = self.target(k), self.place.z

        def span(w):
            return self.own[w].at[pl.ds(first(t), count)]

        def slot(w, s):
            return self.from_z[w].at[pl.ds(s * count, count)]

        def take(w, s, sem):
            self.arrived(slot(w, s), sem.at[w, t])
            self.add(w, first(t), count, self.from_z[w], s * count)

        if k < Z - 1:
            @pl.when(t > z)
            def _():
                for w in ws:
                    @pl.when(z > 0)
                    def _():
                        take(w, t, self.rl)

                    self.copy(span(w), slot(w, t), self.sr.at[w], self.rl.at[w, t], self.place.right).start()

            @pl.when(t < z)
            def _():
                there = t + (Z - t) * (t == z - 1).astype(jnp.int32)
                for w in ws:
                    @pl.when(z < Z - 1)
                    def _():
                        take(w, t, self.rr)

                    self.copy(span(w), slot(w, there), self.sl.at[w], self.rr.at[w, t], self.place.left).start()
        else:
            for w in ws:
                @pl.when(z > 0)
                def _():
                    take(w, t, self.rl)

                @pl.when(z < Z - 1)
                def _():
                    take(w, Z, self.rr)

    def down(self, k, ws):
        t, p = self.target(k), self.place
        for w in ws:
            self.arrived(self.from_y[w].at[t], self.ry.at[w, t])
            self.add(w, (t * X + p.x) * Y + p.y, 1, self.from_y[w], t)
        self.along(k, ws, lambda t: (t * X + p.x) * Y + p.y, 1)

    def plane(self, k, ws):
        p = self.place
        self.along(k, ws, lambda t: t * X * Y, X * Y)
        if k == Z - 1:
            for w in ws:
                for xx in range(X):
                    self.copy(
                        self.own[w].at[(p.z * X + xx) * Y + 1 - p.y], self.from_y[w].at[xx], self.sy.at[w], self.ry.at[w, xx], p.ydev
                    ).start()

    def plane_across(self, ws):
        p = self.place
        for w in ws:
            for xx in range(X):
                self.arrived(self.from_y[w].at[xx], self.ry.at[w, xx])
                self.add(w, (p.z * X + xx) * Y + p.y, 1, self.from_y[w], xx)
            self.copy(
                self.own[w].at[(p.z * X + 1 - p.x) * Y + p.y], self.from_x[w].at[0], self.sx.at[w], self.rx.at[w, 0], p.xdev
            ).start()

    def steps(self, rounds):
        def some(i, plane):
            k, ws = rounds[i]
            return k, [w for w in ws if (w in self.plane_first) == plane]

        def step(i):
            if i < len(rounds):
                self.core(*rounds[i])
                k, ws = some(i, True)
                self.plane(k, ws)
            if 0 <= i - 1 < len(rounds):
                k, ws = some(i - 1, True)
                if k == Z - 1:
                    self.plane_across(ws)
                self.across(*some(i - 1, False))
            if 0 <= i - 2 < len(rounds):
                self.down(*some(i - 2, False))

        return step

    def finish(self, outs):
        p = self.place
        at = (p.z * X + p.x) * Y + p.y
        for w, out in enumerate(outs):
            plane = w in self.plane_first
            total = self.own[w][at].astype(f32)
            if plane:
                self.arrived(self.from_x[w].at[0], self.rx.at[w, 0])
                total = total + self.from_x[w][0].astype(f32)
            out[...] = total

            def sent(count, sem):
                span = self.own[w].at[pl.ds(0, count)]
                pltpu.make_async_copy(span, span, sem.at[w]).wait()

            sent(Z * X * Y, self.score)
            sent(1 if plane else Z * Y, self.sx)
            sent(X if plane else Z, self.sy)
            per = X * Y if plane else 1
            for k in range(Z):
                @pl.when(p.z == k)
                def _():
                    if k > 0:
                        sent(per * k, self.sl)
                    if k < Z - 1:
                        sent(per * (Z - 1 - k), self.sr)


def backward_kernel(plane_first, rounds, plan, *refs):
    nw = 8
    refs = list(refs)

    def take(count):
        got = refs[:count]
        del refs[:count]
        return got

    norms, g_third = take(2)
    text, image, w_qkv, w_out, w_cq, w_kv, w_co = take(7)
    mixed, probs, ctx, n1, r1, memory, query, cprobs, cctx, n2, r2 = take(11)
    grad_after, g_in, g_outer = take(3)
    outs, (swapped, text_grad) = take(nw), take(2)
    g_qkv, g_out, g_cq, g_kv, g_co, image_grad = take(6)
    own, from_core, from_x, from_y, from_z = (take(nw) for _ in range(5))
    g_blocks, grad_self, g_second = take(3)
    sems = take(11)
    psend, precv, plocal, fetch, store = take(5)
    p = Place()
    me = p.me
    barrier = pltpu.get_barrier_semaphore()
    p.greet(barrier)
    scatter = Scatter(
        p, plane_first, [g_qkv, g_out, g_cq, g_kv, g_co, g_in, g_outer, g_blocks], own, from_core, from_x, from_y, from_z, sems
    )
    step = scatter.steps(rounds)
    here = swapped.shape[1] // (Y * C)
    place = swapped.at[:, pl.ds(pl.multiple_of(me * here, here), here)]
    peers = ((p.ydev, p.ypeer), (p.cdev, p.cpeer), (p.ddev, p.dpeer))

    def swap(k):
        return scatter.copy(image_grad.at[peers[k][1]], place, psend.at[k], precv.at[k], peers[k][0])

    def stay():
        return pltpu.make_async_copy(image_grad.at[me], place, plocal)

    def run(tokens):
        for token in tokens:
            if token == 200:
                for k in range(3):
                    swap(k).start()
                stay().start()
            elif token >= 100:
                scatter.begin(*rounds[token - 100])
            else:
                step(token)

    left = list(plan)

    def pause():
        run(left.pop(0))

    def copies(pairs, sem):
        made = [pltpu.make_async_copy(src, dst, sem.at[k]) for k, (src, dst) in enumerate(pairs)]
        for copy in made:
            copy.start()
        return made

    def done(made):
        for copy in made:
            copy.wait()

    p.met(barrier)

    def cross(flat):
        def attention(*scope):
            made = copies(list(zip((memory, query, cprobs, cctx, n2, r2, n1, grad_after, w_cq, w_co), scope)), fetch)
            pause()
            done(made)
            cross_backward(*scope[:10], norms, *scope[10:12], grad_self, g_second, flat, *scope[12:], scope[7], pause, 2)
            made = copies([(scope[10], g_cq), (scope[11], g_co)], store)
            pause()
            done(made)

        row = pltpu.VMEM(n1.shape, f32)
        pl.run_scoped(
            attention,
            *[pltpu.VMEM(r.shape, r.dtype) for r in (memory, query, cprobs, cctx, n2, r2, n1, grad_after, w_cq, w_co, g_cq, g_co)],
            row, row,
        )

        def weights(image_in, w_in, g_low, back, grad_mem):
            made = copies([(image, image_in), (w_kv, w_in)], fetch)
            pause()
            done(made)
            memory_backward(image_in, w_in, flat, g_low, back, grad_mem, pause, 1)
            made = copies([(g_low, g_kv)], store)
            count = image_grad.shape[1]

            def out(k, carry):
                rows = pl.ds(pl.multiple_of(k * here, here), here)
                pltpu.make_async_copy(back.at[rows], image_grad.at[k // count, k % count], store.at[1]).start()
                return carry

            lax.fori_loop(0, Y * C * count, out, 0)
            pause()
            done(made)
            pltpu.make_async_copy(back, back, store.at[1]).wait()

        pl.run_scoped(
            weights, pltpu.VMEM(image.shape, bf16), pltpu.VMEM(w_kv.shape, bf16), pltpu.VMEM(g_kv.shape, bf16),
            pltpu.VMEM(image.shape, bf16), pltpu.VMEM((image.shape[0], 2 * D), bf16),
        )

    pl.run_scoped(cross, pltpu.VMEM((2 * PAIRS, image.shape[0], PAIR), f32))

    def alone(*scope):
        made = copies(list(zip((text, mixed, probs, ctx, n1, r1, w_qkv, w_out), scope)), fetch)
        pause()
        done(made)
        text_in, mixed_in, probs_in, ctx_in, normed, inverse, w_mix, w_ctx, g_mix, g_ctx, back, *work = scope
        self_backward(
            text_in, mixed_in, probs_in, ctx_in, normed, inverse, grad_self, w_mix, w_ctx, norms, g_second, g_third,
            g_mix, g_ctx, back, g_blocks, *work, pause, 2, 1,
        )
        made = copies([(g_mix, g_qkv), (g_ctx, g_out), (back, text_grad)], store)
        pause()
        done(made)

    rows = text.shape[0]
    pl.run_scoped(
        alone, *[pltpu.VMEM(r.shape, r.dtype) for r in (text, mixed, probs, ctx, n1, r1, w_qkv, w_out, g_qkv, g_out, text_grad)],
        pltpu.VMEM((rows, 3 * D), f32), pltpu.VMEM((rows, D), f32), pltpu.VMEM((rows, 3 * D), f32), pltpu.VMEM((rows, 3 * D), bf16),
    )
    while left:
        pause()
    scatter.finish(outs)
    for k in range(3):
        swap(k).wait()
    stay().wait()


def backward_all(text, image, ws, norms, saved, grad_after, g_third, g_in, g_outer, slots,
                 plane_first=PLANE_LAST, rounds=ROUNDS, plan=BACK_PLAN, collective=1):
    nw = 8
    n = Z * X * Y * C
    every = Z * X * Y
    items = image.shape[0] // slots
    shapes = [w.shape for w in ws] + [g_in.shape, g_outer.shape, (n * 8, 128)]
    blocks = [(s[0] // n, s[1]) for s in shapes]
    kinds = [bf16] * (nw - 1) + [f32]
    anyspec = pl.BlockSpec(memory_space=pl.ANY)
    dma = pltpu.SemaphoreType.DMA
    shape = jax.ShapeDtypeStruct

    def room(line, plane):
        return [
            pltpu.VMEM((plane if w in plane_first else line,) + b, k) for w, (b, k) in enumerate(zip(blocks, kinds))
        ]

    out = pl.pallas_call(
        functools.partial(backward_kernel, plane_first, rounds, plan),
        out_shape=[shape(b, f32) for b in blocks]
        + [shape((slots // (Y * C), items * Y * C, ENC), bf16), shape(text.shape, f32)]
        + [shape(s, bf16) for s in shapes[:5]] + [shape((Y * C, slots // (Y * C), items, ENC), bf16)],
        in_specs=[VM] * 2 + [anyspec] * 21,
        out_specs=[VM] * nw + [anyspec] * 8,
        scratch_shapes=room(every, every) + room(every, every) + room(Z * Y, 1) + room(Z, X) + room(Z + 1, (Z + 1) * X * Y)
        + [pltpu.VMEM((n * 8, 128), f32), pltpu.VMEM(text.shape, f32), pltpu.VMEM((2, D), f32)]
        + [dma((nw, Z))] * 6 + [dma((nw,))] * 5 + [dma((3,)), dma((3,)), dma, dma((12,)), dma((4,))],
        compiler_params=pltpu.CompilerParams(collective_id=collective, has_side_effects=True, vmem_limit_bytes=60 << 20),
        name="backward",
    )(norms, g_third, text, image, *ws, *saved, grad_after, g_in, g_outer)
    return list(out[:nw]), out[nw], out[nw + 1]


step_rates = (0.05, 0.15, 0.05, 0.05, 0.3, 0.05, 0.05, 0.5)
step_decays = (0.01, 0.01, 0.01, 0.01, 0.01, 0.01, 0.01, 0.0)
BOTH = ("items", "patch")


def in_blocks(norms, count):
    width = D // count
    return jnp.pad(norms.reshape(6, count, width).transpose(1, 0, 2), ((0, 0), (0, 2), (0, 128 - width))).reshape(8 * count, 128)


def on_device(direct, text, cotangent, patches, text_lengths, patch_mask, *state):
    masters, firsts, seconds = state[:8], state[8:16], state[16:]
    group, local = patch_mask.shape
    chunks = lax.axis_size("patch")
    items = group // chunks
    devices = chunks * lax.axis_size("items")
    by_slot = patches.transpose(1, 0, 2)
    if direct:
        weights, image, norms, saved = forward_all(text, text_lengths, masters, by_slot, patch_mask, VALID)
    else:
        weights = [lax.all_gather(m.astype(bf16), BOTH, axis=0, tiled=True) for m in masters[:7]]
        blocks = in_blocks(lax.all_gather(masters[7].astype(bf16), BOTH, axis=1, tiled=True).astype(f32), devices)
        image = lax.all_to_all(by_slot.reshape(local, chunks, items, ENC), "patch", 1, 0)
        image = image.reshape(chunks * local * items, ENC)
        masks = patch_bias(patch_mask, lax.axis_index("patch") * local, VALID)
        masks = jnp.pad(masks, ((0, 0), (0, 128 - local))).reshape(chunks, items, 128)
        masks = lax.all_to_all(masks, "patch", 0, 0)
        norms, saved = forward_local(text, text_lengths, image, masks, weights, blocks)
    block_output, g_in, g_outer, grad_after, g_third = feed_forward_call(cotangent, weights[5:7], norms, saved[9])
    if direct:
        reduced, image_grad, text_grad = backward_all(
            text, image, weights[:5], norms, saved, grad_after, g_third, g_in, g_outer, chunks * local
        )
    else:
        text_grad, image_grad, grads, grad_blocks = backward_local(
            text, image, weights[:5], norms, saved, grad_after, g_third, devices
        )
        grads = (*grads, g_in, g_outer)
        reduced = [lax.psum_scatter(g, BOTH, scatter_dimension=0, tiled=True).astype(f32) for g in grads]
        reduced.append(lax.psum_scatter(grad_blocks, BOTH, scatter_dimension=0, tiled=True))
        image_grad = lax.all_to_all(image_grad.reshape(chunks, local, items, ENC), "patch", 0, 1)
        image_grad = image_grad.reshape(local, group, ENC)
    state_shapes = [(m.shape, f32) for m in masters]
    *updated, patch_grad = call(
        functools.partial(adamw, 8, step_decays, step_rates),
        (*masters, *firsts, *seconds, *reduced, image_grad),
        [*state_shapes * 3, (image_grad.shape, f32)], [], "adamw",
    )
    return (block_output, text_grad, patch_grad.transpose(1, 0, 2), *updated)


def solution(mesh):
    rows, cols = P(BOTH, None), P(None, BOTH)
    state = (*[rows] * 7, cols)
    direct = dict(mesh.shape) == {"items": Z * X, "patch": Y * C}
    return jax.shard_map(
        functools.partial(on_device, direct),
        mesh=mesh,
        in_specs=(rows, rows, P("items", "patch", None), P(BOTH), P("items", "patch"), *state * 3),
        out_specs=(rows, rows, P("items", "patch", None), *state * 3),
        check_vma=False,
    )
```

time: 333 us -> 279 us (0.84)
  Pallas kernels: 332 us -> 277 us
    pallas_call x6 -> x2, Pallas kernels: 115 us -> 29.6 us  [call(): pl.pallas_call(body, out_shape=[jax.ShapeDtypeStruct(s, k) for s, k in ou...]
    pallas_call x2, Pallas kernels: 217 us -> 247 us  [the longest x1 144 us: backward_all(): pl.pallas_call(functools.partial(backward_kernel, plane_first, rounds, pl...]
where the time goes in v3:
time: 279 us; the launch traced here: 278 us
  Pallas kernels  277 us (99%)
    pallas_call x1, Pallas kernels, backward_all(): pl.pallas_call(functools.partial(backward_kernel, plane_first, rounds, pl...  144 us
    pallas_call x1, Pallas kernels, forward_all(): pl.pallas_call(functools.partial(forward_kernel, plane_first, sets, plan,...  103 us
    pallas_call x2, Pallas kernels, call(): pl.pallas_call(body, out_shape=[jax.ShapeDtypeStruct(s, k) for s, k in ou...  29.6 us

profile of v3, /device:TPU:16, one launch (start us, length us, event | category | flops | bytes accessed | tf_op | source)
XLA Modules:
  0.0 278.2 jit_solution(307399401288423022)
XLA Ops:
  0.7 103.0 %forward.1 = (bf16[768,2304]{1,0:T(8,128)(2,1)}, bf16[768,768]{1,0:T(8,128)(2,1)}, bf16[768,768]{1,0:T(8,128)(2,1)}, bf16[1024,1536]{1,0:T(8,128)(2,1)}, bf16[76...) custom-call(s32[8]{0:T(128)} %refs_0_.2, ...), custom_call_target="tpu_custom_call" | custom-call | tf_op jit(solution)/shard_map/forward/pallas_call | solution.py:795
  103.7 22.4 %feed_forward.1 = (bf16[320,768]{1,0:T(8,128)(2,1)}, bf16[768,3072]{1,0:T(8,128)(2,1)}, bf16[3072,768]{1,0:T(8,128)(2,1)}, f32[320,768]{1,0:T(8,128)}, f32[2,768]{1,0:T(2,128)}) custom-call(f32[320,768]{1,0:T(8,128)} %get-tuple-element.87.normed_two.refs_18_, bf16[320,768]{1,0:T(8,128)(2,1)} %cotangent.1, bf16[768,3072]{1,0:T(8,128)(2,1)} %get-tuple-element.88.w_inner, ...), custom_call_target="tpu_custom_call" | custom-call | tf_op jit(solution)/shard_map/feed_forward/pallas_call | solution.py:356
  126.0 143.9 %backward.1 = (f32[24,2304]{1,0:T(8,128)}, f32[24,768]{1,0:T(8,128)}, f32[24,768]{1,0:T(8,128)}, f32[32,1536]{1,0:T(8,128)}, f32[24,768]{1,0:T(8,128)}, /*index=...) custom-call(f32[8,768]{1,0:T(8,128)} %get-tuple-element.90.norms.ref, ...), custom_call_target="tpu_custom_call" | custom-call | tf_op jit(solution)/shard_map/backward/pallas_call | solution.py:1151
  270.0 0.0 copy-start
  270.0 7.2 %adamw.1 = (f32[24,2304]{1,0:T(8,128)}, f32[24,768]{1,0:T(8,128)}, f32[24,768]{1,0:T(8,128)}, f32[32,1536]{1,0:T(8,128)}, f32[24,768]{1,0:T(8,128)}, /*index=5*/...) custom-call(f32[24,2304]{1,0:T(8,128)} %refs_0_.3, ...), custom_call_target="tpu_custom_call" | custom-call | tf_op jit(solution)/shard_map/adamw/pallas_call | solution.py:356
  277.2 0.0 copy-done
  277.2 0.9 copy.57
Async XLA Ops:
  270.0 7.2 %copy-start = (f32[320,768]{1,0:T(8,128)S(1)}, f32[320,768]{1,0:T(8,128)}, u32[]{:S(2)}) copy-start(f32[320,768]{1,0:T(8,128)} %get-tuple-element.175) | copy-start | bytes 2949124

commit v4 on v3

--- a/solution.py
+++ b/solution.py
@@ -434,20 +434,31 @@
 
 MESH = pl.DeviceIdType.MESH
 Z, X, Y, C = 4, 2, 2, 2
-PLANE_FIRST = (0, 6)
+PLANE_FIRST, TURNED = (0,), (6,)
 SETS = ((0, 1, 7, 3, 2, 4), (5, 6))
-PLANE_LAST = (6, 3)
 PLAN = (
-    ("0", "00", "01", "1", "02", "10", "swap", "03", "11", "04", "12", "05", "06", "swapped"),
-    ((), ("13",)),
+    ("0", "00", "01", "1", "02", "swap", "03", "10", "04", "11", "05", "06", "swapped"),
+    (("12",),),
     (),
-    (("14",), (), (), ("15",)),
+    (("13",), (), ("14",), ("15",)),
     ("16",),
 )
-ROUNDS = tuple((k, (6, 5)) for k in range(4)) + tuple((k, (0, 1, 2, 3, 4, 7)) for k in range(4))
+PLANE_LAST, TURNED_BACK = (3,), (6,)
+ROUNDS = tuple((k, ws) for ws in ((6, 5), (3, 2, 4), (0, 1, 7)) for k in range(4))
 BACK_PLAN = (
-    (100, 101), (0, 102), (), (1, 103), (), (2,), (), (3,), (), (), (), (),
-    (104, 105, 200, 4, 106), (5, 107), (6,), (7,), (8,), (9,),
+    ("b0", "b1", "c0", "b2"),
+    ("c1", "b3"),
+    ("c2", "a0"),
+    ("c3", "a1"),
+    ("a2",),
+    ("d0", "a3"),
+    ("d1",),
+    ("b4", "b5", "s", "d2"),
+    ("c4", "e4", "b6"),
+    ("c5", "e5", "a4", "b7"),
+    ("c6", "e6", "a5", "d3"),
+    ("c7", "a6", "m4"),
+    ("b8", "b9", "c8", "b10", "c9", "b11", "a7", "a8", "c10", "d4", "m5", "d5", "a9", "c11", "m6", "d6", "d8", "a10", "p7", "d7", "d9", "a11", "q7", "d10", "d11"),
 )
 bf16, f32 = jnp.bfloat16, jnp.float32
 
@@ -501,8 +512,9 @@
 
 
 class Gather:
-    def __init__(self, place, plane_first, low, outs, recv, to_x, to_y, to_c, to_l, to_r, local):
-        self.place, self.plane_first, self.low, self.outs, self.recv, self.local = place, plane_first, low, outs, recv, local
+    def __init__(self, place, plane_first, turned, low, outs, recv, to_x, to_y, to_c, to_l, to_r, local):
+        self.place, self.plane_first, self.turned = place, plane_first, turned
+        self.low, self.outs, self.recv, self.local = low, outs, recv, local
         self.sems = {"x": to_x, "y": to_y, "c": to_c, "l": to_l, "r": to_r}
         self.devs = {"x": place.xdev, "y": place.ydev, "c": place.cdev, "l": place.left, "r": place.right}
         self.mine = place.at(place.z, place.x, place.y, place.c)
@@ -578,12 +590,18 @@
 
         def line_y(zz, _):
             for w in line:
-                self.pass_on(w, p.at(zz, x, 1 - y, c), "xc")
+                if w in self.turned:
+                    self.pass_on(w, p.at(zz, 1 - x, y, c), "yc")
+                else:
+                    self.pass_on(w, p.at(zz, x, 1 - y, c), "xc")
 
         def line_x(zz, _):
-            for yy in (y, 1 - y):
+            for near in (True, False):
                 for w in line:
-                    self.pass_on(w, p.at(zz, 1 - x, yy, c), "c")
+                    if w in self.turned:
+                        self.pass_on(w, p.at(zz, x if near else 1 - x, 1 - y, c), "c")
+                    else:
+                        self.pass_on(w, p.at(zz, 1 - x, y if near else 1 - y, c), "c")
 
         def from_core():
             for zz in range(Z):
@@ -630,8 +648,9 @@
 
             plane = w in self.plane_first
             wide = X * Y if plane else 1
-            sent(1 if plane else Z * Y, "x")
-            sent(X if plane else Z, "y")
+            turned = w in self.turned
+            sent(1 if plane else Z if turned else Z * Y, "x")
+            sent(X if plane else Z * X if turned else Z, "y")
             sent(Z * X * Y, "c")
             for k in range(Z):
                 @pl.when(z == k)
@@ -642,7 +661,7 @@
                         sent(wide * (k + 1), "r")
 
 
-def forward_kernel(plane_first, sets, plan, valid, *refs):
+def forward_kernel(plane_first, turned, sets, plan, valid, *refs):
     nw = 8
     refs = list(refs)
 
@@ -693,7 +712,7 @@
     def stay(s):
         return pltpu.make_async_copy(part(s, me), swaps[s].at[me], plocal.at[s])
 
-    gather = Gather(p, plane_first, low, [*whole, blocks], recv, to_x, to_y, to_c, to_l, to_r, local)
+    gather = Gather(p, plane_first, turned, low, [*whole, blocks], recv, to_x, to_y, to_c, to_l, to_r, local)
     staged = [gather.stages(ws) for ws in sets]
     p.met(barrier)
 
@@ -774,7 +793,7 @@
         copy.wait()
 
 
-def forward_all(text, lengths, shards, image, mask, valid, plane_first=PLANE_FIRST, sets=SETS, plan=PLAN, collective=0):
+def forward_all(text, lengths, shards, image, mask, valid, plane_first=PLANE_FIRST, turned=TURNED, sets=SETS, plan=PLAN, collective=0):
     nw = len(shards)
     n = Z * X * Y * C
     shapes = [s.shape for s in shards[:-1]] + [(8, 128)]
@@ -793,7 +812,7 @@
     dma = pltpu.SemaphoreType.DMA
     shape = jax.ShapeDtypeStruct
     out = pl.pallas_call(
-        functools.partial(forward_kernel, plane_first, sets, plan, valid),
+        functools.partial(forward_kernel, plane_first, turned, sets, plan, valid),
         out_shape=[shape((n * s[0], s[1]), bf16) for s in shapes[:-1]]
         + [shape((Y * C, slots, items, width), image.dtype), shape((8, D), f32)]
         + [shape(*k) for k in keep],
@@ -813,8 +832,8 @@
 
 
 class Scatter:
-    def __init__(self, place, plane_first, grads, own, from_core, from_x, from_y, from_z, sems):
-        self.place, self.plane_first, self.grads, self.own = place, plane_first, grads, own
+    def __init__(self, place, plane_first, turned, grads, own, from_core, from_x, from_y, from_z, sems):
+        self.place, self.plane_first, self.turned, self.grads, self.own = place, plane_first, turned, grads, own
         self.from_core, self.from_x, self.from_y, self.from_z = from_core, from_x, from_y, from_z
         self.load, self.rcore, self.rx, self.ry, self.rl, self.rr, self.score, self.sx, self.sy, self.sl, self.sr = sems
 
@@ -865,7 +884,13 @@
             pltpu.make_async_copy(mine, mine, self.load.at[w, t]).wait()
             self.arrived(self.from_core[w].at[span], self.rcore.at[w, t])
             self.add(w, t * X * Y, X * Y, self.from_core[w], t * X * Y)
-            if w not in self.plane_first:
+            if w in self.turned:
+                for xx in range(X):
+                    self.copy(
+                        self.own[w].at[(t * X + xx) * Y + 1 - p.y], self.from_y[w].at[t * X + xx],
+                        self.sy.at[w], self.ry.at[w, t], p.ydev,
+                    ).start()
+            elif w not in self.plane_first:
                 self.copy(
                     self.own[w].at[pl.ds((t * X + 1 - p.x) * Y, Y)], self.from_x[w].at[pl.ds(t * Y, Y)],
                     self.sx.at[w], self.rx.at[w, t], p.xdev,
@@ -874,6 +899,14 @@
     def across(self, k, ws):
         t, p = self.target(k), self.place
         for w in ws:
+            if w in self.turned:
+                self.arrived(self.from_y[w].at[pl.ds(t * X, X)], self.ry.at[w, t])
+                for xx in range(X):
+                    self.add(w, (t * X + xx) * Y + p.y, 1, self.from_y[w], t * X + xx)
+                self.copy(
+                    self.own[w].at[(t * X + 1 - p.x) * Y + p.y], self.from_x[w].at[t], self.sx.at[w], self.rx.at[w, t], p.xdev
+                ).start()
+                continue
             self.arrived(self.from_x[w].at[pl.ds(t * Y, Y)], self.rx.at[w, t])
             self.add(w, (t * X + p.x) * Y, Y, self.from_x[w], t * Y)
             self.copy(
@@ -925,8 +958,9 @@
     def down(self, k, ws):
         t, p = self.target(k), self.place
         for w in ws:
-            self.arrived(self.from_y[w].at[t], self.ry.at[w, t])
-            self.add(w, (t * X + p.x) * Y + p.y, 1, self.from_y[w], t)
+            ref, sem = (self.from_x, self.rx) if w in self.turned else (self.from_y, self.ry)
+            self.arrived(ref[w].at[t], sem.at[w, t])
+            self.add(w, (t * X + p.x) * Y + p.y, 1, ref[w], t)
         self.along(k, ws, lambda t: (t * X + p.x) * Y + p.y, 1)
 
     def plane(self, k, ws):
@@ -949,25 +983,30 @@
                 self.own[w].at[(p.z * X + 1 - p.x) * Y + p.y], self.from_x[w].at[0], self.sx.at[w], self.rx.at[w, 0], p.xdev
             ).start()
 
-    def steps(self, rounds):
-        def some(i, plane):
-            k, ws = rounds[i]
-            return k, [w for w in ws if (w in self.plane_first) == plane]
-
-        def step(i):
-            if i < len(rounds):
-                self.core(*rounds[i])
-                k, ws = some(i, True)
-                self.plane(k, ws)
-            if 0 <= i - 1 < len(rounds):
-                k, ws = some(i - 1, True)
-                if k == Z - 1:
-                    self.plane_across(ws)
-                self.across(*some(i - 1, False))
-            if 0 <= i - 2 < len(rounds):
-                self.down(*some(i - 2, False))
-
-        return step
+    def act(self, name, k, ws):
+        line = [w for w in ws if w not in self.plane_first]
+        plane = [w for w in ws if w in self.plane_first]
+        z = self.place.z
+        if name == "b":
+            self.begin(k, ws)
+        elif name == "c":
+            self.core(k, ws)
+        elif name == "a":
+            self.across(k, line)
+        elif name == "d":
+            self.down(k, line)
+        elif name == "e":
+            @pl.when((z == 0) | (z == Z - 1))
+            def _():
+                self.plane(k, plane)
+        elif name == "m":
+            @pl.when((z > 0) & (z < Z - 1))
+            def _():
+                self.plane(k, plane)
+        elif name == "p":
+            self.plane(k, plane)
+        elif name == "q":
+            self.plane_across(plane)
 
     def finish(self, outs):
         p = self.place
@@ -985,8 +1024,9 @@
                 pltpu.make_async_copy(span, span, sem.at[w]).wait()
 
             sent(Z * X * Y, self.score)
-            sent(1 if plane else Z * Y, self.sx)
-            sent(X if plane else Z, self.sy)
+            turned = w in self.turned
+            sent(1 if plane else Z if turned else Z * Y, self.sx)
+            sent(X if plane else Z * X if turned else Z, self.sy)
             per = X * Y if plane else 1
             for k in range(Z):
                 @pl.when(p.z == k)
@@ -997,7 +1037,7 @@
                         sent(per * (Z - 1 - k), self.sr)
 
 
-def backward_kernel(plane_first, rounds, plan, *refs):
+def backward_kernel(plane_first, turned, rounds, plan, *refs):
     nw = 8
     refs = list(refs)
 
@@ -1021,9 +1061,8 @@
     barrier = pltpu.get_barrier_semaphore()
     p.greet(barrier)
     scatter = Scatter(
-        p, plane_first, [g_qkv, g_out, g_cq, g_kv, g_co, g_in, g_outer, g_blocks], own, from_core, from_x, from_y, from_z, sems
+        p, plane_first, turned, [g_qkv, g_out, g_cq, g_kv, g_co, g_in, g_outer, g_blocks], own, from_core, from_x, from_y, from_z, sems
     )
-    step = scatter.steps(rounds)
     here = swapped.shape[1] // (Y * C)
     place = swapped.at[:, pl.ds(pl.multiple_of(me * here, here), here)]
     peers = ((p.ydev, p.ypeer), (p.cdev, p.cpeer), (p.ddev, p.dpeer))
@@ -1036,14 +1075,12 @@
 
     def run(tokens):
         for token in tokens:
-            if token == 200:
+            if token == "s":
                 for k in range(3):
                     swap(k).start()
                 stay().start()
-            elif token >= 100:
-                scatter.begin(*rounds[token - 100])
             else:
-                step(token)
+                scatter.act(token[0], *rounds[int(token[1:])])
 
     left = list(plan)
 
@@ -1131,7 +1168,7 @@
 
 
 def backward_all(text, image, ws, norms, saved, grad_after, g_third, g_in, g_outer, slots,
-                 plane_first=PLANE_LAST, rounds=ROUNDS, plan=BACK_PLAN, collective=1):
+                 plane_first=PLANE_LAST, turned=TURNED_BACK, rounds=ROUNDS, plan=BACK_PLAN, collective=1):
     nw = 8
     n = Z * X * Y * C
     every = Z * X * Y
@@ -1143,19 +1180,20 @@
     dma = pltpu.SemaphoreType.DMA
     shape = jax.ShapeDtypeStruct
 
-    def room(line, plane):
+    def room(line, plane, other=None):
         return [
-            pltpu.VMEM((plane if w in plane_first else line,) + b, k) for w, (b, k) in enumerate(zip(blocks, kinds))
+            pltpu.VMEM((plane if w in plane_first else other or line if w in turned else line,) + b, k)
+            for w, (b, k) in enumerate(zip(blocks, kinds))
         ]
 
     out = pl.pallas_call(
-        functools.partial(backward_kernel, plane_first, rounds, plan),
+        functools.partial(backward_kernel, plane_first, turned, rounds, plan),
         out_shape=[shape(b, f32) for b in blocks]
         + [shape((slots // (Y * C), items * Y * C, ENC), bf16), shape(text.shape, f32)]
         + [shape(s, bf16) for s in shapes[:5]] + [shape((Y * C, slots // (Y * C), items, ENC), bf16)],
         in_specs=[VM] * 2 + [anyspec] * 21,
         out_specs=[VM] * nw + [anyspec] * 8,
-        scratch_shapes=room(every, every) + room(every, every) + room(Z * Y, 1) + room(Z, X) + room(Z + 1, (Z + 1) * X * Y)
+        scratch_shapes=room(every, every) + room(every, every) + room(Z * Y, 1, Z) + room(Z, X, Z * X) + room(Z + 1, (Z + 1) * X * Y)
         + [pltpu.VMEM((n * 8, 128), f32), pltpu.VMEM(text.shape, f32), pltpu.VMEM((2, D), f32)]
         + [dma((nw, Z))] * 6 + [dma((nw,))] * 5 + [dma((3,)), dma((3,)), dma, dma((12,)), dma((4,))],
         compiler_params=pltpu.CompilerParams(collective_id=collective, has_side_effects=True, vmem_limit_bytes=60 << 20),

time: 279 us -> 253 us (0.907)
  Pallas kernels: 277 us -> 251 us
    pallas_call x2, Pallas kernels: 247 us -> 221 us  [the longest x1 115 us: backward_all(): pl.pallas_call(functools.partial(backward_kernel, plane_first, turned, ro...]
where the time goes in v4:
time: 253 us
  Pallas kernels  251 us (99%)
    pallas_call x1, Pallas kernels, backward_all(): pl.pallas_call(functools.partial(backward_kernel, plane_first, turned, ro...  115 us
    pallas_call x1, Pallas kernels, forward_all(): pl.pallas_call(functools.partial(forward_kernel, plane_first, turned, set...  106 us
    pallas_call x2, Pallas kernels, call(): pl.pallas_call(body, out_shape=[jax.ShapeDtypeStruct(s, k) for s, k in ou...  29.6 us

profile of v4, /device:TPU:16, one launch (start us, length us, event | category | flops | bytes accessed | tf_op | source)
XLA Modules:
  0.0 252.6 jit_solution(15651197564253021060)
XLA Ops:
  0.7 105.8 %forward.1 = (bf16[768,2304]{1,0:T(8,128)(2,1)}, bf16[768,768]{1,0:T(8,128)(2,1)}, bf16[768,768]{1,0:T(8,128)(2,1)}, bf16[1024,1536]{1,0:T(8,128)(2,1)}, bf16[76...) custom-call(s32[8]{0:T(128)} %refs_0_.2, ...), custom_call_target="tpu_custom_call" | custom-call | tf_op jit(solution)/shard_map/forward/pallas_call | solution.py:814
  106.5 22.4 %feed_forward.1 = (bf16[320,768]{1,0:T(8,128)(2,1)}, bf16[768,3072]{1,0:T(8,128)(2,1)}, bf16[3072,768]{1,0:T(8,128)(2,1)}, f32[320,768]{1,0:T(8,128)}, f32[2,768]{1,0:T(2,128)}) custom-call(f32[320,768]{1,0:T(8,128)} %get-tuple-element.87.normed_two.refs_18_, bf16[320,768]{1,0:T(8,128)(2,1)} %cotangent.1, bf16[768,3072]{1,0:T(8,128)(2,1)} %get-tuple-element.88.w_inner, ...), custom_call_target="tpu_custom_call" | custom-call | tf_op jit(solution)/shard_map/feed_forward/pallas_call | solution.py:356
  128.9 115.5 %backward.1 = (f32[24,2304]{1,0:T(8,128)}, f32[24,768]{1,0:T(8,128)}, f32[24,768]{1,0:T(8,128)}, f32[32,1536]{1,0:T(8,128)}, f32[24,768]{1,0:T(8,128)}, /*index=...) custom-call(f32[8,768]{1,0:T(8,128)} %get-tuple-element.90.norms.ref, ...), custom_call_target="tpu_custom_call" | custom-call | tf_op jit(solution)/shard_map/backward/pallas_call | solution.py:1189
  244.4 0.0 copy-start
  244.4 7.2 %adamw.1 = (f32[24,2304]{1,0:T(8,128)}, f32[24,768]{1,0:T(8,128)}, f32[24,768]{1,0:T(8,128)}, f32[32,1536]{1,0:T(8,128)}, f32[24,768]{1,0:T(8,128)}, /*index=5*/...) custom-call(f32[24,2304]{1,0:T(8,128)} %refs_0_.3, ...), custom_call_target="tpu_custom_call" | custom-call | tf_op jit(solution)/shard_map/adamw/pallas_call | solution.py:356
  251.6 0.0 copy-done
  251.6 0.9 copy.57
Async XLA Ops:
  244.4 7.2 %copy-start = (f32[320,768]{1,0:T(8,128)S(1)}, f32[320,768]{1,0:T(8,128)}, u32[]{:S(2)}) copy-start(f32[320,768]{1,0:T(8,128)} %get-tuple-element.175) | copy-start | bytes 2949124

commit v5 on v4

--- a/solution.py
+++ b/solution.py
@@ -316,21 +316,47 @@
 
 
 def feed_forward(normed_two, cotangent, w_inner, w_outer, norms,
-                 block_output, g_inner, g_outer, grad_after, g_norm, low_in, hidden, slope, total, grad_low, grad_hid):
+                 block_output, g_inner, g_outer, grad_after, g_norm, low_in, hidden, slope, total, grad_low,
+                 inner_in, outer_in, inner_out, outer_out, load, store):
+    step = D
+    count = w_inner.shape[1] // step
+
+    def part(k):
+        return pl.ds(pl.multiple_of(k * step, step), step)
+
+    def loads(k):
+        cols = part(k)
+        return (
+            pltpu.make_async_copy(w_inner.at[:, cols], inner_in.at[:, cols], load.at[0, k]),
+            pltpu.make_async_copy(w_outer.at[cols], outer_in.at[cols], load.at[1, k]),
+        )
+
+    def stores(k):
+        cols = part(k)
+        return (
+            pltpu.make_async_copy(inner_out.at[:, cols], g_inner.at[:, cols], store.at[0, k]),
+            pltpu.make_async_copy(outer_out.at[cols], g_outer.at[cols], store.at[1, k]),
+        )
+
+    for k in range(count):
+        for copy in loads(k):
+            copy.start()
     after = normed_two[...] * norms[2:3, :] + norms[3:4, :]
     low_in[...] = after.astype(bf16)
     total[...] = after
 
-    def up(cols):
-        pre = dot(low_in[...], w_inner[:, cols])
+    def up(k):
+        cols = part(k)
+        for copy in loads(k):
+            copy.wait()
+        pre = dot(low_in[...], inner_in[:, cols])
         bell = 0.5 * (1.0 + lax.erf(pre * (0.5 ** 0.5)))
         low = (pre * bell).astype(bf16)
         hidden[:, cols] = low
         slope[:, cols] = bell + pre * jnp.exp(-0.5 * pre * pre) * 0.3989422804014327
-        total[...] += dot(low, w_outer[cols, :])
-
-    ff = w_inner.shape[1]
-    tiles(ff, 768, up)
+        total[...] += dot(low, outer_in[cols, :])
+
+    chunks_of(count, 1, up, quiet)
     n, r = norm_forward(total[...])
     gain = norms[4:5, :]
     block_output[...] = (n * gain + norms[5:6, :]).astype(bf16)
@@ -340,25 +366,34 @@
     grad_after[...] = grad_pre
     grad_low[...] = grad_pre.astype(bf16)
 
-    def down(cols):
-        low = (dot_nt(grad_low[...], w_outer[cols, :]) * slope[:, cols]).astype(bf16)
-        g_inner[:, cols] = dot_tn(low_in[...], low).astype(bf16)
-        g_outer[cols, :] = dot_tn(hidden[:, cols], grad_low[...]).astype(bf16)
-        grad_after[...] += dot_nt(low, w_inner[:, cols])
-
-    tiles(ff, 768, down)
+    def down(k):
+        cols = part(k)
+        low = (dot_nt(grad_low[...], outer_in[cols, :]) * slope[:, cols]).astype(bf16)
+        inner_out[:, cols] = dot_tn(low_in[...], low).astype(bf16)
+        outer_out[cols, :] = dot_tn(hidden[:, cols], grad_low[...]).astype(bf16)
+        for copy in stores(k):
+            copy.start()
+        grad_after[...] += dot_nt(low, inner_in[:, cols])
+
+    chunks_of(count, 1, down, quiet)
+    for k in range(count):
+        for copy in stores(k):
+            copy.wait()
 
 
 VM = pl.BlockSpec(memory_space=pltpu.VMEM)
 
 
-def call(body, args, outs, scratch, name, smem=0, limit=60 << 20):
+def call(body, args, outs, scratch, name, smem=0, limit=60 << 20, left=(), sems=()):
+    def where(k):
+        return pl.BlockSpec(memory_space=pl.ANY) if k in left else VM
+
     return pl.pallas_call(
         body,
         out_shape=[jax.ShapeDtypeStruct(s, k) for s, k in outs],
-        in_specs=[pl.BlockSpec(memory_space=pltpu.SMEM)] * smem + [VM] * (len(args) - smem),
-        out_specs=[VM] * len(outs),
-        scratch_shapes=[pltpu.VMEM(s, k) for s, k in scratch],
+        in_specs=[pl.BlockSpec(memory_space=pltpu.SMEM)] * smem + [where(k) for k in range(smem, len(args))],
+        out_specs=[where(len(args) + k) for k in range(len(outs))],
+        scratch_shapes=[pltpu.VMEM(s, k) for s, k in scratch] + [pltpu.SemaphoreType.DMA(s) for s in sems],
         compiler_params=pltpu.CompilerParams(vmem_limit_bytes=limit),
         name=name,
     )(*args)
@@ -410,7 +445,8 @@
     return call(
         feed_forward, (n2, cotangent, w_in, w_outer, norms),
         [rowl, ((D, ff), bf16), ((ff, D), bf16), row, ((2, D), f32)],
-        [rowl, ((rows, ff), bf16), ((rows, ff), f32), row, rowl, rowl], "feed_forward")
+        [rowl, ((rows, ff), bf16), ((rows, ff), f32), row, rowl, *[(w.shape, bf16) for w in (w_in, w_outer)] * 2],
+        "feed_forward", left=(2, 3, 6, 7), sems=[(2, ff // D)] * 2)
 
 
 def backward_local(text, image, ws, norms, saved, grad_after, gn3, count):

time: 253 us -> 251 us (level)
  no operation moved by 1% of the time
where the time goes in v5:
time: 251 us; the launch traced here: 250 us
  Pallas kernels  249 us (99%)
    pallas_call x1, Pallas kernels, backward_all(): pl.pallas_call(functools.partial(backward_kernel, plane_first, turned, ro...  116 us
    pallas_call x1, Pallas kernels, forward_all(): pl.pallas_call(functools.partial(forward_kernel, plane_first, turned, set...  106 us
    pallas_call x2, Pallas kernels, call(): pl.pallas_call(body, out_shape=[jax.ShapeDtypeStruct(s, k) for s, k in ou...  27.3 us

profile of v5, /device:TPU:16, one launch (start us, length us, event | category | flops | bytes accessed | tf_op | source)
XLA Modules:
  0.0 250.3 jit_solution(4882874406943713072)
XLA Ops:
  0.7 105.8 %forward.1 = (bf16[768,2304]{1,0:T(8,128)(2,1)}, bf16[768,768]{1,0:T(8,128)(2,1)}, bf16[768,768]{1,0:T(8,128)(2,1)}, bf16[1024,1536]{1,0:T(8,128)(2,1)}, bf16[76...) custom-call(s32[8]{0:T(128)} %refs_0_.2, ...), custom_call_target="tpu_custom_call" | custom-call | tf_op jit(solution)/shard_map/forward/pallas_call | solution.py:850
  106.5 20.1 %feed_forward.1 = (bf16[320,768]{1,0:T(8,128)(2,1)}, bf16[768,3072]{1,0:T(8,128)(2,1)}, bf16[3072,768]{1,0:T(8,128)(2,1)}, f32[320,768]{1,0:T(8,128)}, f32[2,768]{1,0:T(2,128)}) custom-call(f32[320,768]{1,0:T(8,128)} %get-tuple-element.87.normed_two.refs_18_, bf16[320,768]{1,0:T(8,128)(2,1)} %cotangent.1, bf16[768,3072]{1,0:T(8,128)(2,1)} %get-tuple-element.88.w_inner, ...), custom_call_target="tpu_custom_call" | custom-call | tf_op jit(solution)/shard_map/feed_forward/pallas_call | solution.py:391
  126.6 115.6 %backward.1 = (f32[24,2304]{1,0:T(8,128)}, f32[24,768]{1,0:T(8,128)}, f32[24,768]{1,0:T(8,128)}, f32[32,1536]{1,0:T(8,128)}, f32[24,768]{1,0:T(8,128)}, /*index=...) custom-call(f32[8,768]{1,0:T(8,128)} %get-tuple-element.90.norms.ref, ...), custom_call_target="tpu_custom_call" | custom-call | tf_op jit(solution)/shard_map/backward/pallas_call | solution.py:1225
  242.1 0.0 copy-start
  242.2 7.2 %adamw.1 = (f32[24,2304]{1,0:T(8,128)}, f32[24,768]{1,0:T(8,128)}, f32[24,768]{1,0:T(8,128)}, f32[32,1536]{1,0:T(8,128)}, f32[24,768]{1,0:T(8,128)}, /*index=5*/...) custom-call(f32[24,2304]{1,0:T(8,128)} %refs_0_.3, ...), custom_call_target="tpu_custom_call" | custom-call | tf_op jit(solution)/shard_map/adamw/pallas_call | solution.py:391
  249.4 0.0 copy-done
  249.4 0.9 copy.57
Async XLA Ops:
  242.1 7.2 %copy-start = (f32[320,768]{1,0:T(8,128)S(1)}, f32[320,768]{1,0:T(8,128)}, u32[]{:S(2)}) copy-start(f32[320,768]{1,0:T(8,128)} %get-tuple-element.175) | copy-start | bytes 2949124

commit v6 on v5

--- a/solution.py
+++ b/solution.py
@@ -480,7 +480,7 @@
     ("16",),
 )
 PLANE_LAST, TURNED_BACK = (3,), (6,)
-ROUNDS = tuple((k, ws) for ws in ((6, 5), (3, 2, 4), (0, 1, 7)) for k in range(4))
+ROUNDS = tuple((k, ws) for ws in ((5, 6), (3, 2, 4), (0, 1, 7)) for k in range(4))
 BACK_PLAN = (
     ("b0", "b1", "c0", "b2"),
     ("c1", "b3"),

time: 251 us -> 250 us (level)
  no operation moved by 1% of the time
where the time goes in v6:
time: 250 us
  Pallas kernels  248 us (99%)
    pallas_call x1, Pallas kernels, backward_all(): pl.pallas_call(functools.partial(backward_kernel, plane_first, turned, ro...  115 us
    pallas_call x1, Pallas kernels, forward_all(): pl.pallas_call(functools.partial(forward_kernel, plane_first, turned, set...  106 us
    pallas_call x2, Pallas kernels, call(): pl.pallas_call(body, out_shape=[jax.ShapeDtypeStruct(s, k) for s, k in ou...  27.3 us

profile of v6, /device:TPU:16, one launch (start us, length us, event | category | flops | bytes accessed | tf_op | source)
XLA Modules:
  0.0 249.8 jit_solution(10280588559486708489)
XLA Ops:
  0.7 105.8 %forward.1 = (bf16[768,2304]{1,0:T(8,128)(2,1)}, bf16[768,768]{1,0:T(8,128)(2,1)}, bf16[768,768]{1,0:T(8,128)(2,1)}, bf16[1024,1536]{1,0:T(8,128)(2,1)}, bf16[76...) custom-call(s32[8]{0:T(128)} %refs_0_.2, ...), custom_call_target="tpu_custom_call" | custom-call | tf_op jit(solution)/shard_map/forward/pallas_call | solution.py:850
  106.5 20.1 %feed_forward.1 = (bf16[320,768]{1,0:T(8,128)(2,1)}, bf16[768,3072]{1,0:T(8,128)(2,1)}, bf16[3072,768]{1,0:T(8,128)(2,1)}, f32[320,768]{1,0:T(8,128)}, f32[2,768]{1,0:T(2,128)}) custom-call(f32[320,768]{1,0:T(8,128)} %get-tuple-element.87.normed_two.refs_18_, bf16[320,768]{1,0:T(8,128)(2,1)} %cotangent.1, bf16[768,3072]{1,0:T(8,128)(2,1)} %get-tuple-element.88.w_inner, ...), custom_call_target="tpu_custom_call" | custom-call | tf_op jit(solution)/shard_map/feed_forward/pallas_call | solution.py:391
  126.6 115.1 %backward.1 = (f32[24,2304]{1,0:T(8,128)}, f32[24,768]{1,0:T(8,128)}, f32[24,768]{1,0:T(8,128)}, f32[32,1536]{1,0:T(8,128)}, f32[24,768]{1,0:T(8,128)}, /*index=...) custom-call(f32[8,768]{1,0:T(8,128)} %get-tuple-element.90.norms.ref, ...), custom_call_target="tpu_custom_call" | custom-call | tf_op jit(solution)/shard_map/backward/pallas_call | solution.py:1225
  241.6 0.0 copy-start
  241.6 7.2 %adamw.1 = (f32[24,2304]{1,0:T(8,128)}, f32[24,768]{1,0:T(8,128)}, f32[24,768]{1,0:T(8,128)}, f32[32,1536]{1,0:T(8,128)}, f32[24,768]{1,0:T(8,128)}, /*index=5*/...) custom-call(f32[24,2304]{1,0:T(8,128)} %refs_0_.3, ...), custom_call_target="tpu_custom_call" | custom-call | tf_op jit(solution)/shard_map/adamw/pallas_call | solution.py:391
  248.9 0.0 copy-done
  248.9 0.9 copy.57
Async XLA Ops:
  241.6 7.2 %copy-start = (f32[320,768]{1,0:T(8,128)S(1)}, f32[320,768]{1,0:T(8,128)}, u32[]{:S(2)}) copy-start(f32[320,768]{1,0:T(8,128)} %get-tuple-element.175) | copy-start | bytes 2949124
